TPU v7x, 32 devices: a whole 2x2x4 slice. The times are simulated.
32 devices in a mesh: half: 2 (over core), owner: 16 (over z, y, x).
Axes of the slice: x: 2, y: 2, z: 4, core: 2. Of those that a mesh axis runs over, the one named last changes fastest.
Arguments:
- images: bfloat16 [4096, 16, 512], P(('half', 'owner')), parts along dimension 0, may hold values from -6 to 6
- defocus: bfloat16 [4096], P(('half', 'owner')), parts along dimension 0, may hold values from 1 to 3
- owner_of: int32 [4096, 1], P(('half', 'owner')), parts along dimension 0, may hold values from 0 to 15; in each aligned block of 128 rows (0 to 127, 128 to 255, ...) at most 16 rows name the same one
- pair_of: int32 [4096], P(('half', 'owner')), parts along dimension 0, may hold values from 0 to 31
- shift_of: int32 [4096], P(('half', 'owner')), parts along dimension 0, may hold values from 0 to 127
- projections: bfloat16 [1024, 16, 1024], P(('half', 'owner')), parts along dimension 0, may hold values from -6 to 6
- interp_weights: bfloat16 [1024, 4, 16], P(('half', 'owner')), parts along dimension 0, may hold values from 0 to 0.099609375
- pair_class: int32 [1024], P(('half', 'owner')), parts along dimension 0, may hold values from 0 to 63
Outputs:
- slab: float32 [512, 1024], P(('half', 'owner')), parts along dimension 0
- weights_slab: float32 [512, 512], P(('half', 'owner')), parts along dimension 0
There are 2 independent parts, one for each index of `half`. A program takes and returns all parts, laid end to end along the dimension named above; each array names one. Nothing has to cross between parts.
Inputs may be any that keep to these rules, and one draw needn't show every extreme that they name: `owner_of`: at most 16 particles of one device are assigned to one owner, and that many in some case.
All inputs are finite; a program needn't handle non-finite values.
Results may differ from a plain program's by a relative error of at most 0.0057.
Values may be sent and summed in bfloat16 or wider, within the bound.
No kernel may reach another device: no remote copies, remote signals or barrier semaphores. Data moves between devices by JAX's collectives and lax.ppermute only.
A program may use at most 64 MiB of HBM per device.

v0:
```python
import math

import jax
import jax.numpy as jnp
from jax import lax
from jax.sharding import PartitionSpec as P

CLASSES = 64


def dft_table(length):
    column = jnp.arange(length, dtype=jnp.int32)
    product = column[:, None] * column[None, :] % length
    angles = product.astype(jnp.float32) * (2.0 * math.pi / length)
    scaled = jnp.concatenate([jnp.cos(angles), -jnp.sin(angles)], axis=1) / math.sqrt(length)
    return scaled.astype(jnp.bfloat16)


def contrast(defocus_values, length):
    column = jnp.arange(length, dtype=jnp.int32)
    folded = jnp.minimum(column, length - column).astype(jnp.float32) / length
    return -jnp.sin(defocus_values[:, None] * 1500.0 * (folded * folded)[None, :] + 0.2)


def align_weight(spectra, defocus_values, shift_values, references):
    length = spectra.shape[-1] // 2
    line_count = spectra.shape[1]
    factor = contrast(defocus_values, length)[:, None, :]
    column = jnp.arange(length, dtype=jnp.int32)
    angles = (shift_values[:, None] * column[None, :] % length).astype(jnp.float32) * (
        2.0 * math.pi / length
    )
    cosine = jnp.cos(angles)[:, None, :]
    sine_part = jnp.sin(angles)[:, None, :]
    real_part = factor * spectra[..., :length].astype(jnp.float32)
    imag_part = factor * spectra[..., length:].astype(jnp.float32)
    aligned_real = real_part * cosine + imag_part * sine_part
    aligned_imag = imag_part * cosine - real_part * sine_part
    scores = jnp.sum(
        aligned_real * references[..., :length].astype(jnp.float32)
        + aligned_imag * references[..., length:].astype(jnp.float32),
        axis=(1, 2),
    ) / math.sqrt(line_count * length)
    weight = 1.0 / (1.0 + jnp.exp(-2.0 * scores))
    contrib = (
        weight[:, None, None] * jnp.concatenate([aligned_real, aligned_imag], axis=-1)
    ).astype(jnp.bfloat16)
    powers = weight[:, None] * factor[:, 0, :] * factor[:, 0, :]
    return (contrib, powers)


def on_device(
    images, defocus, owner_of, pair_of, shift_of, projections, interp_weights, pair_class
):
    particles, line_count, length = images.shape
    owners = lax.axis_size("owner")
    capacity = 2 * particles // owners
    slot_total = owners * capacity
    pairs_here = projections.shape[0]
    slab_lines = interp_weights.shape[1]
    transform = dft_table(length)
    target_owner = owner_of[:, 0]
    owner_hits = (target_owner[:, None] == jnp.arange(owners, dtype=jnp.int32)[None, :]).astype(
        jnp.int32
    )
    earlier = jnp.cumsum(owner_hits, axis=0) - owner_hits
    position = target_owner * capacity + jnp.sum(earlier * owner_hits, axis=1)
    matches = (position[None, :] == jnp.arange(slot_total, dtype=jnp.int32)[:, None]).astype(
        jnp.int32
    )
    source_row = jnp.sum(matches * jnp.arange(particles, dtype=jnp.int32)[None, :], axis=1)
    filled = jnp.sum(matches, axis=1) > 0
    details = jnp.stack(
        [
            defocus,
            pair_of.astype(jnp.bfloat16),
            shift_of.astype(jnp.bfloat16),
            jnp.ones_like(defocus),
        ],
        axis=1,
    )
    packed_details = jnp.where(
        filled[:, None], jnp.take(details, source_row, axis=0), jnp.zeros((), jnp.bfloat16)
    ).reshape(owners, capacity, 4)
    payload = images.reshape(particles, line_count * length)
    packed = jnp.where(
        filled[:, None], jnp.take(payload, source_row, axis=0), jnp.zeros((), jnp.bfloat16)
    ).reshape(owners, capacity, -1)
    arrived = lax.all_to_all(packed, "owner", split_axis=0, concat_axis=0, tiled=True)
    arrived_details = lax.all_to_all(
        packed_details, "owner", split_axis=0, concat_axis=0, tiled=True
    )
    senders = arrived.shape[0]
    per_sender = arrived.shape[1]
    spectra = jnp.dot(
        arrived.reshape(senders * per_sender * line_count, length),
        transform,
        preferred_element_type=jnp.float32,
    ).astype(jnp.bfloat16)
    spectra = spectra.reshape(senders * per_sender, line_count, 2 * length)
    flat_details = arrived_details.reshape(senders * per_sender, 4)
    defocus_values = flat_details[:, 0].astype(jnp.float32)
    pair_index = flat_details[:, 1].astype(jnp.int32)
    shift_values = flat_details[:, 2].astype(jnp.int32)
    present = flat_details[:, 3].astype(jnp.float32)
    references = jnp.take(projections, pair_index, axis=0)
    contrib, powers = align_weight(spectra, defocus_values, shift_values, references)
    selector = (pair_index[:, None] == jnp.arange(pairs_here, dtype=jnp.int32)[None, :]).astype(
        jnp.float32
    ) * present[:, None]
    contribs, powers, selectors = (
        contrib.reshape(senders, per_sender, -1),
        powers.reshape(senders, per_sender, length),
        selector.reshape(senders, per_sender, pairs_here),
    )
    contribs = contribs.reshape(slot_total, line_count * 2 * length)
    powers = powers.reshape(slot_total, length)
    selectors = selectors.reshape(slot_total, pairs_here)
    line_sums = jnp.einsum(
        "sp,sk->pk", selectors.astype(jnp.bfloat16), contribs, preferred_element_type=jnp.float32
    )
    power_sums = jnp.einsum("sp,sk->pk", selectors, powers, precision=lax.Precision.HIGHEST)
    interp_float = interp_weights.astype(jnp.float32)
    image_part = jnp.einsum(
        "pvr,prk->pvk",
        interp_float,
        line_sums.reshape(pairs_here, line_count, 2 * length),
        precision=lax.Precision.HIGHEST,
    )
    power_part = jnp.sum(interp_float, axis=2)[:, :, None] * power_sums[:, None, :]
    combined = jnp.concatenate([image_part, power_part], axis=2)
    class_selector = (pair_class[None, :] == jnp.arange(CLASSES, dtype=jnp.int32)[:, None]).astype(
        jnp.float32
    )
    term = jnp.einsum(
        "cp,pvk->cvk", class_selector, combined, precision=lax.Precision.HIGHEST
    ).reshape(CLASSES * slab_lines, 3 * length)
    reduced = lax.psum_scatter(term, "owner", scatter_dimension=0, tiled=True)
    return (reduced[:, : 2 * length], reduced[:, 2 * length :] * (CLASSES / (particles * owners)))


def solution(mesh):
    return jax.shard_map(
        on_device,
        mesh=mesh,
        in_specs=(
            P(("half", "owner"), None, None),
            P(("half", "owner")),
            P(("half", "owner"), None),
            P(("half", "owner")),
            P(("half", "owner")),
            P(("half", "owner"), None, None),
            P(("half", "owner"), None, None),
            P(("half", "owner")),
        ),
        out_specs=(P(("half", "owner"), None), P(("half", "owner"), None)),
        check_vma=False,
    )
```

profile of v0, /device:TPU:0, one launch (start us, length us, event | category | flops | bytes accessed | tf_op | source)
XLA Modules:
  0.0 341.7 jit_solution(5321774585542133246)
XLA Ops:
  13.3 8.3 %all-to-all-start = ((bf16[16,16,4]{1,2,0:T(4,128)(2,1)}), bf16[16,16,4]{1,2,0:T(4,128)(2,1)S(1)}, u32[]{:S(2)}, u32[]{:S(2)}) async-start(bf16[16,16,4]{1,2,0:T(4,128)(2,1)} %select_select_fusion.1), calls=%async_computation | async-start | bytes 32768 | tf_op jit(solution)/shard_map/all_to_all | solution.py:90
  21.7 3.0 copy.44
  24.6 5.1 %gather_fusion.1 = bf16[256,8192]{1,0:T(8,128)(2,1)} fusion(bf16[128,8192]{1,0:T(8,128)(2,1)S(1)} %bitcast.38, s32[1024]{0:T(1024)S(1)} %pad_clamp_fusion.1), kind=kCustom, calls=%fused_computation.1 | custom fusion | bytes 8389632 | tf_op jit(solution)/shard_map/jit(_take)/gather | solution.py:87
  29.8 4.7 %select_select_fusion = bf16[16,16,8192]{2,1,0:T(8,128)(2,1)} fusion(bf16[16,16,8192]{2,1,0:T(8,128)(2,1)} %bitcast.42, pred[16,16]{1,0:T(8,128)(4,1)S(1)} %compare_and_fusion, pred[16,16]{1,0:T(8,128)(4,1)S(1)} %gt.19), kind=kLoop, calls=%fused_computation.13 | loop fusion | flops 4194304 | bytes 8389120 | tf_op jit(solution)/shard_map/jit(_where)/select_n | solution.py:86
  34.5 7.0 %all-to-all-start.1 = ((bf16[16,16,8192]{2,1,0:T(8,128)(2,1)}), bf16[16,16,8192]{2,1,0:T(8,128)(2,1)}, u32[]{:S(2)}, u32[]{:S(2)}) async-start(bf16[16,16,8192]{2,1,0:T(8,128)(2,1)} %select_select_fusion), calls=%async_computation.1 | async-start | bytes 8388608 | tf_op jit(solution)/shard_map/all_to_all | solution.py:89
  41.9 5.3 %sine_negate_fusion = (f32[512,512]{1,0:T(8,128)S(1)}, f32[512,512]{1,0:T(8,128)}) fusion(), kind=kLoop, calls=%fused_computation.26 | loop fusion | flops 3932160 | bytes 2097152 | tf_op jit(solution)/shard_map/neg | solution.py:15
  47.3 8.4 %gather_fusion.2 = bf16[256,16,1024]{2,1,0:T(8,128)(2,1)} fusion(bf16[32,16,1024]{2,1,0:T(8,128)(2,1)S(1)} %copy-done, s32[1024]{0:T(1024)S(1)} %pad_clamp_fusion), kind=kCustom, calls=%fused_computation.2 | custom fusion | bytes 16778240 | tf_op jit(solution)/shard_map/jit(_take)/gather | solution.py:106
  55.7 1.8 sine_negate_fusion.1
  57.5 2.1 fusion.27
  59.7 7.4 %broadcast_select_fusion = bf16[256,16,1024]{2,1,0:T(8,128)(2,1)} fusion(bf16[256,16,1024]{2,1,0:T(8,128)(2,1)} %gather_fusion.2, pred[256]{0:T(512)(128)(4,1)S(1)} %get-tuple-element.7), kind=kLoop, calls=%fused_computation.11 | loop fusion | flops 4194304 | bytes 16777472 | tf_op jit(solution)/shard_map/jit(_take)/select_n | solution.py:106
  67.1 53.0 %all-to-all-done.1 = bf16[16,16,8192]{2,1,0:T(8,128)(2,1)} async-done(((bf16[16,16,8192]{2,1,0:T(8,128)(2,1)}), bf16[16,16,8192]{2,1,0:T(8,128)(2,1)}, u32[]{:S(2)}, u32[]{:S(2)}) %all-to-all-start.1) | async-done | bytes 4194336 | tf_op jit(solution)/shard_map/all_to_all | solution.py:89
  120.1 7.4 %reshape.185 = bf16[4096,512]{1,0:T(8,128)(2,1)} reshape(bf16[16,16,8192]{2,1,0:T(8,128)(2,1)} %all-to-all-done.1) | data formatting | bytes 8388608 | tf_op jit(solution)/shard_map/reshape | solution.py:96
  127.5 7.2 %convolution_convert_fusion = bf16[4096,1024]{1,0:T(8,128)(2,1)S(1)} fusion(bf16[4096,512]{1,0:T(8,128)(2,1)} %reshape.185, f32[512,512]{1,0:T(8,128)S(1)} %get-tuple-element.16, f32[512,512]{1,0:T(8,128)} %get-tuple-element.17), kind=kOutput, calls=%fused_computation.12 | convolution fusion | flops 4300734464 | bytes 14680064 | tf_op jit(solution)/shard_map/dot_general | solution.py:95
  134.7 11.4 %add_reduce_fusion = (f32[256]{0:T(256)S(1)}, f32[256,16,512]{2,1,0:T(8,128)}, f32[256,16,512]{2,1,0:T(8,128)}) fusion(bf16[256,16,1024]{2,1,0:T(8,128)(2,1)S(1)} %copy-done.2, f32[256,512]{1,0:T(8,128)S(1)} %get-tuple-element.13, bf16[256,16,1024]{2,1,0:T(8,128)(2,1)S(1)} %bitcast.43, f32[256,512]{1,0:T(8,128)S(1)} %get-tuple-element.12, ...), kind=kLoop, calls=%fused_computation.6 | loop fusion | flops 33554176 | bytes 35128320 | tf_op jit(solution)/shard_map/reduce_sum | solution.py:39
  146.1 6.8 %pad_maximum_fusion = f32[256,16,1024]{2,1,0:T(8,128)S(1)} fusion(f32[256,16,512]{2,1,0:T(8,128)} %get-tuple-element.6, f32[256,16,512]{2,1,0:T(8,128)} %get-tuple-element.5), kind=kLoop, calls=%fused_computation.3 | loop fusion | flops 4194304 | bytes 33554432 | tf_op jit(solution)/shard_map/concatenate | solution.py:46
  152.9 10.3 %copy.45 = f32[32,8,16,1024]{3,1,2,0:T(8,128)S(1)} copy(f32[32,8,16,1024]{3,2,1,0:T(8,128)S(1)} %bitcast.40) | data formatting | bytes 33554432
  163.2 4.0 %fusion = bf16[16384,256]{0,1:T(8,128)(2,1)} fusion(f32[256,16384]{1,0:T(8,128)S(1)} %bitcast.39, f32[256]{0:T(256)S(1)} %add_divide_fusion), kind=kLoop, calls=%fused_computation.5 | loop fusion | flops 8388608 | bytes 25166848 | tf_op jit(solution)/shard_map/sp,sk->pk/dot_general | solution.py:119
  167.2 11.9 %copy.38 = bf16[16384,256]{1,0:T(8,128)(2,1)} copy(bf16[16384,256]{0,1:T(8,128)(2,1)} %fusion) | data formatting | bytes 16777216 | tf_op jit(solution)/shard_map/sp,sk->pk/dot_general | solution.py:119
  179.0 2.3 fusion.20
  181.4 6.0 %fusion.31 = f32[32,16,1024]{2,0,1:T(8,128)S(1)} fusion(bf16[16,1024,256]{2,1,0:T(8,128)(2,1)} %bitcast.41, f32[256]{0:T(256)S(1)} %bitcast.52, s32[256]{0:T(256)S(1)} %bitcast.50), kind=kOutput, calls=%fused_computation.63 | convolution fusion | flops 268451840 | bytes 10487808 | tf_op jit(solution)/shard_map/sp,sk->pk/dot_general | solution.py:119
  187.4 2.0 fusion.4
  191.8 1.7 reshape.187
  193.5 138.5 %reduce-scatter.2.cloned.1.call-done = f32[16,1536]{1,0:T(8,128)} async-done(((f32[256,1536]{1,0:T(8,128)}), f32[16,1536]{1,0:T(8,128)}) %reduce-scatter.2.cloned.1.call-update) | async-done | bytes 98320 | tf_op jit(solution)/shard_map/reduce_scatter | solution.py:138
  332.0 1.5 slice.54
  (47 shorter events, 10.4 us)
Async XLA Ops:
  7.2 40.2 %copy-start = (bf16[32,16,1024]{2,1,0:T(8,128)(2,1)S(1)}, bf16[32,16,1024]{2,1,0:T(8,128)(2,1)}, u32[]{:S(2)}) copy-start(bf16[32,16,1024]{2,1,0:T(8,128)(2,1)} %param.13) | copy-start | bytes 3145732
  13.3 21.1 %all-to-all-start = ((bf16[16,16,4]{1,2,0:T(4,128)(2,1)}), bf16[16,16,4]{1,2,0:T(4,128)(2,1)S(1)}, u32[]{:S(2)}, u32[]{:S(2)}) async-start(bf16[16,16,4]{1,2,0:T(4,128)(2,1)} %select_select_fusion.1), calls=%async_computation | async-start | bytes 32768 | tf_op jit(solution)/shard_map/all_to_all | solution.py:90
  29.8 11.9 %copy-start.3 = (bf16[32,4,16]{0,2,1:T(8,128)(2,1)S(1)}, bf16[32,4,16]{0,2,1:T(8,128)(2,1)}, u32[]{:S(2)}) copy-start(bf16[32,4,16]{0,2,1:T(8,128)(2,1)} %param.14) | copy-start | bytes 12292
  34.5 85.6 %all-to-all-start.1 = ((bf16[16,16,8192]{2,1,0:T(8,128)(2,1)}), bf16[16,16,8192]{2,1,0:T(8,128)(2,1)}, u32[]{:S(2)}, u32[]{:S(2)}) async-start(bf16[16,16,8192]{2,1,0:T(8,128)(2,1)} %select_select_fusion), calls=%async_computation.1 | async-start | bytes 8388608 | tf_op jit(solution)/shard_map/all_to_all | solution.py:89
  41.4 290.6 %reduce-scatter.2.cloned.1.call-start = ((), (), s32[]{:S(2)}) async-start(), calls=%async_computation.3 | async-start | bytes 1671168 | tf_op jit(solution)/shard_map/reduce_scatter | solution.py:138
  127.5 7.2 %copy-start.2 = (bf16[256,16,1024]{2,1,0:T(8,128)(2,1)S(1)}, bf16[256,16,1024]{2,1,0:T(8,128)(2,1)}, u32[]{:S(2)}) copy-start(bf16[256,16,1024]{2,1,0:T(8,128)(2,1)} %broadcast_select_fusion) | copy-start | bytes 25165828
  179.0 10.7 %copy-start.4 = (s32[32]{0:T(128)S(1)}, s32[32]{0:T(128)}, u32[]{:S(2)}) copy-start(s32[32]{0:T(128)} %param.15) | copy-start | bytes 388
  181.4 153.5 %copy-start.1 = (bf16[32,16,1024]{2,1,0:T(8,128)(2,1)S(1)}, bf16[32,16,1024]{2,1,0:T(8,128)(2,1)}, u32[]{:S(2)}) copy-start(bf16[32,16,1024]{2,1,0:T(8,128)(2,1)} %param.13) | copy-start | bytes 3145732
Sparse Core Ops, SparseCore 0:
  193.6 138.3 reduce-scatter.1
where the time goes:
time: 343 us; the launch traced here: 342 us
  waiting for transfers between devices  192 us (56%)
  local copies, waits for them, and re-layouts  52 us (15%)
  other arithmetic  50 us (15%)
  matrix products  18.5 us (5%)
  starting transfers between devices  15.5 us (5%)
  between operations  14.2 us (4%)
    reduce_scatter x1, waiting for transfers between devices, on_device(): reduced = lax.psum_scatter(term, 'owner', scatter_dimension=0, tiled=True)  139 us
    all_to_all x1, waiting for transfers between devices, on_device(): lax.all_to_all(packed, 'owner', split_axis=0, concat_axis=0, tiled=True)  53 us
    unnamed x13, local copies, waits for them, and re-layouts  13.4 us
    dot_general x1, local copies, waits for them, and re-layouts, on_device(): jnp.einsum('sp,sk->pk', selectors.astype(jnp.bfloat16), contribs, preferr...  11.9 us
    reduce_sum x1, other arithmetic, align_weight(): jnp.sum(aligned_real * references[..., :length].astype(jnp.float32) + ali...  11.4 us
    gather x1, local copies, waits for them, and re-layouts, on_device(): references = jnp.take(projections, pair_index, axis=0)  8.38 us
    all_to_all x1, starting transfers between devices, on_device(): lax.all_to_all(packed_details, 'owner', split_axis=0, concat_axis=0, tile...  8.31 us
    select_n x1, other arithmetic, on_device(): references = jnp.take(projections, pair_index, axis=0)  7.44 us
  transfers between devices with their start and end apart: 3, of which 2 were waited for; matrix products, arithmetic and copies ran while one was open for 11% of the time, Pallas kernels for 0%

commit v1 on v0

v1 whole, which is shorter than its diff:
```python
import math

import jax
import jax.numpy as jnp
import numpy as np
from jax import lax
from jax.experimental import pallas as pl
from jax.experimental.pallas import tpu as pltpu
from jax.sharding import PartitionSpec as P

CLASSES = 64
F32 = jnp.float32
BF16 = jnp.bfloat16
VMEM_LIMIT = 48 * 1024 * 1024


def packed_table(length):
    half = length // 2
    product = np.arange(length)[:, None] * np.arange(half + 1)[None, :] % length
    angles = product * (2.0 * math.pi / length)
    cosine, sine = np.cos(angles), -np.sin(angles)
    sine[:, 0] = cosine[:, half]
    table = np.concatenate([cosine[:, :half], sine[:, :half]], axis=1) / math.sqrt(length)
    return jnp.asarray(table, F32).astype(BF16)


def mirror(half):
    row = lax.broadcasted_iota(jnp.int32, (half, half), 0)
    column = lax.broadcasted_iota(jnp.int32, (half, half), 1)
    return jnp.where(row + column == half, 1.0, 0.0).astype(BF16)


def fold_kernel(x_ref, out_ref):
    half = x_ref.shape[1] // 4
    flip = mirror(half)
    real_low, real_high = x_ref[:, :half], x_ref[:, half : 2 * half]
    imag_low, imag_high = x_ref[:, 2 * half : 3 * half], x_ref[:, 3 * half :]
    real = real_low.astype(F32) + jnp.dot(real_high, flip, preferred_element_type=F32)
    imag = imag_low.astype(F32) - jnp.dot(imag_high, flip, preferred_element_type=F32)
    lane = lax.broadcasted_iota(jnp.int32, imag.shape, 1)
    imag = jnp.where(lane == 0, real_high.astype(F32)[:, :1], imag)
    out_ref[:, :half] = real.astype(BF16)
    out_ref[:, half:] = imag.astype(BF16)


def fold(projections):
    pairs, lines, width = projections.shape
    return pl.pallas_call(
        fold_kernel,
        grid=(lines,),
        in_specs=[pl.BlockSpec((pairs, width), lambda r: (0, r))],
        out_specs=pl.BlockSpec((pairs, width // 2), lambda r: (0, r)),
        out_shape=jax.ShapeDtypeStruct((pairs, lines * width // 2), BF16),
        name="fold_projections",
    )(projections.reshape(pairs, lines * width))


def factors(defocus, shift, length):
    half = length // 2
    column = jnp.arange(half + 128, dtype=jnp.int32)
    folded = column.astype(F32) / length
    ctf = -jnp.sin(defocus[:, None] * 1500.0 * (folded * folded)[None, :] + 0.2)
    angles = (shift[:, None] * column[None, :half] % length).astype(F32) * (2.0 * math.pi / length)
    nyquist = ctf[:, half] * (1 - 2 * (shift % 2)).astype(F32)
    cosine = ctf[:, :half] * jnp.cos(angles)
    sine = ctf[:, :half] * jnp.sin(angles)
    cosine_imag = jnp.where(column[None, :half] == 0, nyquist[:, None], cosine)
    keep = (column <= half)[None, :]
    return cosine, cosine_imag, sine, jnp.where(keep, ctf * ctf, 0.0).astype(BF16)


def score_kernel(
    scale, x_ref, table_ref, cos_ref, cosi_ref, sin_ref, power_ref, ref_ref, interp_ref,
    class_ref, pair_ref, valid_ref, out_ref, aligned, scores,
):
    step = pl.program_id(0)
    lines = pl.num_programs(0)
    half = cos_ref.shape[1]
    pairs, slots = scores.shape
    spectra = jnp.dot(x_ref[...], table_ref[...], preferred_element_type=F32)
    real, imag = spectra[:, :half], spectra[:, half:]
    sine = sin_ref[...]
    aligned[step, :, :half] = (cos_ref[...] * real + sine * imag).astype(BF16)
    aligned[step, :, half:] = (cosi_ref[...] * imag - sine * real).astype(BF16)
    term = lax.dot_general(
        ref_ref[...], aligned[step], (((1,), (1,)), ((), ())), preferred_element_type=F32
    )

    @pl.when(step == 0)
    def _():
        scores[...] = term

    @pl.when(step > 0)
    def _():
        scores[...] += term

    @pl.when(step == lines - 1)
    def _():
        chosen = lax.broadcasted_iota(jnp.int32, (pairs, slots), 0) == pair_ref[...]
        total = jnp.sum(jnp.where(chosen, scores[...], 0.0), axis=0, keepdims=True)
        weight = valid_ref[...] / (1.0 + jnp.exp(total * (-2.0 * scale)))
        onehot = jnp.where(chosen, 1.0, 0.0).astype(BF16)
        taps = jnp.dot(interp_ref[...], onehot, preferred_element_type=F32)
        label = jnp.dot(class_ref[...], onehot, preferred_element_type=F32)[:1]
        rows = out_ref.shape[0]
        group = lax.broadcasted_iota(jnp.int32, (rows, slots), 0) // (rows // CLASSES)
        spread = jnp.where(group == label.astype(jnp.int32), weight, 0.0).reshape(rows // 8, 8, slots)
        slab = jnp.zeros((rows, 2 * half), F32)
        tap_sum = jnp.zeros((8, slots), F32)
        for line in range(taps.shape[0] // 8):
            tap = taps[line * 8 : line * 8 + 8]
            tap_sum = tap_sum + tap
            mixer = (spread * tap[None]).reshape(rows, slots).astype(BF16)
            slab = slab + jnp.dot(mixer, aligned[line], preferred_element_type=F32)
        mixer = (spread * tap_sum[None]).reshape(rows, slots).astype(BF16)
        out_ref[:, : 2 * half] = slab.astype(BF16)
        out_ref[:, 2 * half :] = jnp.dot(mixer, power_ref[...], preferred_element_type=F32).astype(BF16)


def score_and_spread(images, tables, references, interp, classes, pair, valid, rows):
    cosine, cosine_imag, sine, power = tables
    slots, pairs = images.shape[0], references.shape[0]
    half = cosine.shape[1]
    length = 2 * half
    lines = images.shape[1] // length
    whole = lambda a: pl.BlockSpec(a.shape, lambda r: (0,) * a.ndim)
    line = lambda n: pl.BlockSpec((n, length), lambda r: (0, r))
    table = packed_table(length)
    small = [table, cosine, cosine_imag, sine, power]
    tail = [interp, classes, pair, valid]
    width = length + power.shape[1]
    return pl.pallas_call(
        lambda *refs: score_kernel(1.0 / math.sqrt(lines * length), *refs),
        grid=(lines,),
        in_specs=[line(slots)] + [whole(a) for a in small] + [line(pairs)] + [whole(a) for a in tail],
        out_specs=pl.BlockSpec((rows, width), lambda r: (0, 0)),
        out_shape=jax.ShapeDtypeStruct((rows, width), BF16),
        scratch_shapes=[pltpu.VMEM((lines, slots, length), BF16), pltpu.VMEM((pairs, slots), F32)],
        compiler_params=pltpu.CompilerParams(vmem_limit_bytes=VMEM_LIMIT),
        name="score_and_spread",
    )(images, *small, references, *tail)


def finish_kernel(scale, x_ref, slab_ref, weights_ref):
    half = weights_ref.shape[1] // 2
    total = jnp.sum(x_ref[...].astype(F32), axis=0)
    flip = mirror(half)

    def mirrored(part):
        out = jnp.zeros(part.shape, F32)
        for _ in range(3):
            piece = part.astype(BF16)
            out = out + jnp.dot(piece, flip, preferred_element_type=F32)
            part = part - piece.astype(F32)
        return out

    real, imag, power = total[:, :half], total[:, half : 2 * half], total[:, 2 * half : 3 * half] * scale
    first = lax.broadcasted_iota(jnp.int32, real.shape, 1) == 0
    slab_ref[:, :half] = real
    slab_ref[:, half : 2 * half] = jnp.where(first, imag[:, :1], mirrored(real))
    slab_ref[:, 2 * half : 3 * half] = jnp.where(first, 0.0, imag)
    slab_ref[:, 3 * half :] = jnp.where(first, 0.0, -mirrored(imag))
    weights_ref[:, :half] = power
    weights_ref[:, half:] = jnp.where(first, total[:, 3 * half : 3 * half + 1] * scale, mirrored(power))


def finish(received, length, scale):
    rows = received.shape[1]
    return pl.pallas_call(
        lambda *refs: finish_kernel(scale, *refs),
        out_shape=(
            jax.ShapeDtypeStruct((rows, 2 * length), F32),
            jax.ShapeDtypeStruct((rows, length), F32),
        ),
        name="finish_slab",
    )(received)


def on_device(
    images, defocus, owner_of, pair_of, shift_of, projections, interp_weights, pair_class
):
    particles, lines, length = images.shape
    owners = lax.axis_size("owner")
    capacity = 2 * particles // owners
    slots = owners * capacity
    pairs, slab_lines, _ = interp_weights.shape
    rows = CLASSES * slab_lines
    owner = owner_of[:, 0]
    hits = (owner[:, None] == jnp.arange(owners, dtype=jnp.int32)[None, :]).astype(BF16)
    below = jnp.tril(jnp.ones((particles, particles), BF16), -1)
    earlier = jnp.dot(below, hits, preferred_element_type=F32)
    place = owner * capacity + jnp.sum(earlier * hits.astype(F32), axis=1).astype(jnp.int32)
    pick = (place[None, :] == jnp.arange(slots, dtype=jnp.int32)[:, None]).astype(BF16)
    details = jnp.stack(
        [defocus, pair_of.astype(BF16), shift_of.astype(BF16), jnp.ones_like(defocus)], axis=1
    )
    details = jnp.pad(details, ((0, 0), (0, 124)))
    payload = jnp.concatenate([images.reshape(particles, lines * length), details], axis=1)
    packed = jnp.dot(pick, payload, preferred_element_type=F32).astype(BF16)
    arrived = lax.all_to_all(packed, "owner", split_axis=0, concat_axis=0, tiled=True)
    found = arrived[:, lines * length :].astype(F32)
    pair, shift = found[:, 1].astype(jnp.int32), found[:, 2].astype(jnp.int32)
    tables = factors(found[:, 0], shift, length)
    references = fold(projections)
    repeat = 8 // slab_lines
    interp = jnp.tile(interp_weights.transpose(2, 1, 0), (1, repeat, 1)).reshape(lines * 8, pairs)
    classes = jnp.broadcast_to(pair_class.astype(BF16)[None, :], (8, pairs))
    partial = score_and_spread(
        arrived, tables, references, interp, classes, pair[None, :], found[:, 3][None, :], rows
    )
    received = lax.all_to_all(partial, "owner", split_axis=0, concat_axis=0, tiled=True)
    return finish(
        received.reshape(owners, rows // owners, -1), length, CLASSES / (particles * owners)
    )


def solution(mesh):
    return jax.shard_map(
        on_device,
        mesh=mesh,
        in_specs=(
            P(("half", "owner"), None, None),
            P(("half", "owner")),
            P(("half", "owner"), None),
            P(("half", "owner")),
            P(("half", "owner")),
            P(("half", "owner"), None, None),
            P(("half", "owner"), None, None),
            P(("half", "owner")),
        ),
        out_specs=(P(("half", "owner"), None), P(("half", "owner"), None)),
        check_vma=False,
    )
```

time: 343 us -> 152 us (0.44)
  waiting for transfers between devices: 192 us -> 69.4 us
  local copies, waits for them, and re-layouts: 52 us -> 4.88 us
  other arithmetic: 50 us -> 5.48 us
  blocking collectives: 0 us -> 33.3 us
  Pallas kernels: 0 us -> 25 us
  matrix products: 18.5 us -> 3.49 us
  between operations: 14.2 us -> 0.81 us
  starting transfers between devices: 15.5 us -> 8.49 us
    reduce_scatter x1 -> x0, waiting for transfers between devices: 139 us -> none  [on_device(): reduced = lax.psum_scatter(term, 'owner', scatter_dimension=0, tiled=True)]
    all_to_all x0 -> x1, blocking collectives: none -> 33.3 us  [on_device(): lax.all_to_all(partial, 'owner', split_axis=0, concat_axis=0, tiled=True)]
    pallas_call x0 -> x3, Pallas kernels: none -> 25 us  [the longest x1 13.3 us: score_and_spread(): pl.pallas_call(lambda *refs: score_kernel(1.0 / math.sqrt(lines * length)...]
    all_to_all x1, waiting for transfers between devices: 53 us -> 69.4 us  [on_device(): lax.all_to_all(packed, 'owner', split_axis=0, concat_axis=0, tiled=True)]
    dot_general x5 -> x2, matrix products: 18.5 us -> 3.49 us  [the longest x1 3.27 us: on_device(): packed = jnp.dot(pick, payload, preferred_element_type=F32).astype(BF16)]
    gather x4 -> x0, local copies, waits for them, and re-layouts: 14.5 us -> none  [the longest x1 8.38 us: on_device(): references = jnp.take(projections, pair_index, axis=0)]
    dot_general x2 -> x0, local copies, waits for them, and re-layouts: 12.9 us -> none  [the longest x1 11.9 us: on_device(): jnp.einsum('sp,sk->pk', selectors.astype(jnp.bfloat16), contribs, preferr...]
    reduce_sum x4 -> x0, other arithmetic: 12.4 us -> none  [the longest x1 11.4 us: align_weight(): jnp.sum(aligned_real * references[..., :length].astype(jnp.float32) + ali...]
  transfers between devices with their start and end apart: 3 -> 1, of which waited for: 2 -> 1; matrix products, arithmetic and copies ran while one was open for 11% -> 1% of each run, Pallas kernels for 0% -> 6%
where the time goes in v1:
time: 152 us; the launch traced here: 151 us
  waiting for transfers between devices  69.4 us (46%)
  blocking collectives  33.3 us (22%)
  Pallas kernels  25 us (16%)
  starting transfers between devices  8.49 us (6%)
  other arithmetic  5.48 us (4%)
  local copies, waits for them, and re-layouts  4.88 us (3%)
  matrix products  3.49 us (2%)
    all_to_all x1, waiting for transfers between devices, on_device(): lax.all_to_all(packed, 'owner', split_axis=0, concat_axis=0, tiled=True)  69.4 us
    all_to_all x1, blocking collectives, on_device(): lax.all_to_all(partial, 'owner', split_axis=0, concat_axis=0, tiled=True)  33.3 us
    pallas_call x1, Pallas kernels, score_and_spread(): pl.pallas_call(lambda *refs: score_kernel(1.0 / math.sqrt(lines * length)...  13.3 us
    pallas_call x1, Pallas kernels, fold(): pl.pallas_call(fold_kernel, grid=(lines,), in_specs=[pl.BlockSpec((pairs,...  9.75 us
    all_to_all x1, starting transfers between devices, on_device(): lax.all_to_all(packed, 'owner', split_axis=0, concat_axis=0, tiled=True)  8.49 us
    unnamed x15, local copies, waits for them, and re-layouts  4.77 us
    dot_general x1, matrix products, on_device(): packed = jnp.dot(pick, payload, preferred_element_type=F32).astype(BF16)  3.27 us
  transfers between devices with their start and end apart: 1, of which 1 were waited for; matrix products, arithmetic and copies ran while one was open for 1% of the time, Pallas kernels for 6%

profile of v1, /device:TPU:0, one launch (start us, length us, event | category | flops | bytes accessed | tf_op | source)
XLA Modules:
  0.0 150.9 jit_solution(7142015226179813441)
XLA Ops:
  0.6 0.0 copy-start.4
  0.6 0.7 convert_bitcast_fusion
  1.3 0.1 pad.10.clone
  1.4 0.7 maximum_maximum_fusion
  2.1 0.1 copy.17
  2.3 3.0 %copy.18 = bf16[16,8,16,512]{3,1,2,0:T(8,128)(2,1)S(1)} copy(bf16[16,8,16,512]{3,2,1,0:T(8,128)(2,1)} %bitcast.25) | data formatting | bytes 4194304
  5.2 0.0 copy-done.4
  5.3 0.2 fusion.6
  5.5 3.3 %convolution_convert_fusion = bf16[256,8320]{1,0:T(8,128)(2,1)} fusion(bf16[128,4]{1,0:T(8,128)(2,1)S(1)} %copy.17, bf16[128,8192]{1,0:T(8,128)(2,1)S(1)} %bitcast.26, s32[128]{0:T(128)S(1)} %convert_add_fusion), kind=kOutput, calls=%fused_computation | convolution fusion | flops 553811968 | bytes 6358528 | tf_op jit(solution)/shard_map/dot_general | solution.py:199
  8.8 8.5 %all-to-all-start = ((bf16[16,16,8320]{2,1,0:T(8,128)(2,1)}), bf16[16,16,8320]{2,1,0:T(8,128)(2,1)}, u32[]{:S(2)}, u32[]{:S(2)}) async-start(bf16[16,16,8320]{2,1,0:T(8,128)(2,1)} %bitcast.23), calls=%async_computation | async-start | bytes 8519680 | tf_op jit(solution)/shard_map/all_to_all | solution.py:200
  17.3 0.0 copy-start.3
  17.3 0.0 copy-start.5
  17.3 1.6 %copy.19 = bf16[4,8,16,1024]{3,1,2,0:T(8,128)(2,1)} copy(bf16[4,8,16,1024]{3,2,1,0:T(8,128)(2,1)S(1)} %bitcast.27) | data formatting | bytes 2097152
  19.0 9.7 %fold_projections.1.refs_6_ = bf16[32,8192]{1,0:T(8,128)(2,1)} custom-call(bf16[32,16384]{1,0:T(8,128)(2,1)} %bitcast.24), custom_call_target="tpu_custom_call" | custom-call | tf_op jit(solution)/shard_map/fold_projections/pallas_call | solution.py:48
  28.8 69.4 %all-to-all-done = bf16[16,16,8320]{2,1,0:T(8,128)(2,1)} async-done(((bf16[16,16,8320]{2,1,0:T(8,128)(2,1)}), bf16[16,16,8320]{2,1,0:T(8,128)(2,1)}, u32[]{:S(2)}, u32[]{:S(2)}) %all-to-all-start) | async-done | bytes 4259872 | tf_op jit(solution)/shard_map/all_to_all | solution.py:200
  98.2 0.8 slice_convert_fusion.2
  99.0 0.1 fusion.19
  99.2 0.3 fusion.18
  99.4 1.4 select_convert_fusion
  100.8 0.3 slice_reduce_fusion
  101.1 1.1 broadcast_select_fusion
  102.3 13.3 %score_and_spread.1 = bf16[256,896]{1,0:T(8,128)(2,1)S(1)} custom-call(bf16[256,8320]{1,0:T(8,128)(2,1)} %bitcast.5.refs_0_, bf16[512,512]{1,0:T(8,128)(2,1)S(1)} %copy-done.1, f32[256,256]{1,0:T(8,128)S(1)} %get-tuple-element.7.refs_2_, f32[256,256]{1,0:T(8,128)S(1)} %get-tuple-element.6.refs_3_, f32[256,256]{1,0:T(8,128)S(1)} %get-tuple-element.8.refs_4_, ...), custom_call_target="tpu_custom_call" | custom-call | tf_op jit(solution)/shard_map/score_and_spread/pallas_call | solution.py:132
  115.6 33.3 %all_to_all.20.refs_0_ = bf16[16,16,896]{2,1,0:T(8,128)(2,1)} all-to-all(bf16[16,16,896]{2,1,0:T(8,128)(2,1)S(1)} %bitcast.19), channel_id=1, replica_groups=mesh['half'=2,'owner'=16] {'owner'}, dimensions={0} | all-to-all | bytes 917504 | tf_op jit(solution)/shard_map/all_to_all | solution.py:211
  148.9 1.9 %finish_slab.1 = (f32[16,1024]{1,0:T(8,128)}, f32[16,512]{1,0:T(8,128)}) custom-call(bf16[16,16,896]{2,1,0:T(8,128)(2,1)} %all_to_all.20.refs_0_), custom_call_target="tpu_custom_call" | custom-call | tf_op jit(solution)/shard_map/finish_slab/pallas_call | solution.py:169
  (19 shorter events, 0.1 us)
Async XLA Ops:
  0.6 4.6 %copy-start.4 = (s32[128,1]{0,1:T(1,128)S(1)}, s32[128,1]{0,1:T(1,128)}, u32[]{:S(2)}) copy-start(s32[128,1]{0,1:T(1,128)} %param.11) | copy-start | bytes 1540
  8.8 8.5 %copy-start.2 = (bf16[32,16,1024]{2,1,0:T(8,128)(2,1)S(1)}, bf16[32,16,1024]{2,1,0:T(8,128)(2,1)}, u32[]{:S(2)}) copy-start(bf16[32,16,1024]{2,1,0:T(8,128)(2,1)} %param.14) | copy-start | bytes 3145732
  8.8 89.4 %all-to-all-start = ((bf16[16,16,8320]{2,1,0:T(8,128)(2,1)}), bf16[16,16,8320]{2,1,0:T(8,128)(2,1)}, u32[]{:S(2)}, u32[]{:S(2)}) async-start(bf16[16,16,8320]{2,1,0:T(8,128)(2,1)} %bitcast.23), calls=%async_computation | async-start | bytes 8519680 | tf_op jit(solution)/shard_map/all_to_all | solution.py:200
  17.3 11.4 %copy-start.3 = (bf16[32,4,16]{0,2,1:T(8,128)(2,1)S(1)}, bf16[32,4,16]{0,2,1:T(8,128)(2,1)}, u32[]{:S(2)}) copy-start(bf16[32,4,16]{0,2,1:T(8,128)(2,1)} %param.15) | copy-start | bytes 12292
  17.3 11.4 %copy-start.5 = (s32[32]{0:T(128)S(1)}, s32[32]{0:T(128)}, u32[]{:S(2)}) copy-start(s32[32]{0:T(128)} %param.16) | copy-start | bytes 388
  19.0 83.3 %copy-start.1 = (bf16[512,512]{1,0:T(8,128)(2,1)S(1)}, bf16[512,512]{1,0:T(8,128)(2,1)}, u32[]{:S(2)}) copy-start(bf16[512,512]{1,0:T(8,128)(2,1)} %constant.63.refs_1_) | copy-start | bytes 1572868
  28.7 73.6 %copy-start = (bf16[32,8192]{1,0:T(8,128)(2,1)S(1)}, bf16[32,8192]{1,0:T(8,128)(2,1)}, u32[]{:S(2)}) copy-start(bf16[32,8192]{1,0:T(8,128)(2,1)} %fold_projections.1.refs_6_) | copy-start | bytes 1572868

commit v2 on v1

v2 whole, which is shorter than its diff:
```python
import math

import jax
import jax.numpy as jnp
import numpy as np
from jax import lax
from jax.experimental import pallas as pl
from jax.experimental.pallas import tpu as pltpu
from jax.sharding import PartitionSpec as P

CLASSES = 64
F32 = jnp.float32
BF16 = jnp.bfloat16
VMEM_LIMIT = 48 * 1024 * 1024


def packed_table(length):
    half = length // 2
    product = np.arange(length)[:, None] * np.arange(half + 1)[None, :] % length
    angles = product * (2.0 * math.pi / length)
    cosine, sine = np.cos(angles), -np.sin(angles)
    sine[:, 0] = cosine[:, half]
    table = np.concatenate([cosine[:, :half], sine[:, :half]], axis=1) / math.sqrt(length)
    return jnp.asarray(table, F32).astype(BF16)


def mirror(half):
    row = lax.broadcasted_iota(jnp.int32, (half, half), 0)
    column = lax.broadcasted_iota(jnp.int32, (half, half), 1)
    return jnp.where(row + column == half, 1.0, 0.0).astype(BF16)


def put_tiles(ref, values):
    for t in range(ref.shape[0]):
        ref[t] = values[:, t * 128 : (t + 1) * 128]


def every(ref, start, count, stride):
    picked = [ref[t, pl.ds(start, count, stride=stride), :] for t in range(ref.shape[0])]
    return jnp.concatenate(picked, axis=1)


def fold_kernel(x_ref, info_ref, out_ref, folded):
    pairs, width = out_ref.shape
    half = x_ref.shape[1] // 4
    lines = x_ref.shape[0] // pairs
    flip = mirror(half)
    real_low, real_high = x_ref[:, :half], x_ref[:, half : 2 * half]
    imag_low, imag_high = x_ref[:, 2 * half : 3 * half], x_ref[:, 3 * half :]
    real = real_low.astype(F32) + jnp.dot(real_high, flip, preferred_element_type=F32)
    imag = imag_low.astype(F32) - jnp.dot(imag_high, flip, preferred_element_type=F32)
    lane = lax.broadcasted_iota(jnp.int32, imag.shape, 1)
    imag = jnp.where(lane == 0, real_high.astype(F32)[:, :1], imag)
    put_tiles(folded, jnp.concatenate([real, imag], axis=1))
    for line in range(lines):
        out_ref[:, line * 2 * half : (line + 1) * 2 * half] = every(
            folded, line, pairs, lines
        ).astype(BF16)
    out_ref[:, lines * 2 * half :] = info_ref[...]


def fold(projections, info):
    pairs, lines, width = projections.shape
    return pl.pallas_call(
        fold_kernel,
        out_shape=jax.ShapeDtypeStruct((pairs, lines * width // 2 + info.shape[1]), BF16),
        scratch_shapes=[pltpu.VMEM((width // 256, pairs * lines, 128), F32)],
        compiler_params=pltpu.CompilerParams(vmem_limit_bytes=VMEM_LIMIT),
        name="fold_projections",
    )(projections.reshape(pairs * lines, width), info)


def sort_kernel(capacity, x_ref, bin_ref, pair_ref, shift_ref, defocus_ref, *refs):
    outs, facts_ref, wide = refs[:-2], refs[-2], refs[-1]
    particles = bin_ref.shape[1]
    length = x_ref.shape[1]
    lines = x_ref.shape[0] // particles
    slots = facts_ref.shape[1]
    bins = -(-(slots // capacity) // 8) * 8
    hits = lax.broadcasted_iota(jnp.int32, (bins, particles), 0) == bin_ref[...]
    row = lax.broadcasted_iota(jnp.int32, (particles, particles), 0)
    column = lax.broadcasted_iota(jnp.int32, (particles, particles), 1)
    before = jnp.where(row < column, 1.0, 0.0).astype(BF16)
    earlier = jnp.dot(jnp.where(hits, 1.0, 0.0).astype(BF16), before, preferred_element_type=F32)
    earlier = jnp.sum(jnp.where(hits, earlier, 0.0), axis=0, keepdims=True)
    place = bin_ref[...] * capacity + earlier.astype(jnp.int32)
    pick = lax.broadcasted_iota(jnp.int32, (slots, particles), 0) == place
    pick = jnp.where(pick, 1.0, 0.0).astype(BF16)
    kind = lax.broadcasted_iota(jnp.int32, (8, particles), 0)
    facts = jnp.where(kind == 0, defocus_ref[...], jnp.ones((8, particles), F32))
    facts = jnp.where(kind == 1, pair_ref[...].astype(F32), facts)
    facts = jnp.where(kind == 2, shift_ref[...].astype(F32), facts).astype(BF16)
    facts_ref[...] = lax.dot_general(
        facts, pick, (((1,), (1,)), ((), ())), preferred_element_type=F32
    )
    put_tiles(wide, x_ref[...].astype(F32))
    for line in range(lines):
        picked = jnp.dot(
            pick, every(wide, line, particles, lines).astype(BF16), preferred_element_type=F32
        ).astype(BF16)
        each = slots // len(outs)
        for i, out_ref in enumerate(outs):
            out_ref[:, line * length : (line + 1) * length] = picked[i * each : (i + 1) * each]


def sort_particles(images, bins, pair, shift, defocus, count, capacity, pieces):
    particles, lines, length = images.shape
    slots = count * capacity
    return pl.pallas_call(
        lambda *refs: sort_kernel(capacity, *refs),
        out_shape=[jax.ShapeDtypeStruct((slots // pieces, lines * length), BF16)] * pieces
        + [jax.ShapeDtypeStruct((8, slots), F32)],
        scratch_shapes=[pltpu.VMEM((length // 128, particles * lines, 128), F32)],
        compiler_params=pltpu.CompilerParams(vmem_limit_bytes=VMEM_LIMIT),
        name="sort_particles",
    )(
        images.reshape(particles * lines, length),
        bins[None, :], pair[None, :], shift[None, :], defocus.astype(F32)[None, :],
    )


def factors(defocus, shift, length):
    half = length // 2
    column = jnp.arange(half + 128, dtype=jnp.int32)
    folded = column.astype(F32) / length
    ctf = -jnp.sin(defocus[:, None] * 1500.0 * (folded * folded)[None, :] + 0.2)
    angles = (shift[:, None] * column[None, :half] % length).astype(F32) * (2.0 * math.pi / length)
    nyquist = ctf[:, half] * (1 - 2 * (shift % 2)).astype(F32)
    cosine = ctf[:, :half] * jnp.cos(angles)
    sine = ctf[:, :half] * jnp.sin(angles)
    cosine_imag = jnp.where(column[None, :half] == 0, nyquist[:, None], cosine)
    keep = (column <= half)[None, :]
    return cosine, cosine_imag, sine, jnp.where(keep, ctf * ctf, 0.0).astype(BF16)


def score_kernel(scale, n_images, n_refs, slab_lines, *refs):
    images, refs = refs[:n_images], refs[n_images:]
    blocks, refs = refs[:n_refs], refs[n_refs:]
    infos, refs = refs[:n_refs], refs[n_refs:]
    table_ref, cos_ref, cosi_ref, sin_ref, power_ref, facts_ref, out_ref, aligned, scores, taps, spread = refs
    step = pl.program_id(0)
    half = cos_ref.shape[1]
    pairs, slots = scores.shape
    rows = out_ref.shape[0]
    length = 2 * half
    lines = aligned.shape[0]
    here = images[0].shape[1] // length

    def chosen():
        pair = facts_ref[1:2, :].astype(jnp.int32)
        return lax.broadcasted_iota(jnp.int32, (pairs, slots), 0) == pair

    @pl.when(step == 0)
    def _():
        scores[...] = jnp.zeros(scores.shape, F32)
        onehot = jnp.where(chosen(), 1.0, 0.0).astype(BF16)
        info = jnp.concatenate([ref[...] for ref in infos], axis=0)
        found = lax.dot_general(
            info, onehot, (((0,), (0,)), ((), ())), preferred_element_type=F32
        )
        put_tiles(taps, found)
        label = found[slab_lines * lines : slab_lines * lines + 1, :].astype(jnp.int32)
        group = lax.broadcasted_iota(jnp.int32, (rows, slots), 0) // (rows // CLASSES)
        spread[...] = jnp.where(group == label, 1.0, 0.0)

    sine = sin_ref[...]
    total = scores[...]
    for i in range(here):
        at = slice(i * length, (i + 1) * length)
        lines_in = jnp.concatenate([ref[:, at] for ref in images], axis=0)
        spectra = jnp.dot(lines_in, table_ref[...], preferred_element_type=F32)
        spectra = spectra.astype(BF16).astype(F32)
        real, imag = spectra[:, :half], spectra[:, half:]
        turned = jnp.concatenate(
            [cos_ref[...] * real + sine * imag, cosi_ref[...] * imag - sine * real], axis=1
        )
        aligned[step * here + i] = turned
        against = jnp.concatenate([ref[:, at] for ref in blocks], axis=0)
        total = total + lax.dot_general(
            against, turned.astype(BF16), (((1,), (1,)), ((), ())), preferred_element_type=F32
        )
    scores[...] = total

    @pl.when(step == pl.num_programs(0) - 1)
    def _():
        score = jnp.sum(jnp.where(chosen(), scores[...], 0.0), axis=0, keepdims=True)
        weight = facts_ref[3:4, :] / (1.0 + jnp.exp(score * (-2.0 * scale)))
        upright = jnp.broadcast_to(weight, (128, slots)).T
        upright = jnp.concatenate([upright] * (length // 128), axis=1)
        slab = jnp.zeros((rows, length), F32)
        tap_sum = jnp.zeros((slab_lines, slots), F32)
        mask = spread[...].reshape(rows // 8, 8, slots)
        for line in range(lines):
            tap = every(taps, line, slab_lines, lines)
            tap_sum = tap_sum + tap
            tap = jnp.concatenate([tap] * (8 // slab_lines), axis=0)
            mixer = (mask * tap[None]).reshape(rows, slots).astype(BF16)
            contrib = (upright * aligned[line]).astype(BF16)
            slab = slab + jnp.dot(mixer, contrib, preferred_element_type=F32)
        tap = jnp.concatenate([tap_sum * weight] * (8 // slab_lines), axis=0)
        mixer = (mask * tap[None]).reshape(rows, slots).astype(BF16)
        out_ref[:, :length] = slab.astype(BF16)
        out_ref[:, length:] = jnp.dot(mixer, power_ref[...], preferred_element_type=F32).astype(BF16)


def score_and_spread(images, references, facts, tables, rows, slab_lines, lines, length):
    slots = sum(a.shape[0] for a in images)
    pairs = sum(a.shape[0] for a in references)
    here = 4
    whole = lambda a: pl.BlockSpec(a.shape, lambda r: (0,) * a.ndim)
    line = lambda a: pl.BlockSpec((a.shape[0], here * length), lambda r: (0, r))
    info = lambda a: pl.BlockSpec((a.shape[0], 128), lambda r: (0, lines * length // 128))
    small = [packed_table(length), *tables, facts]
    width = length + tables[3].shape[1]
    return pl.pallas_call(
        lambda *refs: score_kernel(
            1.0 / math.sqrt(lines * length), len(images), len(references), slab_lines, *refs
        ),
        grid=(lines // here,),
        in_specs=[line(a) for a in images] + [line(a) for a in references]
        + [info(a) for a in references] + [whole(a) for a in small],
        out_specs=pl.BlockSpec((rows, width), lambda r: (0, 0)),
        out_shape=jax.ShapeDtypeStruct((rows, width), BF16),
        scratch_shapes=[
            pltpu.VMEM((lines, slots, length), F32),
            pltpu.VMEM((pairs, slots), F32),
            pltpu.VMEM((slots // 128, 128, 128), F32),
            pltpu.VMEM((rows, slots), F32),
        ],
        compiler_params=pltpu.CompilerParams(vmem_limit_bytes=VMEM_LIMIT),
        name="score_and_spread",
    )(*images, *references, *references, *small)


def finish_kernel(scale, x_ref, slab_ref, weights_ref):
    half = weights_ref.shape[1] // 2
    total = jnp.sum(x_ref[...].astype(F32), axis=0)
    flip = mirror(half)

    def mirrored(part):
        out = jnp.zeros(part.shape, F32)
        for _ in range(3):
            piece = part.astype(BF16)
            out = out + jnp.dot(piece, flip, preferred_element_type=F32)
            part = part - piece.astype(F32)
        return out

    real, imag, power = total[:, :half], total[:, half : 2 * half], total[:, 2 * half : 3 * half] * scale
    first = lax.broadcasted_iota(jnp.int32, real.shape, 1) == 0
    slab_ref[:, :half] = real
    slab_ref[:, half : 2 * half] = jnp.where(first, imag[:, :1], mirrored(real))
    slab_ref[:, 2 * half : 3 * half] = jnp.where(first, 0.0, imag)
    slab_ref[:, 3 * half :] = jnp.where(first, 0.0, -mirrored(imag))
    weights_ref[:, :half] = power
    weights_ref[:, half:] = jnp.where(first, total[:, 3 * half : 3 * half + 1] * scale, mirrored(power))


def finish(received, length, scale):
    rows = received.shape[1]
    return pl.pallas_call(
        lambda *refs: finish_kernel(scale, *refs),
        out_shape=(
            jax.ShapeDtypeStruct((rows, 2 * length), F32),
            jax.ShapeDtypeStruct((rows, length), F32),
        ),
        name="finish_slab",
    )(received)


def on_device(
    images, defocus, owner_of, pair_of, shift_of, projections, interp_weights, pair_class
):
    particles, lines, length = images.shape
    owners = lax.axis_size("owner")
    capacity = 2 * particles // owners
    pairs, slab_lines, _ = interp_weights.shape
    rows = CLASSES * slab_lines
    reach = max(1, capacity // 4)
    count = owners // reach
    here = lax.axis_index("owner")
    owner = owner_of[:, 0]
    pair = (here // count - owner // count) % reach * pairs + pair_of
    info = jnp.concatenate(
        [
            interp_weights.reshape(pairs, slab_lines * lines),
            pair_class.astype(BF16)[:, None],
            jnp.zeros((pairs, 127 - slab_lines * lines), BF16),
        ],
        axis=1,
    )
    references = [fold(projections, info)]
    for shift in range(1, reach):
        ring = [(i, (i + shift * count) % owners) for i in range(owners)]
        references.append(lax.ppermute(references[0], "owner", ring))
    columns = owner % count
    if reach > 1:
        *sorted_lines, facts = sort_particles(
            images, columns ^ here % count, pair, shift_of, defocus, count, reach * capacity, count
        )
        swap = lambda a, i: lax.ppermute(a, "owner", [(k, k ^ i) for k in range(owners)]) if i else a
        arrived = [swap(a, i) for i, a in enumerate(sorted_lines)]
        facts = jnp.concatenate(
            [swap(a, i) for i, a in enumerate(jnp.split(facts, count, axis=1))], axis=1
        )
    else:
        sorted_lines, facts = sort_particles(
            images, columns, pair, shift_of, defocus, count, capacity, 1
        )
        send = lambda a: lax.all_to_all(a, "owner", split_axis=0, concat_axis=0, tiled=True)
        arrived, facts = [send(sorted_lines)], send(facts.T).T
    tables = factors(facts[0], facts[2].astype(jnp.int32), length)
    partial = score_and_spread(
        arrived, references, facts, tables, rows, slab_lines, lines, length
    )
    received = lax.all_to_all(partial, "owner", split_axis=0, concat_axis=0, tiled=True)
    return finish(
        received.reshape(owners, rows // owners, -1), length, CLASSES / (particles * owners)
    )


def solution(mesh):
    return jax.shard_map(
        on_device,
        mesh=mesh,
        in_specs=(
            P(("half", "owner"), None, None),
            P(("half", "owner")),
            P(("half", "owner"), None),
            P(("half", "owner")),
            P(("half", "owner")),
            P(("half", "owner"), None, None),
            P(("half", "owner"), None, None),
            P(("half", "owner")),
        ),
        out_specs=(P(("half", "owner"), None), P(("half", "owner"), None)),
        check_vma=False,
    )
```

time: 152 us -> 93.9 us (0.62)
  waiting for transfers between devices: 69.4 us -> 38.5 us
  blocking collectives: 33.3 us -> 16.7 us
  Pallas kernels: 25 us -> 17.3 us
  starting transfers between devices: 8.49 us -> 13 us
  matrix products: 3.49 us -> 0 us
  local copies, waits for them, and re-layouts: 4.88 us -> 2.46 us
    all_to_all x1 -> x0, waiting for transfers between devices: 69.4 us -> none  [on_device(): lax.all_to_all(packed, 'owner', split_axis=0, concat_axis=0, tiled=True)]
    ppermute x0 -> x9, waiting for transfers between devices: none -> 38.5 us  [the longest x3 36.3 us: on_device(): references.append(lax.ppermute(references[0], 'owner', ring))]
    all_to_all x1, blocking collectives: 33.3 us -> 16.7 us  [on_device(): lax.all_to_all(partial, 'owner', split_axis=0, concat_axis=0, tiled=True)]
    ppermute x0 -> x9, starting transfers between devices: none -> 13 us  [the longest x6 8.5 us: on_device(): lax.ppermute(a, 'owner', [(k, k ^ i) for k in range(owners)])]
    all_to_all x1 -> x0, starting transfers between devices: 8.49 us -> none  [on_device(): lax.all_to_all(packed, 'owner', split_axis=0, concat_axis=0, tiled=True)]
    pallas_call x1 -> x2, Pallas kernels: 9.75 us -> 5.62 us  [the longest x1 4.99 us: sort_particles(): pl.pallas_call(lambda *refs: sort_kernel(capacity, *refs), out_shape=[jax...]
    pallas_call x1, Pallas kernels: 13.3 us -> 9.77 us  [score_and_spread(): pl.pallas_call(lambda *refs: score_kernel(1.0 / math.sqrt(lines * length)...]
    dot_general x2 -> x0, matrix products: 3.49 us -> none  [the longest x1 3.27 us: on_device(): packed = jnp.dot(pick, payload, preferred_element_type=F32).astype(BF16)]
  transfers between devices with their start and end apart: 1 -> 9, of which waited for: 1 -> 4; matrix products, arithmetic and copies ran while one was open for 1% -> 4% of each run, Pallas kernels for 6% -> 1%
where the time goes in v2:
time: 93.9 us; the launch traced here: 93.6 us
  waiting for transfers between devices  38.5 us (41%)
  Pallas kernels  17.3 us (18%)
  blocking collectives  16.7 us (18%)
  starting transfers between devices  13 us (14%)
  other arithmetic  4.99 us (5%)
  local copies, waits for them, and re-layouts  2.46 us (3%)
    ppermute x3, waiting for transfers between devices, on_device(): references.append(lax.ppermute(references[0], 'owner', ring))  36.3 us
    all_to_all x1, blocking collectives, on_device(): lax.all_to_all(partial, 'owner', split_axis=0, concat_axis=0, tiled=True)  16.7 us
    pallas_call x1, Pallas kernels, score_and_spread(): pl.pallas_call(lambda *refs: score_kernel(1.0 / math.sqrt(lines * length)...  9.77 us
    ppermute x6, starting transfers between devices, on_device(): lax.ppermute(a, 'owner', [(k, k ^ i) for k in range(owners)])  8.5 us
    pallas_call x1, Pallas kernels, sort_particles(): pl.pallas_call(lambda *refs: sort_kernel(capacity, *refs), out_shape=[jax...  4.99 us
    ppermute x3, starting transfers between devices, on_device(): references.append(lax.ppermute(references[0], 'owner', ring))  4.48 us
    ppermute x6, waiting for transfers between devices, on_device(): lax.ppermute(a, 'owner', [(k, k ^ i) for k in range(owners)])  2.19 us
    unnamed x14, local copies, waits for them, and re-layouts  1.98 us
  transfers between devices with their start and end apart: 9, of which 4 were waited for; matrix products, arithmetic and copies ran while one was open for 4% of the time, Pallas kernels for 1%

profile of v2, /device:TPU:0, one launch (start us, length us, event | category | flops | bytes accessed | tf_op | source)
XLA Modules:
  0.0 93.6 jit_solution(14155623704576781036)
XLA Ops:
  0.7 0.7 bitcast_convert_fusion.refs_4_
  1.4 0.7 fusion.10.refs_1_
  2.1 0.7 fusion.15.refs_2_
  2.8 0.6 copy-done.2
  3.4 5.0 %sort_particles.1 = (bf16[64,8192]{1,0:T(8,128)(2,1)S(1)}, bf16[64,8192]{1,0:T(8,128)(2,1)}, bf16[64,8192]{1,0:T(8,128)(2,1)S(1)}, bf16[64,8192]{1,0:T(8,128)(2,1)S(1)}, f32[8,256]{1,0:T(8,128)S(1)}) custom-call(bf16[2048,512]{1,0:T(8,128)(2,1)} %bitcast.33, s32[1,128]{1,0:T(1,128)S(1)} %fusion.10.refs_1_, s32[1,128]{1,0:T(1,128)S(1)} %fusion.15.refs_2_, ...), custom_call_target="tpu_custom_call" | custom-call | tf_op jit(solution)/shard_map/sort_particles/pallas_call | solution.py:109
  8.5 0.9 copy-done.3
  9.4 0.4 copy-done.4
  9.8 2.9 %collective-permute-start.6 = (f32[8,64]{1,0:T(8,128)S(1)}, f32[8,64]{1,0:T(8,128)S(1)}, u32[]{:S(2)}, u32[]{:S(2)}) collective-permute-start(f32[8,64]{1,0:T(8,128)S(1)} %get-tuple-element.21), channel_id=1, source_target_pairs={{0,1},{1,0},{2,3},{3,2},{4,5},{5,4},{6,7},{7,6},{8,9},{9,8},{10,11... | collective-permute-start | bytes 6152 | tf_op jit(solution)/shard_map/ppermute | solution.py:300
  12.7 1.5 %collective-permute-start.7 = (f32[8,64]{1,0:T(8,128)S(1)}, f32[8,64]{1,0:T(8,128)S(1)}, u32[]{:S(2)}, u32[]{:S(2)}) collective-permute-start(f32[8,64]{1,0:T(8,128)S(1)} %get-tuple-element.20), channel_id=1, source_target_pairs={{0,2},{1,3},{2,0},{3,1},{4,6},{5,7},{6,4},{7,5},{8,10},{9,11},{10,... | collective-permute-start | bytes 6152 | tf_op jit(solution)/shard_map/ppermute | solution.py:300
  14.3 2.0 %collective-permute-start = (bf16[64,8192]{1,0:T(8,128)(2,1)}, bf16[64,8192]{1,0:T(8,128)(2,1)}, u32[]{:S(2)}, u32[]{:S(2)}) collective-permute-start(bf16[64,8192]{1,0:T(8,128)(2,1)} %get-tuple-element.8), channel_id=1, source_target_pairs={{0,1},{1,0},{2,3},{3,2},{4,5},{5,4},{6,7},{7,6},{8,9},{9,8},{10,11... | collective-permute-start | bytes 3145736 | tf_op jit(solution)/shard_map/ppermute | solution.py:300
  16.6 0.6 fold_projections.1.refs_4_.refs_8_
  17.2 1.6 %collective-permute-start.3 = (bf16[32,8320]{1,0:T(8,128)(2,1)S(1)}, bf16[32,8320]{1,0:T(8,128)(2,1)S(1)}, u32[]{:S(2)}, u32[]{:S(2)}) collective-permute-start(bf16[32,8320]{1,0:T(8,128)(2,1)S(1)} %fold_projections.1.refs_4_.refs_8_), channel_id=1, source_target_pairs={{0,4},{1,5},{2,6},{3,7},{4,8},{5,9},{6,10},{7,11},{8,12},{9,13},{1... | collective-permute-start | bytes 1597448 | tf_op jit(solution)/shard_map/ppermute | solution.py:294
  18.9 1.6 %collective-permute-start.1 = (bf16[64,8192]{1,0:T(8,128)(2,1)}, bf16[64,8192]{1,0:T(8,128)(2,1)}, u32[]{:S(2)}, u32[]{:S(2)}) collective-permute-start(bf16[64,8192]{1,0:T(8,128)(2,1)} %copy-done.4), channel_id=1, source_target_pairs={{0,2},{1,3},{2,0},{3,1},{4,6},{5,7},{6,4},{7,5},{8,10},{9,11},{10,... | collective-permute-start | bytes 3145736 | tf_op jit(solution)/shard_map/ppermute | solution.py:300
  20.5 0.5 collective-permute-start.2
  21.0 2.7 %collective-permute-start.4 = (bf16[32,8320]{1,0:T(8,128)(2,1)S(1)}, bf16[32,8320]{1,0:T(8,128)(2,1)S(1)}, u32[]{:S(2)}, u32[]{:S(2)}) collective-permute-start(bf16[32,8320]{1,0:T(8,128)(2,1)S(1)} %fold_projections.1.refs_4_.refs_8_), channel_id=1, source_target_pairs={{0,8},{1,9},{2,10},{3,11},{4,12},{5,13},{6,14},{7,15},{8,0},{9,1},... | collective-permute-start | bytes 1597448 | tf_op jit(solution)/shard_map/ppermute | solution.py:294
  23.9 10.4 %collective-permute-done.3.refs_5_.refs_9_ = bf16[32,8320]{1,0:T(8,128)(2,1)S(1)} collective-permute-done((bf16[32,8320]{1,0:T(8,128)(2,1)S(1)}, bf16[32,8320]{1,0:T(8,128)(2,1)S(1)}, u32[]{:S(2)}, u32[]{:S(2)}) %collective-permute-start.3) | collective-permute-done | bytes 532512 | tf_op jit(solution)/shard_map/ppermute | solution.py:294
  34.4 1.4 %select_convert_fusion = (bf16[256,384]{1,0:T(8,128)(2,1)S(1)}, f32[256,384]{1,0:T(8,128)S(1)}) fusion(f32[384]{0:T(512)S(1)} %multiply_multiply_fusion, f32[256]{0:T(256)S(1)} %bitcast.36, pred[384]{0:T(512)(128)(4,1)S(1)} %iota_compare_fusion), kind=kLoop, calls=%fused_computation.3 | loop fusion | flops 589824 | bytes 592768 | tf_op jit(solution)/shard_map/convert_element_type | solution.py:133
  36.0 1.1 %broadcast_select_fusion = (f32[256,256]{1,0:T(8,128)S(1)}, f32[256,256]{1,0:T(8,128)S(1)}, f32[256,256]{1,0:T(8,128)S(1)}) fusion(f32[256]{0:T(256)S(1)} %fusion.9, pred[256]{0:T(512)(128)(4,1)S(1)} %broadcast_compare_fusion, s32[256]{0:T(256)S(1)} %slice.22, s32[256]{0:T(256)S(1)} %bitcast.35, f32[256,384]{1,0:T(8,128)S(1)} %get-tuple-element.23), kind=kLoop, calls=%fused_computation.22 | loop fusion | flops 1114112 | bytes 1051904 | tf_op jit(solution)/shard_map/jit(_where)/select_n | solution.py:131
  37.1 17.7 %collective-permute-done.4.refs_6_.refs_10_ = bf16[32,8320]{1,0:T(8,128)(2,1)S(1)} collective-permute-done((bf16[32,8320]{1,0:T(8,128)(2,1)S(1)}, bf16[32,8320]{1,0:T(8,128)(2,1)S(1)}, u32[]{:S(2)}, u32[]{:S(2)}) %collective-permute-start.4) | collective-permute-done | bytes 532512 | tf_op jit(solution)/shard_map/ppermute | solution.py:294
  54.8 8.2 %collective-permute-done.5.refs_7_.refs_11_ = bf16[32,8320]{1,0:T(8,128)(2,1)S(1)} collective-permute-done((bf16[32,8320]{1,0:T(8,128)(2,1)S(1)}, bf16[32,8320]{1,0:T(8,128)(2,1)S(1)}, u32[]{:S(2)}, u32[]{:S(2)}) %collective-permute-start.5) | collective-permute-done | bytes 532512 | tf_op jit(solution)/shard_map/ppermute | solution.py:294
  63.1 2.2 %collective-permute-done.1.refs_2_ = bf16[64,8192]{1,0:T(8,128)(2,1)} collective-permute-done((bf16[64,8192]{1,0:T(8,128)(2,1)}, bf16[64,8192]{1,0:T(8,128)(2,1)}, u32[]{:S(2)}, u32[]{:S(2)}) %collective-permute-start.1) | collective-permute-done | bytes 1048608 | tf_op jit(solution)/shard_map/ppermute | solution.py:300
  65.2 9.8 %score_and_spread.1 = bf16[256,896]{1,0:T(8,128)(2,1)S(1)} custom-call(bf16[64,8192]{1,0:T(8,128)(2,1)S(1)} %get-tuple-element.7.refs_0_, bf16[64,8192]{1,0:T(8,128)(2,1)} %collective-permute-done.refs_1_, bf16[64,8192]{1,0:T(8,128)(2,1)} %collective-permute-done.1.refs_2_, bf16[64,8192]{1,0:T(8,128)(2,1)} %collective-permute-done.2.refs_3_, ...), custom_call_target="tpu_custom_call" | custom-call | tf_op jit(solution)/shard_map/score_and_spread/pallas_call | solution.py:215
  75.0 16.7 %all_to_all.9.refs_0_ = bf16[16,16,896]{2,1,0:T(8,128)(2,1)} all-to-all(bf16[16,16,896]{2,1,0:T(8,128)(2,1)S(1)} %bitcast.30), channel_id=1, replica_groups=mesh['half'=2,'owner'=16] {'owner'}, dimensions={0} | all-to-all | bytes 917504 | tf_op jit(solution)/shard_map/all_to_all | solution.py:315
  91.7 1.9 %finish_slab.1 = (f32[16,1024]{1,0:T(8,128)}, f32[16,512]{1,0:T(8,128)}) custom-call(bf16[16,16,896]{2,1,0:T(8,128)(2,1)} %all_to_all.9.refs_0_), custom_call_target="tpu_custom_call" | custom-call | tf_op jit(solution)/shard_map/finish_slab/pallas_call | solution.py:260
  (34 shorter events, 1.1 us)
Async XLA Ops:
  0.6 16.0 %copy-start = (bf16[32,16,1024]{2,1,0:T(8,128)(2,1)S(1)}, bf16[32,16,1024]{2,1,0:T(8,128)(2,1)}, u32[]{:S(2)}) copy-start(bf16[32,16,1024]{2,1,0:T(8,128)(2,1)} %param.14) | copy-start | bytes 3145732
  2.8 0.7 copy-start.2
  3.4 12.8 %copy-start.6 = (s32[32]{0:T(128)S(1)}, s32[32]{0:T(128)}, u32[]{:S(2)}) copy-start(s32[32]{0:T(128)} %param.16) | copy-start | bytes 388
  3.4 12.9 %copy-start.5 = (bf16[32,4,16]{0,2,1:T(8,128)(2,1)S(1)}, bf16[32,4,16]{0,2,1:T(8,128)(2,1)}, u32[]{:S(2)}) copy-start(bf16[32,4,16]{0,2,1:T(8,128)(2,1)} %param.15) | copy-start | bytes 12292
  8.4 1.0 %copy-start.3 = (bf16[64,8192]{1,0:T(8,128)(2,1)}, bf16[64,8192]{1,0:T(8,128)(2,1)S(1)}, u32[]{:S(2)}) copy-start(bf16[64,8192]{1,0:T(8,128)(2,1)S(1)} %get-tuple-element.10) | copy-start | bytes 3145732
  8.4 1.4 %copy-start.4 = (bf16[64,8192]{1,0:T(8,128)(2,1)}, bf16[64,8192]{1,0:T(8,128)(2,1)S(1)}, u32[]{:S(2)}) copy-start(bf16[64,8192]{1,0:T(8,128)(2,1)S(1)} %get-tuple-element.9) | copy-start | bytes 3145732
  8.4 56.8 %copy-start.1 = (bf16[512,512]{1,0:T(8,128)(2,1)S(1)}, bf16[512,512]{1,0:T(8,128)(2,1)}, u32[]{:S(2)}) copy-start(bf16[512,512]{1,0:T(8,128)(2,1)} %constant.101.refs_12_) | copy-start | bytes 1572868
  9.8 9.1 %collective-permute-start.6 = (f32[8,64]{1,0:T(8,128)S(1)}, f32[8,64]{1,0:T(8,128)S(1)}, u32[]{:S(2)}, u32[]{:S(2)}) collective-permute-start(f32[8,64]{1,0:T(8,128)S(1)} %get-tuple-element.21), channel_id=1, source_target_pairs={{0,1},{1,0},{2,3},{3,2},{4,5},{5,4},{6,7},{7,6},{8,9},{9,8},{10,11... | collective-permute-start | bytes 6152 | tf_op jit(solution)/shard_map/ppermute | solution.py:300
  12.7 7.7 %collective-permute-start.7 = (f32[8,64]{1,0:T(8,128)S(1)}, f32[8,64]{1,0:T(8,128)S(1)}, u32[]{:S(2)}, u32[]{:S(2)}) collective-permute-start(f32[8,64]{1,0:T(8,128)S(1)} %get-tuple-element.20), channel_id=1, source_target_pairs={{0,2},{1,3},{2,0},{3,1},{4,6},{5,7},{6,4},{7,5},{8,10},{9,11},{10,... | collective-permute-start | bytes 6152 | tf_op jit(solution)/shard_map/ppermute | solution.py:300
  14.3 6.7 %collective-permute-start.8 = (f32[8,64]{1,0:T(8,128)S(1)}, f32[8,64]{1,0:T(8,128)S(1)}, u32[]{:S(2)}, u32[]{:S(2)}) collective-permute-start(f32[8,64]{1,0:T(8,128)S(1)} %get-tuple-element.19), channel_id=1, source_target_pairs={{0,3},{1,2},{2,1},{3,0},{4,7},{5,6},{6,5},{7,4},{8,11},{9,10},{10,... | collective-permute-start | bytes 6152 | tf_op jit(solution)/shard_map/ppermute | solution.py:300
  14.3 48.8 %collective-permute-start = (bf16[64,8192]{1,0:T(8,128)(2,1)}, bf16[64,8192]{1,0:T(8,128)(2,1)}, u32[]{:S(2)}, u32[]{:S(2)}) collective-permute-start(bf16[64,8192]{1,0:T(8,128)(2,1)} %get-tuple-element.8), channel_id=1, source_target_pairs={{0,1},{1,0},{2,3},{3,2},{4,5},{5,4},{6,7},{7,6},{8,9},{9,8},{10,11... | collective-permute-start | bytes 3145736 | tf_op jit(solution)/shard_map/ppermute | solution.py:300
  17.2 17.0 %collective-permute-start.3 = (bf16[32,8320]{1,0:T(8,128)(2,1)S(1)}, bf16[32,8320]{1,0:T(8,128)(2,1)S(1)}, u32[]{:S(2)}, u32[]{:S(2)}) collective-permute-start(bf16[32,8320]{1,0:T(8,128)(2,1)S(1)} %fold_projections.1.refs_4_.refs_8_), channel_id=1, source_target_pairs={{0,4},{1,5},{2,6},{3,7},{4,8},{5,9},{6,10},{7,11},{8,12},{9,13},{1... | collective-permute-start | bytes 1597448 | tf_op jit(solution)/shard_map/ppermute | solution.py:294
  18.9 46.4 %collective-permute-start.1 = (bf16[64,8192]{1,0:T(8,128)(2,1)}, bf16[64,8192]{1,0:T(8,128)(2,1)}, u32[]{:S(2)}, u32[]{:S(2)}) collective-permute-start(bf16[64,8192]{1,0:T(8,128)(2,1)} %copy-done.4), channel_id=1, source_target_pairs={{0,2},{1,3},{2,0},{3,1},{4,6},{5,7},{6,4},{7,5},{8,10},{9,11},{10,... | collective-permute-start | bytes 3145736 | tf_op jit(solution)/shard_map/ppermute | solution.py:300
  20.5 44.8 %collective-permute-start.2 = (bf16[64,8192]{1,0:T(8,128)(2,1)}, bf16[64,8192]{1,0:T(8,128)(2,1)}, u32[]{:S(2)}, u32[]{:S(2)}) collective-permute-start(bf16[64,8192]{1,0:T(8,128)(2,1)} %copy-done.3), channel_id=1, source_target_pairs={{0,3},{1,2},{2,1},{3,0},{4,7},{5,6},{6,5},{7,4},{8,11},{9,10},{10,... | collective-permute-start | bytes 3145736 | tf_op jit(solution)/shard_map/ppermute | solution.py:300
  21.0 33.8 %collective-permute-start.4 = (bf16[32,8320]{1,0:T(8,128)(2,1)S(1)}, bf16[32,8320]{1,0:T(8,128)(2,1)S(1)}, u32[]{:S(2)}, u32[]{:S(2)}) collective-permute-start(bf16[32,8320]{1,0:T(8,128)(2,1)S(1)} %fold_projections.1.refs_4_.refs_8_), channel_id=1, source_target_pairs={{0,8},{1,9},{2,10},{3,11},{4,12},{5,13},{6,14},{7,15},{8,0},{9,1},... | collective-permute-start | bytes 1597448 | tf_op jit(solution)/shard_map/ppermute | solution.py:294
  34.2 28.8 %collective-permute-start.5 = (bf16[32,8320]{1,0:T(8,128)(2,1)S(1)}, bf16[32,8320]{1,0:T(8,128)(2,1)S(1)}, u32[]{:S(2)}, u32[]{:S(2)}) collective-permute-start(bf16[32,8320]{1,0:T(8,128)(2,1)S(1)} %fold_projections.1.refs_4_.refs_8_), channel_id=1, source_target_pairs={{0,12},{1,13},{2,14},{3,15},{4,0},{5,1},{6,2},{7,3},{8,4},{9,5},{1... | collective-permute-start | bytes 1597448 | tf_op jit(solution)/shard_map/ppermute | solution.py:294

commit v3 on v2

--- a/solution.py
+++ b/solution.py
@@ -70,53 +70,81 @@
     )(projections.reshape(pairs * lines, width), info)
 
 
-def sort_kernel(capacity, x_ref, bin_ref, pair_ref, shift_ref, defocus_ref, *refs):
-    outs, facts_ref, wide = refs[:-2], refs[-2], refs[-1]
-    particles = bin_ref.shape[1]
+def sort_kernel(reach, count, capacity, pairs, x_ref, owner_ref, pair_ref, shift_ref, defocus_ref, *refs):
+    *outs, wide, pick_ref = refs
+    pieces = len(outs) // 2
+    outs, facts_refs = outs[:pieces], outs[pieces:]
+    particles = owner_ref.shape[1]
     length = x_ref.shape[1]
     lines = x_ref.shape[0] // particles
-    slots = facts_ref.shape[1]
-    bins = -(-(slots // capacity) // 8) * 8
-    hits = lax.broadcasted_iota(jnp.int32, (bins, particles), 0) == bin_ref[...]
-    row = lax.broadcasted_iota(jnp.int32, (particles, particles), 0)
-    column = lax.broadcasted_iota(jnp.int32, (particles, particles), 1)
-    before = jnp.where(row < column, 1.0, 0.0).astype(BF16)
-    earlier = jnp.dot(jnp.where(hits, 1.0, 0.0).astype(BF16), before, preferred_element_type=F32)
-    earlier = jnp.sum(jnp.where(hits, earlier, 0.0), axis=0, keepdims=True)
-    place = bin_ref[...] * capacity + earlier.astype(jnp.int32)
-    pick = lax.broadcasted_iota(jnp.int32, (slots, particles), 0) == place
-    pick = jnp.where(pick, 1.0, 0.0).astype(BF16)
-    kind = lax.broadcasted_iota(jnp.int32, (8, particles), 0)
-    facts = jnp.where(kind == 0, defocus_ref[...], jnp.ones((8, particles), F32))
-    facts = jnp.where(kind == 1, pair_ref[...].astype(F32), facts)
-    facts = jnp.where(kind == 2, shift_ref[...].astype(F32), facts).astype(BF16)
-    facts_ref[...] = lax.dot_general(
-        facts, pick, (((1,), (1,)), ((), ())), preferred_element_type=F32
-    )
-    put_tiles(wide, x_ref[...].astype(F32))
-    for line in range(lines):
-        picked = jnp.dot(
-            pick, every(wide, line, particles, lines).astype(BF16), preferred_element_type=F32
-        ).astype(BF16)
-        each = slots // len(outs)
-        for i, out_ref in enumerate(outs):
-            out_ref[:, line * length : (line + 1) * length] = picked[i * each : (i + 1) * each]
-
-
-def sort_particles(images, bins, pair, shift, defocus, count, capacity, pieces):
+    slots = pick_ref.shape[0]
+    each = slots // pieces
+
+    @pl.when(pl.program_id(0) == 0)
+    def _():
+        me = lax.axis_index("owner")
+        owner = owner_ref[...]
+        bins = owner & (count - 1)
+        if pieces > 1:
+            bins = bins ^ (me & (count - 1))
+        step = ((me >> (count.bit_length() - 1)) - (owner >> (count.bit_length() - 1))) & (reach - 1)
+        pair = step * pairs + pair_ref[...]
+        padded = -(-count // 8) * 8
+        hits = lax.broadcasted_iota(jnp.int32, (padded, particles), 0) == bins
+        row = lax.broadcasted_iota(jnp.int32, (particles, particles), 0)
+        column = lax.broadcasted_iota(jnp.int32, (particles, particles), 1)
+        before = jnp.where(row < column, 1.0, 0.0).astype(BF16)
+        earlier = jnp.dot(
+            jnp.where(hits, 1.0, 0.0).astype(BF16), before, preferred_element_type=F32
+        )
+        earlier = jnp.sum(jnp.where(hits, earlier, 0.0), axis=0, keepdims=True)
+        place = bins * capacity + earlier.astype(jnp.int32)
+        pick = lax.broadcasted_iota(jnp.int32, (slots, particles), 0) == place
+        pick_ref[...] = jnp.where(pick, 1.0, 0.0).astype(BF16)
+        kind = lax.broadcasted_iota(jnp.int32, (8, particles), 0)
+        facts = jnp.where(kind == 0, defocus_ref[...].astype(F32), jnp.ones((8, particles), F32))
+        facts = jnp.where(kind == 1, pair.astype(F32), facts)
+        facts = jnp.where(kind == 2, shift_ref[...].astype(F32), facts).astype(BF16)
+        for i, facts_ref in enumerate(facts_refs):
+            facts_ref[...] = lax.dot_general(
+                facts,
+                pick_ref[i * each : (i + 1) * each],
+                (((1,), (1,)), ((), ())),
+                preferred_element_type=F32,
+            )
+        put_tiles(wide, x_ref[...].astype(F32))
+
+    here = outs[0].shape[1] // length
+    for i in range(here):
+        line = pl.program_id(0) * here + i
+        rows = every(wide, line, particles, lines).astype(BF16)
+        picked = jnp.dot(pick_ref[...], rows, preferred_element_type=F32).astype(BF16)
+        for j, out_ref in enumerate(outs):
+            out_ref[:, i * length : (i + 1) * length] = picked[j * each : (j + 1) * each]
+
+
+def sort_particles(images, owner, pair, shift, defocus, reach, count, capacity, pairs, pieces):
     particles, lines, length = images.shape
     slots = count * capacity
+    each = slots // pieces
+    here = 4
+    whole = lambda a: pl.BlockSpec(a.shape, lambda r: (0,) * a.ndim)
+    args = [images.reshape(particles * lines, length)] + [a[None, :] for a in (owner, pair, shift, defocus)]
     return pl.pallas_call(
-        lambda *refs: sort_kernel(capacity, *refs),
-        out_shape=[jax.ShapeDtypeStruct((slots // pieces, lines * length), BF16)] * pieces
-        + [jax.ShapeDtypeStruct((8, slots), F32)],
-        scratch_shapes=[pltpu.VMEM((length // 128, particles * lines, 128), F32)],
+        lambda *refs: sort_kernel(reach, count, capacity, pairs, *refs),
+        grid=(lines // here,),
+        in_specs=[whole(a) for a in args],
+        out_specs=[pl.BlockSpec((each, here * length), lambda r: (0, r))] * pieces
+        + [pl.BlockSpec((8, each), lambda r: (0, 0))] * pieces,
+        out_shape=[jax.ShapeDtypeStruct((each, lines * length), BF16)] * pieces
+        + [jax.ShapeDtypeStruct((8, each), F32)] * pieces,
+        scratch_shapes=[
+            pltpu.VMEM((length // 128, particles * lines, 128), F32),
+            pltpu.VMEM((slots, particles), BF16),
+        ],
         compiler_params=pltpu.CompilerParams(vmem_limit_bytes=VMEM_LIMIT),
         name="sort_particles",
-    )(
-        images.reshape(particles * lines, length),
-        bins[None, :], pair[None, :], shift[None, :], defocus.astype(F32)[None, :],
-    )
+    )(*args)
 
 
 def factors(defocus, shift, length):
@@ -133,7 +161,19 @@
     return cosine, cosine_imag, sine, jnp.where(keep, ctf * ctf, 0.0).astype(BF16)
 
 
-def score_kernel(scale, n_images, n_refs, slab_lines, *refs):
+def joined(refs, sizes, at):
+    blocks, start = [], 0
+    for size in sizes:
+        block = refs[start][:, at]
+        for ref in refs[start + 1 : start + size]:
+            block = block + ref[:, at]
+        blocks.append(block)
+        start += size
+    return jnp.concatenate(blocks, axis=0)
+
+
+def score_kernel(scale, n_images, sizes, slab_lines, *refs):
+    n_refs = sum(sizes)
     images, refs = refs[:n_images], refs[n_images:]
     blocks, refs = refs[:n_refs], refs[n_refs:]
     infos, refs = refs[:n_refs], refs[n_refs:]
@@ -154,7 +194,7 @@
     def _():
         scores[...] = jnp.zeros(scores.shape, F32)
         onehot = jnp.where(chosen(), 1.0, 0.0).astype(BF16)
-        info = jnp.concatenate([ref[...] for ref in infos], axis=0)
+        info = joined(infos, sizes, slice(None))
         found = lax.dot_general(
             info, onehot, (((0,), (0,)), ((), ())), preferred_element_type=F32
         )
@@ -175,7 +215,7 @@
             [cos_ref[...] * real + sine * imag, cosi_ref[...] * imag - sine * real], axis=1
         )
         aligned[step * here + i] = turned
-        against = jnp.concatenate([ref[:, at] for ref in blocks], axis=0)
+        against = joined(blocks, sizes, at)
         total = total + lax.dot_general(
             against, turned.astype(BF16), (((1,), (1,)), ((), ())), preferred_element_type=F32
         )
@@ -205,7 +245,9 @@
 
 def score_and_spread(images, references, facts, tables, rows, slab_lines, lines, length):
     slots = sum(a.shape[0] for a in images)
-    pairs = sum(a.shape[0] for a in references)
+    pairs = sum(a[0].shape[0] for a in references)
+    sizes = [len(a) for a in references]
+    references = [a for blocks in references for a in blocks]
     here = 4
     whole = lambda a: pl.BlockSpec(a.shape, lambda r: (0,) * a.ndim)
     line = lambda a: pl.BlockSpec((a.shape[0], here * length), lambda r: (0, r))
@@ -214,7 +256,7 @@
     width = length + tables[3].shape[1]
     return pl.pallas_call(
         lambda *refs: score_kernel(
-            1.0 / math.sqrt(lines * length), len(images), len(references), slab_lines, *refs
+            1.0 / math.sqrt(lines * length), len(images), sizes, slab_lines, *refs
         ),
         grid=(lines // here,),
         in_specs=[line(a) for a in images] + [line(a) for a in references]
@@ -267,6 +309,17 @@
     )(received)
 
 
+def gather_rows(block, owners, reach, count):
+    turn = lambda i: lax.ppermute(block, "owner", [(k, (k + i * count) % owners) for k in range(owners)])
+    if reach != 4:
+        return [(block,)] + [(turn(i),) for i in range(1, reach)]
+    back, ahead = turn(1), turn(3)
+    inner = range(count, 3 * count)
+    up = lax.ppermute(back, "owner", [(k, k + count) for k in inner])
+    down = lax.ppermute(ahead, "owner", [(k, k - count) for k in inner])
+    return [(block,), (back,), (up, down), (ahead,)]
+
+
 def on_device(
     images, defocus, owner_of, pair_of, shift_of, projections, interp_weights, pair_class
 ):
@@ -277,9 +330,19 @@
     rows = CLASSES * slab_lines
     reach = max(1, capacity // 4)
     count = owners // reach
-    here = lax.axis_index("owner")
     owner = owner_of[:, 0]
-    pair = (here // count - owner // count) % reach * pairs + pair_of
+    pieces = count if reach > 1 else 1
+    moved = sort_particles(
+        images, owner, pair_of, shift_of, defocus, reach, count, reach * capacity, pairs, pieces
+    )
+    lines_out, facts_out = moved[:pieces], moved[pieces:]
+    if reach > 1:
+        swap = lambda a, i: lax.ppermute(a, "owner", [(k, k ^ i) for k in range(owners)]) if i else a
+        arrived = [swap(a, i) for i, a in enumerate(lines_out)]
+        facts = jnp.concatenate([swap(a, i) for i, a in enumerate(facts_out)], axis=1)
+    else:
+        send = lambda a: lax.all_to_all(a, "owner", split_axis=0, concat_axis=0, tiled=True)
+        arrived, facts = [send(lines_out[0])], send(facts_out[0].T).T
     info = jnp.concatenate(
         [
             interp_weights.reshape(pairs, slab_lines * lines),
@@ -288,26 +351,7 @@
         ],
         axis=1,
     )
-    references = [fold(projections, info)]
-    for shift in range(1, reach):
-        ring = [(i, (i + shift * count) % owners) for i in range(owners)]
-        references.append(lax.ppermute(references[0], "owner", ring))
-    columns = owner % count
-    if reach > 1:
-        *sorted_lines, facts = sort_particles(
-            images, columns ^ here % count, pair, shift_of, defocus, count, reach * capacity, count
-        )
-        swap = lambda a, i: lax.ppermute(a, "owner", [(k, k ^ i) for k in range(owners)]) if i else a
-        arrived = [swap(a, i) for i, a in enumerate(sorted_lines)]
-        facts = jnp.concatenate(
-            [swap(a, i) for i, a in enumerate(jnp.split(facts, count, axis=1))], axis=1
-        )
-    else:
-        sorted_lines, facts = sort_particles(
-            images, columns, pair, shift_of, defocus, count, capacity, 1
-        )
-        send = lambda a: lax.all_to_all(a, "owner", split_axis=0, concat_axis=0, tiled=True)
-        arrived, facts = [send(sorted_lines)], send(facts.T).T
+    references = gather_rows(fold(projections, info), owners, reach, count)
     tables = factors(facts[0], facts[2].astype(jnp.int32), length)
     partial = score_and_spread(
         arrived, references, facts, tables, rows, slab_lines, lines, length

time: 93.9 us -> 97.4 us (1.037)
  local copies, waits for them, and re-layouts: 2.46 us -> 4.98 us
  Pallas kernels: 17.3 us -> 19 us
  blocking collectives: 16.7 us -> 15.2 us
  other arithmetic: 4.99 us -> 3.55 us
  starting transfers between devices: 13 us -> 14.1 us
  waiting for transfers between devices: 38.5 us -> 39.5 us
    ppermute x6, waiting for transfers between devices: 2.19 us -> 34.5 us  [on_device(): lax.ppermute(a, 'owner', [(k, k ^ i) for k in range(owners)])]
    ppermute x3 -> x4, waiting for transfers between devices: 36.3 us -> 4.97 us  [the longest x2 4.97 us: gather_rows(): lax.ppermute(block, 'owner', [(k, (k + i * count) % owners) for k in rang...]
    ppermute x3 -> x4, starting transfers between devices: 4.48 us -> 7.13 us  [the longest x2 5.16 us: gather_rows(): lax.ppermute(block, 'owner', [(k, (k + i * count) % owners) for k in rang...]
    unnamed x14 -> x12, local copies, waits for them, and re-layouts: 1.98 us -> 3.86 us
    ppermute x6, starting transfers between devices: 8.5 us -> 6.97 us  [on_device(): lax.ppermute(a, 'owner', [(k, k ^ i) for k in range(owners)])]
    all_to_all x1, blocking collectives: 16.7 us -> 15.2 us  [on_device(): lax.all_to_all(partial, 'owner', split_axis=0, concat_axis=0, tiled=True)]
    broadcast_in_dim x2 -> x0, other arithmetic: 1.43 us -> none  [the longest x1 0.74 us: sort_particles(): defocus.astype(F32)[None, :]]
    pallas_call x1, Pallas kernels: 4.99 us -> 6.24 us  [sort_particles(): pl.pallas_call(lambda *refs: sort_kernel(reach, count, capacity, pairs, *...]
  transfers between devices with their start and end apart: 9 -> 10, of which waited for: 4 -> 5; matrix products, arithmetic and copies ran while one was open for 4% -> 3% of each run, Pallas kernels for 1% -> 6%
where the time goes in v3:
time: 97.4 us; the launch traced here: 97 us
  waiting for transfers between devices  39.5 us (41%)
  Pallas kernels  19 us (20%)
  blocking collectives  15.2 us (16%)
  starting transfers between devices  14.1 us (14%)
  local copies, waits for them, and re-layouts  4.98 us (5%)
  other arithmetic  3.55 us (4%)
    ppermute x6, waiting for transfers between devices, on_device(): lax.ppermute(a, 'owner', [(k, k ^ i) for k in range(owners)])  34.5 us
    all_to_all x1, blocking collectives, on_device(): lax.all_to_all(partial, 'owner', split_axis=0, concat_axis=0, tiled=True)  15.2 us
    pallas_call x1, Pallas kernels, score_and_spread(): pl.pallas_call(lambda *refs: score_kernel(1.0 / math.sqrt(lines * length)...  10.2 us
    ppermute x6, starting transfers between devices, on_device(): lax.ppermute(a, 'owner', [(k, k ^ i) for k in range(owners)])  6.97 us
    pallas_call x1, Pallas kernels, sort_particles(): pl.pallas_call(lambda *refs: sort_kernel(reach, count, capacity, pairs, *...  6.24 us
    ppermute x2, starting transfers between devices, gather_rows(): lax.ppermute(block, 'owner', [(k, (k + i * count) % owners) for k in rang...  5.16 us
    ppermute x2, waiting for transfers between devices, gather_rows(): lax.ppermute(block, 'owner', [(k, (k + i * count) % owners) for k in rang...  4.97 us
    unnamed x12, local copies, waits for them, and re-layouts  3.86 us
  transfers between devices with their start and end apart: 10, of which 5 were waited for; matrix products, arithmetic and copies ran while one was open for 3% of the time, Pallas kernels for 6%

profile of v3, /device:TPU:0, one launch (start us, length us, event | category | flops | bytes accessed | tf_op | source)
XLA Modules:
  0.0 97.0 jit_solution(403879771241889784)
XLA Ops:
  0.6 0.7 convert_bitcast_fusion
  1.4 0.8 copy.13
  2.4 1.2 %copy-done = bf16[32,16,1024]{2,1,0:T(8,128)(2,1)S(1)} copy-done((bf16[32,16,1024]{2,1,0:T(8,128)(2,1)S(1)}, bf16[32,16,1024]{2,1,0:T(8,128)(2,1)}, u32[]{:S(2)}) %copy-start) | copy-done | bytes 1048600
  4.2 3.1 %collective-permute-start.3 = (bf16[32,8320]{1,0:T(8,128)(2,1)S(1)}, bf16[32,8320]{1,0:T(8,128)(2,1)S(1)}, u32[]{:S(2)}, u32[]{:S(2)}) collective-permute-start(bf16[32,8320]{1,0:T(8,128)(2,1)S(1)} %fold_projections.1.refs_4_.refs_9_), channel_id=1, source_target_pairs={{0,4},{1,5},{2,6},{3,7},{4,8},{5,9},{6,10},{7,11},{8,12},{9,13},{1... | collective-permute-start | bytes 1597448 | tf_op jit(solution)/shard_map/ppermute | solution.py:313
  7.3 2.1 %collective-permute-start.5 = (bf16[32,8320]{1,0:T(8,128)(2,1)S(1)}, bf16[32,8320]{1,0:T(8,128)(2,1)S(1)}, u32[]{:S(2)}, u32[]{:S(2)}) collective-permute-start(bf16[32,8320]{1,0:T(8,128)(2,1)S(1)} %fold_projections.1.refs_4_.refs_9_), channel_id=1, source_target_pairs={{0,12},{1,13},{2,14},{3,15},{4,0},{5,1},{6,2},{7,3},{8,4},{9,5},{1... | collective-permute-start | bytes 1597448 | tf_op jit(solution)/shard_map/ppermute | solution.py:313
  9.4 0.7 copy-done.2
  10.0 0.7 copy-done.3
  10.7 0.7 copy-done.4
  12.0 6.2 %sort_particles.1 = (bf16[64,8192]{1,0:T(8,128)(2,1)S(1)}, bf16[64,8192]{1,0:T(8,128)(2,1)}, bf16[64,8192]{1,0:T(8,128)(2,1)}, bf16[64,8192]{1,0:T(8,128)(2,1)},...) custom-call(bf16[2048,512]{1,0:T(8,128)(2,1)} %bitcast.20, ...), custom_call_target="tpu_custom_call" | custom-call | tf_op jit(solution)/shard_map/sort_particles/pallas_call | solution.py:133
  18.3 1.6 %collective-permute-start.7 = (f32[8,64]{1,0:T(8,128)S(1)}, f32[8,64]{1,0:T(8,128)S(1)}, u32[]{:S(2)}, u32[]{:S(2)}) collective-permute-start(f32[8,64]{1,0:T(8,128)S(1)} %get-tuple-element.15), channel_id=1, source_target_pairs={{0,1},{1,0},{2,3},{3,2},{4,5},{5,4},{6,7},{7,6},{8,9},{9,8},{10,11... | collective-permute-start | bytes 6152 | tf_op jit(solution)/shard_map/ppermute | solution.py:340
  19.9 1.5 %collective-permute-start.8 = (f32[8,64]{1,0:T(8,128)S(1)}, f32[8,64]{1,0:T(8,128)S(1)}, u32[]{:S(2)}, u32[]{:S(2)}) collective-permute-start(f32[8,64]{1,0:T(8,128)S(1)} %get-tuple-element.16), channel_id=1, source_target_pairs={{0,2},{1,3},{2,0},{3,1},{4,6},{5,7},{6,4},{7,5},{8,10},{9,11},{10,... | collective-permute-start | bytes 6152 | tf_op jit(solution)/shard_map/ppermute | solution.py:340
  21.9 1.6 %collective-permute-start = (bf16[64,8192]{1,0:T(8,128)(2,1)}, bf16[64,8192]{1,0:T(8,128)(2,1)}, u32[]{:S(2)}, u32[]{:S(2)}) collective-permute-start(bf16[64,8192]{1,0:T(8,128)(2,1)} %get-tuple-element.11), channel_id=1, source_target_pairs={{0,1},{1,0},{2,3},{3,2},{4,5},{5,4},{6,7},{7,6},{8,9},{9,8},{10,11... | collective-permute-start | bytes 3145736 | tf_op jit(solution)/shard_map/ppermute | solution.py:340
  23.5 1.5 %collective-permute-start.1 = (bf16[64,8192]{1,0:T(8,128)(2,1)}, bf16[64,8192]{1,0:T(8,128)(2,1)}, u32[]{:S(2)}, u32[]{:S(2)}) collective-permute-start(bf16[64,8192]{1,0:T(8,128)(2,1)} %get-tuple-element.12), channel_id=1, source_target_pairs={{0,2},{1,3},{2,0},{3,1},{4,6},{5,7},{6,4},{7,5},{8,10},{9,11},{10,... | collective-permute-start | bytes 3145736 | tf_op jit(solution)/shard_map/ppermute | solution.py:340
  25.0 1.0 %collective-permute-done.9 = f32[8,64]{1,0:T(8,128)S(1)} collective-permute-done((f32[8,64]{1,0:T(8,128)S(1)}, f32[8,64]{1,0:T(8,128)S(1)}, u32[]{:S(2)}, u32[]{:S(2)}) %collective-permute-start.9) | collective-permute-done | bytes 2080 | tf_op jit(solution)/shard_map/ppermute | solution.py:340
  26.6 0.7 collective-permute-start.4
  27.3 5.0 %collective-permute-done.5.refs_8_.refs_13_ = bf16[32,8320]{1,0:T(8,128)(2,1)S(1)} collective-permute-done((bf16[32,8320]{1,0:T(8,128)(2,1)S(1)}, bf16[32,8320]{1,0:T(8,128)(2,1)S(1)}, u32[]{:S(2)}, u32[]{:S(2)}) %collective-permute-start.5) | collective-permute-done | bytes 532512 | tf_op jit(solution)/shard_map/ppermute | solution.py:313
  32.3 1.3 %collective-permute-start.6 = (bf16[32,8320]{1,0:T(8,128)(2,1)S(1)}, bf16[32,8320]{1,0:T(8,128)(2,1)S(1)}, u32[]{:S(2)}, u32[]{:S(2)}) collective-permute-start(bf16[32,8320]{1,0:T(8,128)(2,1)S(1)} %collective-permute-done.5.refs_8_.refs_13_), channel_id=1, source_target_pairs={{4,0},{5,1},{6,2},{7,3},{8,4},{9,5},{10,6},{11,7},{20,16},{21,17},... | collective-permute-start | bytes 1597448 | tf_op jit(solution)/shard_map/ppermute | solution.py:319
  33.6 1.4 %select_convert_fusion = (bf16[256,384]{1,0:T(8,128)(2,1)S(1)}, f32[256,384]{1,0:T(8,128)S(1)}) fusion(f32[384]{0:T(512)S(1)} %multiply_multiply_fusion, f32[256]{0:T(256)S(1)} %bitcast.23, pred[384]{0:T(512)(128)(4,1)S(1)} %iota_compare_fusion), kind=kLoop, calls=%fused_computation.3 | loop fusion | flops 589824 | bytes 592768 | tf_op jit(solution)/shard_map/convert_element_type | solution.py:161
  35.1 1.1 %broadcast_select_fusion = (f32[256,256]{1,0:T(8,128)S(1)}, f32[256,256]{1,0:T(8,128)S(1)}, f32[256,256]{1,0:T(8,128)S(1)}) fusion(f32[256]{0:T(256)S(1)} %fusion.9, pred[256]{0:T(512)(128)(4,1)S(1)} %broadcast_compare_fusion, s32[256]{0:T(256)S(1)} %slice.22, s32[256]{0:T(256)S(1)} %bitcast.22, f32[256,384]{1,0:T(8,128)S(1)} %get-tuple-element.25), kind=kLoop, calls=%fused_computation.22 | loop fusion | flops 1114112 | bytes 1051904 | tf_op jit(solution)/shard_map/jit(_where)/select_n | solution.py:159
  36.3 12.0 %collective-permute-done.refs_1_ = bf16[64,8192]{1,0:T(8,128)(2,1)} collective-permute-done((bf16[64,8192]{1,0:T(8,128)(2,1)}, bf16[64,8192]{1,0:T(8,128)(2,1)}, u32[]{:S(2)}, u32[]{:S(2)}) %collective-permute-start) | collective-permute-done | bytes 1048608 | tf_op jit(solution)/shard_map/ppermute | solution.py:340
  48.3 21.4 %collective-permute-done.1.refs_2_ = bf16[64,8192]{1,0:T(8,128)(2,1)} collective-permute-done((bf16[64,8192]{1,0:T(8,128)(2,1)}, bf16[64,8192]{1,0:T(8,128)(2,1)}, u32[]{:S(2)}, u32[]{:S(2)}) %collective-permute-start.1) | collective-permute-done | bytes 1048608 | tf_op jit(solution)/shard_map/ppermute | solution.py:340
  69.7 10.2 %score_and_spread.1 = bf16[256,896]{1,0:T(8,128)(2,1)S(1)} custom-call(bf16[64,8192]{1,0:T(8,128)(2,1)S(1)} %get-tuple-element.10.refs_0_, bf16[64,8192]{1,0:T(8,128)(2,1)} %collective-permute-done.refs_1_, bf16[64,8192]{1,0:T(8,128)(2,1)} %collective-permute-done.1.refs_2_, bf16[64,8192]{1,0:T(8,128)(2,1)} %collective-permute-done.2.refs_3_, ...), custom_call_target="tpu_custom_call" | custom-call | tf_op jit(solution)/shard_map/score_and_spread/pallas_call | solution.py:257
  79.9 15.2 %all_to_all.9.refs_0_ = bf16[16,16,896]{2,1,0:T(8,128)(2,1)} all-to-all(bf16[16,16,896]{2,1,0:T(8,128)(2,1)S(1)} %bitcast.14), channel_id=1, replica_groups=mesh['half'=2,'owner'=16] {'owner'}, dimensions={0} | all-to-all | bytes 917504 | tf_op jit(solution)/shard_map/all_to_all | solution.py:359
  95.1 1.9 %finish_slab.1 = (f32[16,1024]{1,0:T(8,128)}, f32[16,512]{1,0:T(8,128)}) custom-call(bf16[16,16,896]{2,1,0:T(8,128)(2,1)} %all_to_all.9.refs_0_), custom_call_target="tpu_custom_call" | custom-call | tf_op jit(solution)/shard_map/finish_slab/pallas_call | solution.py:302
  (30 shorter events, 2.7 us)
Async XLA Ops:
  2.4 1.2 %copy-start = (bf16[32,16,1024]{2,1,0:T(8,128)(2,1)S(1)}, bf16[32,16,1024]{2,1,0:T(8,128)(2,1)}, u32[]{:S(2)}) copy-start(bf16[32,16,1024]{2,1,0:T(8,128)(2,1)} %param.14) | copy-start | bytes 3145732
  4.2 22.4 %collective-permute-start.3 = (bf16[32,8320]{1,0:T(8,128)(2,1)S(1)}, bf16[32,8320]{1,0:T(8,128)(2,1)S(1)}, u32[]{:S(2)}, u32[]{:S(2)}) collective-permute-start(bf16[32,8320]{1,0:T(8,128)(2,1)S(1)} %fold_projections.1.refs_4_.refs_9_), channel_id=1, source_target_pairs={{0,4},{1,5},{2,6},{3,7},{4,8},{5,9},{6,10},{7,11},{8,12},{9,13},{1... | collective-permute-start | bytes 1597448 | tf_op jit(solution)/shard_map/ppermute | solution.py:313
  7.3 24.9 %collective-permute-start.5 = (bf16[32,8320]{1,0:T(8,128)(2,1)S(1)}, bf16[32,8320]{1,0:T(8,128)(2,1)S(1)}, u32[]{:S(2)}, u32[]{:S(2)}) collective-permute-start(bf16[32,8320]{1,0:T(8,128)(2,1)S(1)} %fold_projections.1.refs_4_.refs_9_), channel_id=1, source_target_pairs={{0,12},{1,13},{2,14},{3,15},{4,0},{5,1},{6,2},{7,3},{8,4},{9,5},{1... | collective-permute-start | bytes 1597448 | tf_op jit(solution)/shard_map/ppermute | solution.py:313
  9.4 0.7 copy-start.2
  10.0 0.7 copy-start.3
  10.7 0.7 copy-start.4
  11.4 0.7 copy-start.5
  12.0 57.7 %copy-start.1 = (bf16[512,512]{1,0:T(8,128)(2,1)S(1)}, bf16[512,512]{1,0:T(8,128)(2,1)}, u32[]{:S(2)}) copy-start(bf16[512,512]{1,0:T(8,128)(2,1)} %constant.50.refs_14_) | copy-start | bytes 1572868
  18.3 3.6 %collective-permute-start.7 = (f32[8,64]{1,0:T(8,128)S(1)}, f32[8,64]{1,0:T(8,128)S(1)}, u32[]{:S(2)}, u32[]{:S(2)}) collective-permute-start(f32[8,64]{1,0:T(8,128)S(1)} %get-tuple-element.15), channel_id=1, source_target_pairs={{0,1},{1,0},{2,3},{3,2},{4,5},{5,4},{6,7},{7,6},{8,9},{9,8},{10,11... | collective-permute-start | bytes 6152 | tf_op jit(solution)/shard_map/ppermute | solution.py:340
  19.9 3.6 %collective-permute-start.8 = (f32[8,64]{1,0:T(8,128)S(1)}, f32[8,64]{1,0:T(8,128)S(1)}, u32[]{:S(2)}, u32[]{:S(2)}) collective-permute-start(f32[8,64]{1,0:T(8,128)S(1)} %get-tuple-element.16), channel_id=1, source_target_pairs={{0,2},{1,3},{2,0},{3,1},{4,6},{5,7},{6,4},{7,5},{8,10},{9,11},{10,... | collective-permute-start | bytes 6152 | tf_op jit(solution)/shard_map/ppermute | solution.py:340
  21.4 4.6 %collective-permute-start.9 = (f32[8,64]{1,0:T(8,128)S(1)}, f32[8,64]{1,0:T(8,128)S(1)}, u32[]{:S(2)}, u32[]{:S(2)}) collective-permute-start(f32[8,64]{1,0:T(8,128)S(1)} %get-tuple-element.17), channel_id=1, source_target_pairs={{0,3},{1,2},{2,1},{3,0},{4,7},{5,6},{6,5},{7,4},{8,11},{9,10},{10,... | collective-permute-start | bytes 6152 | tf_op jit(solution)/shard_map/ppermute | solution.py:340
  21.9 26.4 %collective-permute-start = (bf16[64,8192]{1,0:T(8,128)(2,1)}, bf16[64,8192]{1,0:T(8,128)(2,1)}, u32[]{:S(2)}, u32[]{:S(2)}) collective-permute-start(bf16[64,8192]{1,0:T(8,128)(2,1)} %get-tuple-element.11), channel_id=1, source_target_pairs={{0,1},{1,0},{2,3},{3,2},{4,5},{5,4},{6,7},{7,6},{8,9},{9,8},{10,11... | collective-permute-start | bytes 3145736 | tf_op jit(solution)/shard_map/ppermute | solution.py:340
  23.5 46.2 %collective-permute-start.1 = (bf16[64,8192]{1,0:T(8,128)(2,1)}, bf16[64,8192]{1,0:T(8,128)(2,1)}, u32[]{:S(2)}, u32[]{:S(2)}) collective-permute-start(bf16[64,8192]{1,0:T(8,128)(2,1)} %get-tuple-element.12), channel_id=1, source_target_pairs={{0,2},{1,3},{2,0},{3,1},{4,6},{5,7},{6,4},{7,5},{8,10},{9,11},{10,... | collective-permute-start | bytes 3145736 | tf_op jit(solution)/shard_map/ppermute | solution.py:340
  26.0 43.6 %collective-permute-start.2 = (bf16[64,8192]{1,0:T(8,128)(2,1)}, bf16[64,8192]{1,0:T(8,128)(2,1)}, u32[]{:S(2)}, u32[]{:S(2)}) collective-permute-start(bf16[64,8192]{1,0:T(8,128)(2,1)} %get-tuple-element.13), channel_id=1, source_target_pairs={{0,3},{1,2},{2,1},{3,0},{4,7},{5,6},{6,5},{7,4},{8,11},{9,10},{10,... | collective-permute-start | bytes 3145736 | tf_op jit(solution)/shard_map/ppermute | solution.py:340
  26.6 43.1 %collective-permute-start.4 = (bf16[32,8320]{1,0:T(8,128)(2,1)S(1)}, bf16[32,8320]{1,0:T(8,128)(2,1)S(1)}, u32[]{:S(2)}, u32[]{:S(2)}) collective-permute-start(bf16[32,8320]{1,0:T(8,128)(2,1)S(1)} %collective-permute-done.3.refs_5_.refs_10_), channel_id=1, source_target_pairs={{4,8},{5,9},{6,10},{7,11},{8,12},{9,13},{10,14},{11,15},{20,24},{2... | collective-permute-start | bytes 1597448 | tf_op jit(solution)/shard_map/ppermute | solution.py:318
  32.3 37.4 %collective-permute-start.6 = (bf16[32,8320]{1,0:T(8,128)(2,1)S(1)}, bf16[32,8320]{1,0:T(8,128)(2,1)S(1)}, u32[]{:S(2)}, u32[]{:S(2)}) collective-permute-start(bf16[32,8320]{1,0:T(8,128)(2,1)S(1)} %collective-permute-done.5.refs_8_.refs_13_), channel_id=1, source_target_pairs={{4,0},{5,1},{6,2},{7,3},{8,4},{9,5},{10,6},{11,7},{20,16},{21,17},... | collective-permute-start | bytes 1597448 | tf_op jit(solution)/shard_map/ppermute | solution.py:319

commit v4 on v3

v4 whole, which is shorter than its diff:
```python
import math

import jax
import jax.numpy as jnp
import numpy as np
from jax import lax
from jax.experimental import pallas as pl
from jax.experimental.pallas import tpu as pltpu
from jax.sharding import PartitionSpec as P

CLASSES = 64
F32 = jnp.float32
BF16 = jnp.bfloat16
HBM = pl.BlockSpec(memory_space=pltpu.MemorySpace.HBM)


def vmem(megabytes):
    return pltpu.CompilerParams(vmem_limit_bytes=megabytes * 1024 * 1024)


def packed_table(length):
    half = length // 2
    product = np.arange(length)[:, None] * np.arange(half + 1)[None, :] % length
    angles = product * (2.0 * math.pi / length)
    cosine, sine = np.cos(angles), -np.sin(angles)
    sine[:, 0] = cosine[:, half]
    table = np.concatenate([cosine[:, :half], sine[:, :half]], axis=1) / math.sqrt(length)
    return jnp.asarray(table, F32).astype(BF16)


def mirror(half):
    row = lax.broadcasted_iota(jnp.int32, (half, half), 0)
    column = lax.broadcasted_iota(jnp.int32, (half, half), 1)
    return jnp.where(row + column == half, 1.0, 0.0).astype(BF16)


def put_tiles(ref, values):
    for t in range(ref.shape[0]):
        ref[t] = values[:, t * 128 : (t + 1) * 128]


def every(ref, start, count, stride):
    picked = [ref[t, pl.ds(start, count, stride=stride), :] for t in range(ref.shape[0])]
    return jnp.concatenate(picked, axis=1)


def flipped(rows):
    down, across = rows.shape
    if across < 128:
        rows = jnp.concatenate([rows, jnp.zeros((down, 128 - across), F32)], axis=1)
    if down < 128:
        rows = jnp.concatenate([rows, jnp.zeros((128 - down, 128), F32)], axis=0)
    return rows.T


def short_sine(x):
    square = x * x
    total = jnp.full(x.shape, -1.0 / 39916800.0, F32)
    for factor in (1.0 / 362880.0, -1.0 / 5040.0, 1.0 / 120.0, -1.0 / 6.0, 1.0):
        total = total * square + factor
    return total * x


def sine_of(x):
    turns = jnp.floor(x * (0.5 / math.pi) + 0.5)
    x = ((x - turns * 6.28125) - turns * 0.0019340515136718750) - turns * 1.2556659145e-06
    x = jnp.where(x > 0.5 * math.pi, math.pi - x, jnp.where(x < -0.5 * math.pi, -math.pi - x, x))
    return short_sine(x)


def fold_kernel(x_ref, interp_ref, class_ref, out_ref, folded):
    pairs, width = out_ref.shape
    half = x_ref.shape[1] // 4
    lines = x_ref.shape[0] // pairs
    flip = mirror(half)
    real_low, real_high = x_ref[:, :half], x_ref[:, half : 2 * half]
    imag_low, imag_high = x_ref[:, 2 * half : 3 * half], x_ref[:, 3 * half :]
    real = real_low.astype(F32) + jnp.dot(real_high, flip, preferred_element_type=F32)
    imag = imag_low.astype(F32) - jnp.dot(imag_high, flip, preferred_element_type=F32)
    lane = lax.broadcasted_iota(jnp.int32, imag.shape, 1)
    imag = jnp.where(lane == 0, real_high.astype(F32)[:, :1], imag)
    put_tiles(folded, jnp.concatenate([real, imag], axis=1))
    for line in range(lines):
        out_ref[:, line * 2 * half : (line + 1) * 2 * half] = every(
            folded, line, pairs, lines
        ).astype(BF16)
    label = jnp.broadcast_to(class_ref[...].astype(F32), (8, pairs))
    info = flipped(jnp.concatenate([interp_ref[...].astype(F32), label], axis=0))
    out_ref[:, lines * 2 * half :] = info[:pairs].astype(BF16)


def fold(projections, interp_weights, pair_class):
    pairs, lines, width = projections.shape
    taps = interp_weights.transpose(1, 2, 0).reshape(-1, pairs)
    return pl.pallas_call(
        fold_kernel,
        out_shape=jax.ShapeDtypeStruct((pairs, lines * width // 2 + 128), BF16),
        scratch_shapes=[pltpu.VMEM((width // 256, pairs * lines, 128), F32)],
        compiler_params=vmem(12),
        name="fold_projections",
    )(projections.reshape(pairs * lines, width), taps, pair_class[None, :])


def sort_kernel(reach, count, capacity, pairs, *refs):
    x_hbm, owner_hbm, pair_hbm, shift_hbm, defocus_hbm = refs[:5]
    *outs, x_ref, owner_ref, pair_ref, shift_ref, defocus_ref, wide, sorted_ref, in_sem, out_sem = refs[5:]
    hbm = (owner_hbm, pair_hbm, shift_hbm, defocus_hbm, x_hbm)
    local = (owner_ref, pair_ref, shift_ref, defocus_ref, x_ref)
    loads = [pltpu.make_async_copy(a, b, in_sem.at[i]) for i, (a, b) in enumerate(zip(hbm, local))]
    for load in loads:
        load.start()
    particles = owner_ref.shape[1]
    length = x_ref.shape[1]
    lines = x_ref.shape[0] // particles
    slots = sorted_ref.shape[0]
    each = slots // len(outs)
    row = lax.broadcasted_iota(jnp.int32, (particles, particles), 0)
    column = lax.broadcasted_iota(jnp.int32, (particles, particles), 1)
    before = jnp.where(row < column, 1.0, 0.0).astype(BF16)
    for load in loads[:4]:
        load.wait()
    me = lax.axis_index("owner")
    owner = owner_ref[...]
    bins = owner & (count - 1)
    if len(outs) > 1:
        bins = bins ^ (me & (count - 1))
    step = ((me >> (count.bit_length() - 1)) - (owner >> (count.bit_length() - 1))) & (reach - 1)
    pair = step * pairs + pair_ref[...]
    padded = -(-count // 8) * 8
    hits = lax.broadcasted_iota(jnp.int32, (padded, particles), 0) == bins
    earlier = jnp.dot(jnp.where(hits, 1.0, 0.0).astype(BF16), before, preferred_element_type=F32)
    earlier = jnp.sum(jnp.where(hits, earlier, 0.0), axis=0, keepdims=True)
    place = bins * capacity + earlier.astype(jnp.int32)
    pick = lax.broadcasted_iota(jnp.int32, (slots, particles), 0) == place
    pick = jnp.where(pick, 1.0, 0.0).astype(BF16)
    kind = lax.broadcasted_iota(jnp.int32, (8, particles), 0)
    facts = jnp.where(kind == 0, defocus_ref[...].astype(F32), jnp.ones((8, particles), F32))
    facts = jnp.where(kind == 1, pair.astype(F32), facts)
    facts = jnp.where(kind == 2, shift_ref[...].astype(F32), facts)
    picked = jnp.dot(pick, flipped(facts).astype(BF16), preferred_element_type=F32)
    sorted_ref[:, lines * length :] = picked.astype(BF16)
    loads[4].wait()
    put_tiles(wide, x_ref[...].astype(F32))
    groups = out_sem.shape[1]
    stores = []
    for line in range(lines):
        rows = every(wide, line, particles, lines).astype(BF16)
        picked = jnp.dot(pick, rows, preferred_element_type=F32)
        sorted_ref[:, line * length : (line + 1) * length] = picked.astype(BF16)
        if (line + 1) % (lines // groups) == 0:
            group = line * groups // lines
            wide_group = lines // groups * length
            end = (group + 1) * wide_group + (128 if line == lines - 1 else 0)
            for j, out in enumerate(outs):
                stores.append(
                    pltpu.make_async_copy(
                        sorted_ref.at[j * each : (j + 1) * each, group * wide_group : end],
                        out.at[:, group * wide_group : end],
                        out_sem.at[j, group],
                    )
                )
                stores[-1].start()
    for store in stores:
        store.wait()


def sort_particles(images, owner, pair, shift, defocus, reach, count, capacity, pairs, pieces):
    particles, lines, length = images.shape
    slots = count * capacity
    each, width, groups = slots // pieces, lines * length + 128, 4
    args = [images.reshape(particles * lines, length)] + [a[None, :] for a in (owner, pair, shift, defocus)]
    return pl.pallas_call(
        lambda *refs: sort_kernel(reach, count, capacity, pairs, *refs),
        in_specs=[HBM] * 5,
        out_specs=[HBM] * pieces,
        out_shape=[jax.ShapeDtypeStruct((each, width), BF16)] * pieces,
        scratch_shapes=[pltpu.VMEM(a.shape, a.dtype) for a in args]
        + [
            pltpu.VMEM((length // 128, particles * lines, 128), F32),
            pltpu.VMEM((slots, width), BF16),
            pltpu.SemaphoreType.DMA((5,)),
            pltpu.SemaphoreType.DMA((pieces, groups)),
        ],
        compiler_params=vmem(20),
        name="sort_particles",
    )(*args)


def joined(refs, sizes, at):
    blocks, start = [], 0
    for size in sizes:
        block = refs[start][:, at]
        for ref in refs[start + 1 : start + size]:
            block = block + ref[:, at]
        blocks.append(block)
        start += size
    return jnp.concatenate(blocks, axis=0)


def score_kernel(scale, n_start, n_images, sizes, slab_lines, *refs):
    n_refs = sum(sizes)
    starts, refs = refs[:n_start], refs[n_start:]
    images, refs = refs[:n_images], refs[n_images:]
    facts_refs, refs = refs[:n_images], refs[n_images:]
    blocks, refs = refs[:n_refs], refs[n_refs:]
    infos, refs = refs[:n_refs], refs[n_refs:]
    table_ref, out_ref, aligned, scores, taps, spread, facts, cosine, cosine_imag, sine, power = refs
    step = pl.program_id(0)
    particles, half = cosine.shape
    pairs, slots = scores.shape
    rows = out_ref.shape[0]
    length = 2 * half
    lines = aligned.shape[0]
    here = images[0].shape[1] // length

    def chosen():
        pair = facts[1:2, :].astype(jnp.int32)
        return lax.broadcasted_iota(jnp.int32, (pairs, slots), 0) == pair

    @pl.when(step == 0)
    def _():
        found = jnp.concatenate([ref[...] for ref in facts_refs], axis=0).astype(F32)
        column = lax.broadcasted_iota(jnp.int32, (particles, half + 128), 1)
        folded = column.astype(F32) * (1.0 / length)
        ctf = -sine_of(found[:, :1] * 1500.0 * (folded * folded) + 0.2)
        shift = found[:, 2:3].astype(jnp.int32)
        turn = (shift * column[:, :half]) & (length - 1)
        turn = jnp.where(turn >= half, turn - length, turn).astype(F32) * (2.0 * math.pi / length)
        size = jnp.abs(turn)
        mirrored = jnp.where(size > 0.5 * math.pi, math.pi - size, size)
        swing = short_sine(jnp.where(turn < 0, -mirrored, mirrored))
        along = ctf[:, :half] * short_sine(0.5 * math.pi - size)
        nyquist = ctf[:, half : half + 1] * (1 - 2 * (shift & 1)).astype(F32)
        cosine[...] = along
        cosine_imag[...] = jnp.where(column[:, :half] == 0, nyquist, along)
        sine[...] = ctf[:, :half] * swing
        square = jnp.where(column <= half, ctf * ctf, 0.0)
        if particles < slots:
            square = jnp.concatenate([square, jnp.zeros((slots - particles, half + 128), F32)], axis=0)
            found = jnp.concatenate([found, jnp.zeros((slots - particles, 128), F32)], axis=0)
        power[...] = square.astype(BF16)
        for t in range(slots // 128):
            facts[:, t * 128 : (t + 1) * 128] = found[t * 128 : (t + 1) * 128].T[:8]
        scores[...] = jnp.zeros(scores.shape, F32)
        onehot = jnp.where(chosen(), 1.0, 0.0).astype(BF16)
        info = joined(infos, sizes, slice(None))
        tap = lax.dot_general(info, onehot, (((0,), (0,)), ((), ())), preferred_element_type=F32)
        put_tiles(taps, tap)
        label = tap[slab_lines * lines : slab_lines * lines + 1, :].astype(jnp.int32)
        group = lax.broadcasted_iota(jnp.int32, (rows, slots), 0) // (rows // CLASSES)
        spread[...] = jnp.where(group == label, 1.0, 0.0)

    total = scores[...]
    for i in range(here):
        at = slice(i * length, (i + 1) * length)
        lines_in = jnp.concatenate([ref[:, at] for ref in images], axis=0)
        spectra = jnp.dot(lines_in, table_ref[...], preferred_element_type=F32)
        spectra = spectra.astype(BF16).astype(F32)
        real, imag = spectra[:, :half], spectra[:, half:]
        turned = jnp.concatenate(
            [cosine[...] * real + sine[...] * imag, cosine_imag[...] * imag - sine[...] * real],
            axis=1,
        )
        if particles < slots:
            empty = jnp.zeros((slots - particles, length), F32)
            turned = jnp.concatenate([turned, empty], axis=0)
        aligned[step * here + i] = turned
        against = joined(blocks, sizes, at)
        total = total + lax.dot_general(
            against, turned.astype(BF16), (((1,), (1,)), ((), ())), preferred_element_type=F32
        )
    scores[...] = total

    @pl.when(step == pl.num_programs(0) - 1)
    def _():
        score = jnp.sum(jnp.where(chosen(), scores[...], 0.0), axis=0, keepdims=True)
        weight = facts[3:4, :] / (1.0 + jnp.exp(score * (-2.0 * scale)))
        upright = jnp.broadcast_to(weight, (128, slots)).T
        upright = jnp.concatenate([upright] * (length // 128), axis=1)
        slab = starts[0][:, :length] if starts else jnp.zeros((rows, length), F32)
        tap_sum = jnp.zeros((slab_lines, slots), F32)
        mask = spread[...].reshape(rows // 8, 8, slots)
        for line in range(lines):
            tap = every(taps, line, slab_lines, lines)
            tap_sum = tap_sum + tap
            tap = jnp.concatenate([tap] * (8 // slab_lines), axis=0)
            mixer = (mask * tap[None]).reshape(rows, slots).astype(BF16)
            contrib = (upright * aligned[line]).astype(BF16)
            slab = slab + jnp.dot(mixer, contrib, preferred_element_type=F32)
        tap = jnp.concatenate([tap_sum * weight] * (8 // slab_lines), axis=0)
        mixer = (mask * tap[None]).reshape(rows, slots).astype(BF16)
        powers = jnp.dot(mixer, power[...], preferred_element_type=F32)
        if starts:
            powers = powers + starts[0][:, length:]
        out_ref[:, :length] = slab.astype(out_ref.dtype)
        out_ref[:, length:] = powers.astype(out_ref.dtype)


def score_and_spread(start, images, references, rows, slab_lines, lines, length, dtype):
    half = length // 2
    particles = sum(a.shape[0] for a in images)
    slots = -(-particles // 128) * 128
    pairs = sum(a[0].shape[0] for a in references)
    sizes = [len(a) for a in references]
    references = [a for blocks in references for a in blocks]
    here = 4
    whole = lambda a: pl.BlockSpec(a.shape, lambda r: (0,) * a.ndim)
    line = lambda a: pl.BlockSpec((a.shape[0], here * length), lambda r: (0, r))
    info = lambda a: pl.BlockSpec((a.shape[0], 128), lambda r: (0, lines * length // 128))
    table = packed_table(length)
    width = length + half + 128
    return pl.pallas_call(
        lambda *refs: score_kernel(
            1.0 / math.sqrt(lines * length), len(start), len(images), sizes, slab_lines, *refs
        ),
        grid=(lines // here,),
        in_specs=[whole(a) for a in start]
        + [line(a) for a in images] + [info(a) for a in images]
        + [line(a) for a in references] + [info(a) for a in references] + [whole(table)],
        out_specs=pl.BlockSpec((rows, width), lambda r: (0, 0)),
        out_shape=jax.ShapeDtypeStruct((rows, width), dtype),
        scratch_shapes=[
            pltpu.VMEM((lines, slots, length), F32),
            pltpu.VMEM((pairs, slots), F32),
            pltpu.VMEM((slots // 128, 128, 128), F32),
            pltpu.VMEM((rows, slots), F32),
            pltpu.VMEM((8, slots), F32),
            pltpu.VMEM((particles, half), F32),
            pltpu.VMEM((particles, half), F32),
            pltpu.VMEM((particles, half), F32),
            pltpu.VMEM((slots, half + 128), BF16),
        ],
        compiler_params=vmem(36),
        name="score_and_spread",
    )(*start, *images, *images, *references, *references, table)


def finish_kernel(scale, x_ref, slab_ref, weights_ref):
    half = weights_ref.shape[1] // 2
    total = jnp.sum(x_ref[...].astype(F32), axis=0)
    flip = mirror(half)

    def mirrored(part):
        out = jnp.zeros(part.shape, F32)
        for _ in range(3):
            piece = part.astype(BF16)
            out = out + jnp.dot(piece, flip, preferred_element_type=F32)
            part = part - piece.astype(F32)
        return out

    real, imag, power = total[:, :half], total[:, half : 2 * half], total[:, 2 * half : 3 * half] * scale
    first = lax.broadcasted_iota(jnp.int32, real.shape, 1) == 0
    slab_ref[:, :half] = real
    slab_ref[:, half : 2 * half] = jnp.where(first, imag[:, :1], mirrored(real))
    slab_ref[:, 2 * half : 3 * half] = jnp.where(first, 0.0, imag)
    slab_ref[:, 3 * half :] = jnp.where(first, 0.0, -mirrored(imag))
    weights_ref[:, :half] = power
    weights_ref[:, half:] = jnp.where(first, total[:, 3 * half : 3 * half + 1] * scale, mirrored(power))


def finish(received, length, scale):
    rows = received.shape[1]
    return pl.pallas_call(
        lambda *refs: finish_kernel(scale, *refs),
        out_shape=(
            jax.ShapeDtypeStruct((rows, 2 * length), F32),
            jax.ShapeDtypeStruct((rows, length), F32),
        ),
        name="finish_slab",
    )(received)


def gather_rows(block, owners, reach, count):
    turn = lambda i: lax.ppermute(block, "owner", [(k, (k + i * count) % owners) for k in range(owners)])
    if reach != 4:
        return [(block,)] + [(turn(i),) for i in range(1, reach)]
    back, ahead = turn(1), turn(3)
    inner = range(count, 3 * count)
    up = lax.ppermute(back, "owner", [(k, k + count) for k in inner])
    down = lax.ppermute(ahead, "owner", [(k, k - count) for k in inner])
    return [(block,), (back,), (up, down), (ahead,)]


def on_device(
    images, defocus, owner_of, pair_of, shift_of, projections, interp_weights, pair_class
):
    particles, lines, length = images.shape
    owners = lax.axis_size("owner")
    capacity = 2 * particles // owners
    pairs, slab_lines, _ = interp_weights.shape
    rows = CLASSES * slab_lines
    reach = max(1, capacity // 4)
    count = owners // reach
    pieces = count if reach > 1 else 1
    moved = sort_particles(
        images, owner_of[:, 0], pair_of, shift_of, defocus, reach, count, reach * capacity, pairs, pieces
    )
    references = gather_rows(fold(projections, interp_weights, pair_class), owners, reach, count)
    sizes = (rows, slab_lines, lines, length)
    if reach > 1:
        swap = lambda a, i: lax.ppermute(a, "owner", [(k, k ^ i) for k in range(owners)]) if i else a
        arrived = [swap(a, i) for i, a in enumerate(moved)]
        partial = score_and_spread([], arrived[:-1], references, *sizes, F32)
        partial = score_and_spread([partial], arrived[-1:], references, *sizes, BF16)
    else:
        arrived = lax.all_to_all(moved[0], "owner", split_axis=0, concat_axis=0, tiled=True)
        partial = score_and_spread([], [arrived], references, *sizes, BF16)
    received = lax.all_to_all(partial, "owner", split_axis=0, concat_axis=0, tiled=True)
    return finish(
        received.reshape(owners, rows // owners, -1), length, CLASSES / (particles * owners)
    )


def solution(mesh):
    return jax.shard_map(
        on_device,
        mesh=mesh,
        in_specs=(
            P(("half", "owner"), None, None),
            P(("half", "owner")),
            P(("half", "owner"), None),
            P(("half", "owner")),
            P(("half", "owner")),
            P(("half", "owner"), None, None),
            P(("half", "owner"), None, None),
            P(("half", "owner")),
        ),
        out_specs=(P(("half", "owner"), None), P(("half", "owner"), None)),
        check_vma=False,
    )
```

time: 97.4 us -> 98.9 us (1.015)
  Pallas kernels: 19 us -> 24.3 us
  other arithmetic: 3.55 us -> 0 us
  starting transfers between devices: 14.1 us -> 10.7 us
  blocking collectives: 15.2 us -> 17.3 us
  waiting for transfers between devices: 39.5 us -> 41.4 us
    ppermute x2, waiting for transfers between devices: 4.97 us -> 20.5 us  [gather_rows(): lax.ppermute(block, 'owner', [(k, (k + i * count) % owners) for k in rang...]
    ppermute x6 -> x3, waiting for transfers between devices: 34.5 us -> 21 us  [on_device(): lax.ppermute(a, 'owner', [(k, k ^ i) for k in range(owners)])]
    pallas_call x1 -> x2, Pallas kernels: 10.2 us -> 17.4 us  [score_and_spread(): pl.pallas_call(lambda *refs: score_kernel(1.0 / math.sqrt(lines * length)...]
    ppermute x6 -> x3, starting transfers between devices: 6.97 us -> 4.86 us  [on_device(): lax.ppermute(a, 'owner', [(k, k ^ i) for k in range(owners)])]
    all_to_all x1, blocking collectives: 15.2 us -> 17.3 us  [on_device(): lax.all_to_all(partial, 'owner', split_axis=0, concat_axis=0, tiled=True)]
    pallas_call x1, Pallas kernels: 6.24 us -> 4.31 us  [sort_particles(): pl.pallas_call(lambda *refs: sort_kernel(reach, count, capacity, pairs, *...]
    convert_element_type x2 -> x0, other arithmetic: 1.43 us -> none  [the longest x1 1.42 us: factors(): jnp.where(keep, ctf * ctf, 0.0).astype(BF16)]
    ppermute x2, starting transfers between devices: 5.16 us -> 3.88 us  [gather_rows(): lax.ppermute(block, 'owner', [(k, (k + i * count) % owners) for k in rang...]
  transfers between devices with their start and end apart: 10 -> 7, of which waited for: 5 -> 3; matrix products, arithmetic and copies ran while one was open for 3% -> 0% of each run, Pallas kernels for 6% -> 10%
where the time goes in v4:
time: 98.9 us; the launch traced here: 98.6 us
  waiting for transfers between devices  41.4 us (42%)
  Pallas kernels  24.3 us (25%)
  blocking collectives  17.3 us (17%)
  starting transfers between devices  10.7 us (11%)
  local copies, waits for them, and re-layouts  4.23 us (4%)
    ppermute x3, waiting for transfers between devices, on_device(): lax.ppermute(a, 'owner', [(k, k ^ i) for k in range(owners)])  21 us
    ppermute x2, waiting for transfers between devices, gather_rows(): lax.ppermute(block, 'owner', [(k, (k + i * count) % owners) for k in rang...  20.5 us
    pallas_call x2, Pallas kernels, score_and_spread(): pl.pallas_call(lambda *refs: score_kernel(1.0 / math.sqrt(lines * length)...  17.4 us
    all_to_all x1, blocking collectives, on_device(): lax.all_to_all(partial, 'owner', split_axis=0, concat_axis=0, tiled=True)  17.3 us
    ppermute x3, starting transfers between devices, on_device(): lax.ppermute(a, 'owner', [(k, k ^ i) for k in range(owners)])  4.86 us
    pallas_call x1, Pallas kernels, sort_particles(): pl.pallas_call(lambda *refs: sort_kernel(reach, count, capacity, pairs, *...  4.31 us
    unnamed x18, local copies, waits for them, and re-layouts  4.23 us
    ppermute x2, starting transfers between devices, gather_rows(): lax.ppermute(block, 'owner', [(k, (k + i * count) % owners) for k in rang...  3.88 us
  transfers between devices with their start and end apart: 7, of which 3 were waited for; matrix products, arithmetic and copies ran while one was open for 0% of the time, Pallas kernels for 10%

profile of v4, /device:TPU:0, one launch (start us, length us, event | category | flops | bytes accessed | tf_op | source)
XLA Modules:
  0.0 98.6 jit_solution(4373993302017345299)
XLA Ops:
  0.7 1.6 %copy-done.1 = bf16[128,16,512]{2,1,0:T(8,128)(2,1)S(1)} copy-done((bf16[128,16,512]{2,1,0:T(8,128)(2,1)S(1)}, bf16[128,16,512]{2,1,0:T(8,128)(2,1)}, u32[]{:S(2)}) %copy-start.1) | copy-done | bytes 2097176
  2.2 0.7 copy-done.4
  2.9 0.7 copy-done.5
  3.6 0.7 copy-done.6
  4.2 0.7 copy-done.7
  4.9 4.3 %sort_particles.1 = (bf16[64,8320]{1,0:T(8,128)(2,1)S(1)}, bf16[64,8320]{1,0:T(8,128)(2,1)S(1)}, bf16[64,8320]{1,0:T(8,128)(2,1)S(1)}, bf16[64,8320]{1,0:T(8,128)(2,1)S(1)}) custom-call(bf16[2048,512]{1,0:T(8,128)(2,1)S(1)} %bitcast.11, s32[1,128]{1,0:T(1,128)S(1)} %bitcast.15, s32[1,128]{1,0:T(1,128)S(1)} %bitcast.16, s32[1,128]{1,0:T(1,128)S(1)} %bitcast.17, ...), custom_call_target="tpu_custom_call" | custom-call | tf_op jit(solution)/shard_map/sort_particles/pallas_call | solution.py:172
  9.2 0.0 copy-start
  9.2 3.0 %collective-permute-start = (bf16[64,8320]{1,0:T(8,128)(2,1)S(1)}, bf16[64,8320]{1,0:T(8,128)(2,1)S(1)}, u32[]{:S(2)}, u32[]{:S(2)}) collective-permute-start(bf16[64,8320]{1,0:T(8,128)(2,1)S(1)} %get-tuple-element.7), channel_id=1, source_target_pairs={{0,1},{1,0},{2,3},{3,2},{4,5},{5,4},{6,7},{7,6},{8,9},{9,8},{10,11... | collective-permute-start | bytes 3194888 | tf_op jit(solution)/shard_map/ppermute | solution.py:401
  12.2 0.6 fold_projections.1.refs_6_.refs_11_.refs_3_.refs_8_
  12.9 1.6 %collective-permute-start.2 = (bf16[32,8320]{1,0:T(8,128)(2,1)S(1)}, bf16[32,8320]{1,0:T(8,128)(2,1)S(1)}, u32[]{:S(2)}, u32[]{:S(2)}) collective-permute-start(bf16[32,8320]{1,0:T(8,128)(2,1)S(1)} %fold_projections.1.refs_6_.refs_11_.refs_3_.refs_8_), channel_id=1, source_target_pairs={{0,4},{1,5},{2,6},{3,7},{4,8},{5,9},{6,10},{7,11},{8,12},{9,13},{1... | collective-permute-start | bytes 1597448 | tf_op jit(solution)/shard_map/ppermute | solution.py:374
  14.5 1.5 %collective-permute-start.1 = (bf16[64,8320]{1,0:T(8,128)(2,1)S(1)}, bf16[64,8320]{1,0:T(8,128)(2,1)S(1)}, u32[]{:S(2)}, u32[]{:S(2)}) collective-permute-start(bf16[64,8320]{1,0:T(8,128)(2,1)S(1)} %get-tuple-element.8), channel_id=1, source_target_pairs={{0,2},{1,3},{2,0},{3,1},{4,6},{5,7},{6,4},{7,5},{8,10},{9,11},{10,... | collective-permute-start | bytes 3194888 | tf_op jit(solution)/shard_map/ppermute | solution.py:401
  16.0 2.2 %collective-permute-start.4 = (bf16[32,8320]{1,0:T(8,128)(2,1)S(1)}, bf16[32,8320]{1,0:T(8,128)(2,1)S(1)}, u32[]{:S(2)}, u32[]{:S(2)}) collective-permute-start(bf16[32,8320]{1,0:T(8,128)(2,1)S(1)} %fold_projections.1.refs_6_.refs_11_.refs_3_.refs_8_), channel_id=1, source_target_pairs={{0,12},{1,13},{2,14},{3,15},{4,0},{5,1},{6,2},{7,3},{8,4},{9,5},{1... | collective-permute-start | bytes 1597448 | tf_op jit(solution)/shard_map/ppermute | solution.py:374
  18.3 0.3 collective-permute-start.6
  18.6 11.2 %collective-permute-done.2.refs_7_.refs_12_.refs_4_.refs_9_ = bf16[32,8320]{1,0:T(8,128)(2,1)S(1)} collective-permute-done((bf16[32,8320]{1,0:T(8,128)(2,1)S(1)}, bf16[32,8320]{1,0:T(8,128)(2,1)S(1)}, u32[]{:S(2)}, u32[]{:S(2)}) %collective-permute-start.2) | collective-permute-done | bytes 532512 | tf_op jit(solution)/shard_map/ppermute | solution.py:374
  29.8 0.7 collective-permute-start.3
  30.5 9.3 %collective-permute-done.4.refs_10_.refs_15_.refs_7_.refs_12_ = bf16[32,8320]{1,0:T(8,128)(2,1)S(1)} collective-permute-done((bf16[32,8320]{1,0:T(8,128)(2,1)S(1)}, bf16[32,8320]{1,0:T(8,128)(2,1)S(1)}, u32[]{:S(2)}, u32[]{:S(2)}) %collective-permute-start.4) | collective-permute-done | bytes 532512 | tf_op jit(solution)/shard_map/ppermute | solution.py:374
  39.7 1.3 %collective-permute-start.5 = (bf16[32,8320]{1,0:T(8,128)(2,1)S(1)}, bf16[32,8320]{1,0:T(8,128)(2,1)S(1)}, u32[]{:S(2)}, u32[]{:S(2)}) collective-permute-start(bf16[32,8320]{1,0:T(8,128)(2,1)S(1)} %collective-permute-done.4.refs_10_.refs_15_.refs_7_.refs_12_), channel_id=1, source_target_pairs={{4,0},{5,1},{6,2},{7,3},{8,4},{9,5},{10,6},{11,7},{20,16},{21,17},... | collective-permute-start | bytes 1597448 | tf_op jit(solution)/shard_map/ppermute | solution.py:380
  41.0 21.0 %collective-permute-done.1.refs_2_.refs_5_ = bf16[64,8320]{1,0:T(8,128)(2,1)S(1)} collective-permute-done((bf16[64,8320]{1,0:T(8,128)(2,1)S(1)}, bf16[64,8320]{1,0:T(8,128)(2,1)S(1)}, u32[]{:S(2)}, u32[]{:S(2)}) %collective-permute-start.1) | collective-permute-done | bytes 1064992 | tf_op jit(solution)/shard_map/ppermute | solution.py:401
  62.0 0.0 collective-permute-done.3.refs_8_.refs_13_.refs_5_.refs_10_
  62.0 9.6 %score_and_spread.2.refs_0_ = f32[256,896]{1,0:T(8,128)S(1)} custom-call(bf16[64,8320]{1,0:T(8,128)(2,1)S(1)} %get-tuple-element.6.refs_0_.refs_3_, bf16[64,8320]{1,0:T(8,128)(2,1)S(1)} %collective-permute-done.refs_1_.refs_4_, bf16[64,8320]{1,0:T(8,128)(2,1)S(1)} %collective-permute-done.1.refs_2_.refs_5_, ...), custom_call_target="tpu_custom_call" | custom-call | tf_op jit(solution)/shard_map/score_and_spread/pallas_call | solution.py:312
  71.6 0.0 collective-permute-done.6.refs_1_.refs_2_
  71.6 7.8 %score_and_spread.3 = bf16[256,896]{1,0:T(8,128)(2,1)S(1)} custom-call(f32[256,896]{1,0:T(8,128)S(1)} %score_and_spread.2.refs_0_, bf16[64,8320]{1,0:T(8,128)(2,1)S(1)} %collective-permute-done.6.refs_1_.refs_2_, bf16[64,8320]{1,0:T(8,128)(2,1)S(1)} %collective-permute-done.6.refs_1_.refs_2_, ...), custom_call_target="tpu_custom_call" | custom-call | tf_op jit(solution)/shard_map/score_and_spread/pallas_call | solution.py:312
  79.4 17.3 %all_to_all.9.refs_0_ = bf16[16,16,896]{2,1,0:T(8,128)(2,1)} all-to-all(bf16[16,16,896]{2,1,0:T(8,128)(2,1)S(1)} %bitcast.12), channel_id=1, replica_groups=mesh['half'=2,'owner'=16] {'owner'}, dimensions={0} | all-to-all | bytes 917504 | tf_op jit(solution)/shard_map/all_to_all | solution.py:408
  96.7 1.9 %finish_slab.1 = (f32[16,1024]{1,0:T(8,128)}, f32[16,512]{1,0:T(8,128)}) custom-call(bf16[16,16,896]{2,1,0:T(8,128)(2,1)} %all_to_all.9.refs_0_), custom_call_target="tpu_custom_call" | custom-call | tf_op jit(solution)/shard_map/finish_slab/pallas_call | solution.py:363
  (14 shorter events, 0.0 us)
Async XLA Ops:
  0.6 11.6 %copy-start.8 = (s32[32]{0:T(128)S(1)}, s32[32]{0:T(128)}, u32[]{:S(2)}) copy-start(s32[32]{0:T(128)} %param.17) | copy-start | bytes 388
  0.6 1.6 %copy-start.1 = (bf16[128,16,512]{2,1,0:T(8,128)(2,1)S(1)}, bf16[128,16,512]{2,1,0:T(8,128)(2,1)}, u32[]{:S(2)}) copy-start(bf16[128,16,512]{2,1,0:T(8,128)(2,1)} %param.10) | copy-start | bytes 6291460
  2.2 0.7 copy-start.4
  2.9 0.7 copy-start.5
  3.6 0.7 copy-start.6
  4.2 0.7 copy-start.7
  4.9 7.3 %copy-start.2 = (bf16[32,16,1024]{2,1,0:T(8,128)(2,1)S(1)}, bf16[32,16,1024]{2,1,0:T(8,128)(2,1)}, u32[]{:S(2)}) copy-start(bf16[32,16,1024]{2,1,0:T(8,128)(2,1)} %param.15) | copy-start | bytes 3145732
  4.9 7.3 %copy-start.3 = (bf16[32,4,16]{0,2,1:T(8,128)(2,1)S(1)}, bf16[32,4,16]{0,2,1:T(8,128)(2,1)}, u32[]{:S(2)}) copy-start(bf16[32,4,16]{0,2,1:T(8,128)(2,1)} %param.16) | copy-start | bytes 12292
  9.2 52.8 %copy-start = (bf16[512,512]{1,0:T(8,128)(2,1)S(1)}, bf16[512,512]{1,0:T(8,128)(2,1)}, u32[]{:S(2)}) copy-start(bf16[512,512]{1,0:T(8,128)(2,1)} %constant.3.refs_16_.refs_13_) | copy-start | bytes 1572868
  9.2 31.8 %collective-permute-start = (bf16[64,8320]{1,0:T(8,128)(2,1)S(1)}, bf16[64,8320]{1,0:T(8,128)(2,1)S(1)}, u32[]{:S(2)}, u32[]{:S(2)}) collective-permute-start(bf16[64,8320]{1,0:T(8,128)(2,1)S(1)} %get-tuple-element.7), channel_id=1, source_target_pairs={{0,1},{1,0},{2,3},{3,2},{4,5},{5,4},{6,7},{7,6},{8,9},{9,8},{10,11... | collective-permute-start | bytes 3194888 | tf_op jit(solution)/shard_map/ppermute | solution.py:401
  12.9 16.9 %collective-permute-start.2 = (bf16[32,8320]{1,0:T(8,128)(2,1)S(1)}, bf16[32,8320]{1,0:T(8,128)(2,1)S(1)}, u32[]{:S(2)}, u32[]{:S(2)}) collective-permute-start(bf16[32,8320]{1,0:T(8,128)(2,1)S(1)} %fold_projections.1.refs_6_.refs_11_.refs_3_.refs_8_), channel_id=1, source_target_pairs={{0,4},{1,5},{2,6},{3,7},{4,8},{5,9},{6,10},{7,11},{8,12},{9,13},{1... | collective-permute-start | bytes 1597448 | tf_op jit(solution)/shard_map/ppermute | solution.py:374
  14.5 47.5 %collective-permute-start.1 = (bf16[64,8320]{1,0:T(8,128)(2,1)S(1)}, bf16[64,8320]{1,0:T(8,128)(2,1)S(1)}, u32[]{:S(2)}, u32[]{:S(2)}) collective-permute-start(bf16[64,8320]{1,0:T(8,128)(2,1)S(1)} %get-tuple-element.8), channel_id=1, source_target_pairs={{0,2},{1,3},{2,0},{3,1},{4,6},{5,7},{6,4},{7,5},{8,10},{9,11},{10,... | collective-permute-start | bytes 3194888 | tf_op jit(solution)/shard_map/ppermute | solution.py:401
  16.0 23.7 %collective-permute-start.4 = (bf16[32,8320]{1,0:T(8,128)(2,1)S(1)}, bf16[32,8320]{1,0:T(8,128)(2,1)S(1)}, u32[]{:S(2)}, u32[]{:S(2)}) collective-permute-start(bf16[32,8320]{1,0:T(8,128)(2,1)S(1)} %fold_projections.1.refs_6_.refs_11_.refs_3_.refs_8_), channel_id=1, source_target_pairs={{0,12},{1,13},{2,14},{3,15},{4,0},{5,1},{6,2},{7,3},{8,4},{9,5},{1... | collective-permute-start | bytes 1597448 | tf_op jit(solution)/shard_map/ppermute | solution.py:374
  18.3 53.3 %collective-permute-start.6 = (bf16[64,8320]{1,0:T(8,128)(2,1)S(1)}, bf16[64,8320]{1,0:T(8,128)(2,1)S(1)}, u32[]{:S(2)}, u32[]{:S(2)}) collective-permute-start(bf16[64,8320]{1,0:T(8,128)(2,1)S(1)} %get-tuple-element.9), channel_id=1, source_target_pairs={{0,3},{1,2},{2,1},{3,0},{4,7},{5,6},{6,5},{7,4},{8,11},{9,10},{10,... | collective-permute-start | bytes 3194888 | tf_op jit(solution)/shard_map/ppermute | solution.py:401
  29.8 32.2 %collective-permute-start.3 = (bf16[32,8320]{1,0:T(8,128)(2,1)S(1)}, bf16[32,8320]{1,0:T(8,128)(2,1)S(1)}, u32[]{:S(2)}, u32[]{:S(2)}) collective-permute-start(bf16[32,8320]{1,0:T(8,128)(2,1)S(1)} %collective-permute-done.2.refs_7_.refs_12_.refs_4_.refs_9_), channel_id=1, source_target_pairs={{4,8},{5,9},{6,10},{7,11},{8,12},{9,13},{10,14},{11,15},{20,24},{2... | collective-permute-start | bytes 1597448 | tf_op jit(solution)/shard_map/ppermute | solution.py:379
  39.7 22.3 %collective-permute-start.5 = (bf16[32,8320]{1,0:T(8,128)(2,1)S(1)}, bf16[32,8320]{1,0:T(8,128)(2,1)S(1)}, u32[]{:S(2)}, u32[]{:S(2)}) collective-permute-start(bf16[32,8320]{1,0:T(8,128)(2,1)S(1)} %collective-permute-done.4.refs_10_.refs_15_.refs_7_.refs_12_), channel_id=1, source_target_pairs={{4,0},{5,1},{6,2},{7,3},{8,4},{9,5},{10,6},{11,7},{20,16},{21,17},... | collective-permute-start | bytes 1597448 | tf_op jit(solution)/shard_map/ppermute | solution.py:380

commit v5 on v4

--- a/solution.py
+++ b/solution.py
@@ -181,158 +181,123 @@
             pltpu.SemaphoreType.DMA((5,)),
             pltpu.SemaphoreType.DMA((pieces, groups)),
         ],
-        compiler_params=vmem(20),
+        compiler_params=vmem(60),
         name="sort_particles",
     )(*args)
 
 
-def joined(refs, sizes, at):
-    blocks, start = [], 0
+def joined(blocks, at):
+    return jnp.concatenate([sum((ref[:, at] for ref in block[1:]), block[0][:, at]) for block in blocks], axis=0)
+
+
+def score_kernel(scale, n_images, sizes, slab_lines, lines, *refs):
+    images, refs = refs[:n_images], refs[n_images:]
+    blocks = []
     for size in sizes:
-        block = refs[start][:, at]
-        for ref in refs[start + 1 : start + size]:
-            block = block + ref[:, at]
-        blocks.append(block)
-        start += size
-    return jnp.concatenate(blocks, axis=0)
-
-
-def score_kernel(scale, n_start, n_images, sizes, slab_lines, *refs):
-    n_refs = sum(sizes)
-    starts, refs = refs[:n_start], refs[n_start:]
-    images, refs = refs[:n_images], refs[n_images:]
-    facts_refs, refs = refs[:n_images], refs[n_images:]
-    blocks, refs = refs[:n_refs], refs[n_refs:]
-    infos, refs = refs[:n_refs], refs[n_refs:]
-    table_ref, out_ref, aligned, scores, taps, spread, facts, cosine, cosine_imag, sine, power = refs
-    step = pl.program_id(0)
-    particles, half = cosine.shape
-    pairs, slots = scores.shape
+        blocks.append(refs[:size])
+        refs = refs[size:]
+    table_ref, out_ref, aligned, taps, cosine, cosine_imag, sine, tap_mask = refs
+    slots, half = cosine.shape
+    length = 2 * half
     rows = out_ref.shape[0]
-    length = 2 * half
-    lines = aligned.shape[0]
-    here = images[0].shape[1] // length
-
-    def chosen():
-        pair = facts[1:2, :].astype(jnp.int32)
-        return lax.broadcasted_iota(jnp.int32, (pairs, slots), 0) == pair
-
-    @pl.when(step == 0)
-    def _():
-        found = jnp.concatenate([ref[...] for ref in facts_refs], axis=0).astype(F32)
-        column = lax.broadcasted_iota(jnp.int32, (particles, half + 128), 1)
-        folded = column.astype(F32) * (1.0 / length)
-        ctf = -sine_of(found[:, :1] * 1500.0 * (folded * folded) + 0.2)
-        shift = found[:, 2:3].astype(jnp.int32)
-        turn = (shift * column[:, :half]) & (length - 1)
-        turn = jnp.where(turn >= half, turn - length, turn).astype(F32) * (2.0 * math.pi / length)
-        size = jnp.abs(turn)
-        mirrored = jnp.where(size > 0.5 * math.pi, math.pi - size, size)
-        swing = short_sine(jnp.where(turn < 0, -mirrored, mirrored))
-        along = ctf[:, :half] * short_sine(0.5 * math.pi - size)
-        nyquist = ctf[:, half : half + 1] * (1 - 2 * (shift & 1)).astype(F32)
-        cosine[...] = along
-        cosine_imag[...] = jnp.where(column[:, :half] == 0, nyquist, along)
-        sine[...] = ctf[:, :half] * swing
-        square = jnp.where(column <= half, ctf * ctf, 0.0)
-        if particles < slots:
-            square = jnp.concatenate([square, jnp.zeros((slots - particles, half + 128), F32)], axis=0)
-            found = jnp.concatenate([found, jnp.zeros((slots - particles, 128), F32)], axis=0)
-        power[...] = square.astype(BF16)
-        for t in range(slots // 128):
-            facts[:, t * 128 : (t + 1) * 128] = found[t * 128 : (t + 1) * 128].T[:8]
-        scores[...] = jnp.zeros(scores.shape, F32)
-        onehot = jnp.where(chosen(), 1.0, 0.0).astype(BF16)
-        info = joined(infos, sizes, slice(None))
-        tap = lax.dot_general(info, onehot, (((0,), (0,)), ((), ())), preferred_element_type=F32)
-        put_tiles(taps, tap)
-        label = tap[slab_lines * lines : slab_lines * lines + 1, :].astype(jnp.int32)
-        group = lax.broadcasted_iota(jnp.int32, (rows, slots), 0) // (rows // CLASSES)
-        spread[...] = jnp.where(group == label, 1.0, 0.0)
-
-    total = scores[...]
-    for i in range(here):
-        at = slice(i * length, (i + 1) * length)
-        lines_in = jnp.concatenate([ref[:, at] for ref in images], axis=0)
+    extra = slice(lines * length, lines * length + 128)
+    info = joined(blocks, extra)
+    pairs = info.shape[0]
+
+    found = jnp.concatenate([ref[:, extra] for ref in images], axis=0).astype(F32)
+    column = lax.broadcasted_iota(jnp.int32, (slots, half + 128), 1)
+    folded = column.astype(F32) * (1.0 / length)
+    ctf = -sine_of(found[:, :1] * 1500.0 * (folded * folded) + 0.2)
+    shift = found[:, 2:3].astype(jnp.int32)
+    turn = (shift * column[:, :half]) & (length - 1)
+    turn = jnp.where(turn >= half, turn - length, turn).astype(F32) * (2.0 * math.pi / length)
+    size = jnp.abs(turn)
+    mirrored = jnp.where(size > 0.5 * math.pi, math.pi - size, size)
+    swing = short_sine(jnp.where(turn < 0, -mirrored, mirrored))
+    along = ctf[:, :half] * short_sine(0.5 * math.pi - size)
+    nyquist = ctf[:, half : half + 1] * (1 - 2 * (shift & 1)).astype(F32)
+    cosine[...] = along
+    cosine_imag[...] = jnp.where(column[:, :half] == 0, nyquist, along)
+    sine[...] = ctf[:, :half] * swing
+    power = jnp.where(column <= half, ctf * ctf, 0.0)
+
+    pair_row = jnp.concatenate(
+        [found[t : t + 128].T[1:2] for t in range(0, slots, 128)], axis=1
+    ).astype(jnp.int32)
+    onehot = lax.broadcasted_iota(jnp.int32, (pairs, slots), 0) == pair_row
+    onehot = jnp.where(onehot, 1.0, 0.0).astype(BF16)
+    tap = lax.dot_general(info, onehot, (((0,), (0,)), ((), ())), preferred_element_type=F32)
+    put_tiles(taps, tap)
+    label = tap[slab_lines * lines : slab_lines * lines + 1, :].astype(jnp.int32)
+    group = lax.broadcasted_iota(jnp.int32, (rows, slots), 0) // (rows // CLASSES)
+    tap_mask[...] = jnp.where(group == label, 1.0, 0.0)
+
+    here = 4
+    scores = jnp.zeros((slots, pairs), F32)
+    for first in range(0, lines, here):
+        at = [slice((first + i) * length, (first + i + 1) * length) for i in range(here)]
+        lines_in = jnp.concatenate([ref[:, cut] for cut in at for ref in images], axis=0)
         spectra = jnp.dot(lines_in, table_ref[...], preferred_element_type=F32)
         spectra = spectra.astype(BF16).astype(F32)
-        real, imag = spectra[:, :half], spectra[:, half:]
-        turned = jnp.concatenate(
-            [cosine[...] * real + sine[...] * imag, cosine_imag[...] * imag - sine[...] * real],
-            axis=1,
+        turns = []
+        for i in range(here):
+            real = spectra[i * slots : (i + 1) * slots, :half]
+            imag = spectra[i * slots : (i + 1) * slots, half:]
+            turned = jnp.concatenate(
+                [cosine[...] * real + sine[...] * imag, cosine_imag[...] * imag - sine[...] * real],
+                axis=1,
+            )
+            aligned[first + i] = turned
+            turns.append(turned.astype(BF16))
+        against = joined(blocks, slice(first * length, (first + here) * length))
+        scores = scores + lax.dot_general(
+            jnp.concatenate(turns, axis=1), against, (((1,), (1,)), ((), ())),
+            preferred_element_type=F32,
         )
-        if particles < slots:
-            empty = jnp.zeros((slots - particles, length), F32)
-            turned = jnp.concatenate([turned, empty], axis=0)
-        aligned[step * here + i] = turned
-        against = joined(blocks, sizes, at)
-        total = total + lax.dot_general(
-            against, turned.astype(BF16), (((1,), (1,)), ((), ())), preferred_element_type=F32
-        )
-    scores[...] = total
-
-    @pl.when(step == pl.num_programs(0) - 1)
-    def _():
-        score = jnp.sum(jnp.where(chosen(), scores[...], 0.0), axis=0, keepdims=True)
-        weight = facts[3:4, :] / (1.0 + jnp.exp(score * (-2.0 * scale)))
-        upright = jnp.broadcast_to(weight, (128, slots)).T
-        upright = jnp.concatenate([upright] * (length // 128), axis=1)
-        slab = starts[0][:, :length] if starts else jnp.zeros((rows, length), F32)
-        tap_sum = jnp.zeros((slab_lines, slots), F32)
-        mask = spread[...].reshape(rows // 8, 8, slots)
-        for line in range(lines):
-            tap = every(taps, line, slab_lines, lines)
-            tap_sum = tap_sum + tap
-            tap = jnp.concatenate([tap] * (8 // slab_lines), axis=0)
-            mixer = (mask * tap[None]).reshape(rows, slots).astype(BF16)
-            contrib = (upright * aligned[line]).astype(BF16)
-            slab = slab + jnp.dot(mixer, contrib, preferred_element_type=F32)
-        tap = jnp.concatenate([tap_sum * weight] * (8 // slab_lines), axis=0)
-        mixer = (mask * tap[None]).reshape(rows, slots).astype(BF16)
-        powers = jnp.dot(mixer, power[...], preferred_element_type=F32)
-        if starts:
-            powers = powers + starts[0][:, length:]
-        out_ref[:, :length] = slab.astype(out_ref.dtype)
-        out_ref[:, length:] = powers.astype(out_ref.dtype)
-
-
-def score_and_spread(start, images, references, rows, slab_lines, lines, length, dtype):
+
+    chosen = lax.broadcasted_iota(jnp.int32, (slots, pairs), 1) == found[:, 1:2].astype(jnp.int32)
+    score = jnp.sum(jnp.where(chosen, scores, 0.0), axis=1, keepdims=True)
+    weight = found[:, 3:4] / (1.0 + jnp.exp(score * (-2.0 * scale)))
+    slab = jnp.zeros((rows, length), F32)
+    tap_sum = jnp.zeros((slab_lines, slots), F32)
+
+    def mixer(tap):
+        tap = jnp.concatenate([tap] * (8 // slab_lines), axis=0)
+        mask = tap_mask[...].reshape(rows // 8, 8, slots)
+        return (mask * tap[None]).reshape(rows, slots).astype(BF16)
+
+    for line in range(lines):
+        tap = every(taps, line, slab_lines, lines)
+        tap_sum = tap_sum + tap
+        contrib = (weight * aligned[line]).astype(BF16)
+        slab = slab + jnp.dot(mixer(tap), contrib, preferred_element_type=F32)
+    out_ref[:, :length] = slab.astype(BF16)
+    powers = jnp.dot(mixer(tap_sum), (weight * power).astype(BF16), preferred_element_type=F32)
+    out_ref[:, length:] = powers.astype(BF16)
+
+
+def score_and_spread(images, references, rows, slab_lines, lines, length):
     half = length // 2
-    particles = sum(a.shape[0] for a in images)
-    slots = -(-particles // 128) * 128
-    pairs = sum(a[0].shape[0] for a in references)
+    slots = sum(a.shape[0] for a in images)
     sizes = [len(a) for a in references]
     references = [a for blocks in references for a in blocks]
-    here = 4
-    whole = lambda a: pl.BlockSpec(a.shape, lambda r: (0,) * a.ndim)
-    line = lambda a: pl.BlockSpec((a.shape[0], here * length), lambda r: (0, r))
-    info = lambda a: pl.BlockSpec((a.shape[0], 128), lambda r: (0, lines * length // 128))
-    table = packed_table(length)
     width = length + half + 128
     return pl.pallas_call(
         lambda *refs: score_kernel(
-            1.0 / math.sqrt(lines * length), len(start), len(images), sizes, slab_lines, *refs
+            1.0 / math.sqrt(lines * length), len(images), sizes, slab_lines, lines, *refs
         ),
-        grid=(lines // here,),
-        in_specs=[whole(a) for a in start]
-        + [line(a) for a in images] + [info(a) for a in images]
-        + [line(a) for a in references] + [info(a) for a in references] + [whole(table)],
-        out_specs=pl.BlockSpec((rows, width), lambda r: (0, 0)),
-        out_shape=jax.ShapeDtypeStruct((rows, width), dtype),
+        out_shape=jax.ShapeDtypeStruct((rows, width), BF16),
         scratch_shapes=[
             pltpu.VMEM((lines, slots, length), F32),
-            pltpu.VMEM((pairs, slots), F32),
             pltpu.VMEM((slots // 128, 128, 128), F32),
+            pltpu.VMEM((slots, half), F32),
+            pltpu.VMEM((slots, half), F32),
+            pltpu.VMEM((slots, half), F32),
             pltpu.VMEM((rows, slots), F32),
-            pltpu.VMEM((8, slots), F32),
-            pltpu.VMEM((particles, half), F32),
-            pltpu.VMEM((particles, half), F32),
-            pltpu.VMEM((particles, half), F32),
-            pltpu.VMEM((slots, half + 128), BF16),
         ],
-        compiler_params=vmem(36),
+        compiler_params=vmem(32),
         name="score_and_spread",
-    )(*start, *images, *images, *references, *references, table)
+    )(*images, *references, packed_table(length))
 
 
 def finish_kernel(scale, x_ref, slab_ref, weights_ref):
@@ -396,15 +361,12 @@
         images, owner_of[:, 0], pair_of, shift_of, defocus, reach, count, reach * capacity, pairs, pieces
     )
     references = gather_rows(fold(projections, interp_weights, pair_class), owners, reach, count)
-    sizes = (rows, slab_lines, lines, length)
     if reach > 1:
         swap = lambda a, i: lax.ppermute(a, "owner", [(k, k ^ i) for k in range(owners)]) if i else a
         arrived = [swap(a, i) for i, a in enumerate(moved)]
-        partial = score_and_spread([], arrived[:-1], references, *sizes, F32)
-        partial = score_and_spread([partial], arrived[-1:], references, *sizes, BF16)
     else:
-        arrived = lax.all_to_all(moved[0], "owner", split_axis=0, concat_axis=0, tiled=True)
-        partial = score_and_spread([], [arrived], references, *sizes, BF16)
+        arrived = [lax.all_to_all(moved[0], "owner", split_axis=0, concat_axis=0, tiled=True)]
+    partial = score_and_spread(arrived, references, rows, slab_lines, lines, length)
     received = lax.all_to_all(partial, "owner", split_axis=0, concat_axis=0, tiled=True)
     return finish(
         received.reshape(owners, rows // owners, -1), length, CLASSES / (particles * owners)

time: 98.9 us -> 85.5 us (0.86)
  Pallas kernels: 24.3 us -> 15.6 us
  local copies, waits for them, and re-layouts: 4.23 us -> 0.02 us
  waiting for transfers between devices: 41.4 us -> 39.6 us
  blocking collectives: 17.3 us -> 18.6 us
    pallas_call x2 -> x1, Pallas kernels: 17.4 us -> 7.46 us  [score_and_spread(): pl.pallas_call(lambda *refs: score_kernel(1.0 / math.sqrt(lines * length)...]
    unnamed x18 -> x10, local copies, waits for them, and re-layouts: 4.23 us -> 0.02 us
    ppermute x3, waiting for transfers between devices: 21 us -> 18.3 us  [on_device(): lax.ppermute(a, 'owner', [(k, k ^ i) for k in range(owners)])]
    all_to_all x1, blocking collectives: 17.3 us -> 18.6 us  [on_device(): lax.all_to_all(partial, 'owner', split_axis=0, concat_axis=0, tiled=True)]
    pallas_call x1, Pallas kernels: 4.31 us -> 5.62 us  [sort_particles(): pl.pallas_call(lambda *refs: sort_kernel(reach, count, capacity, pairs, *...]
  transfers between devices with their start and end apart: 7 -> 7, of which waited for: 3 -> 3; matrix products, arithmetic and copies ran while one was open for 0% -> 0% of each run, Pallas kernels for 10% -> 1%
where the time goes in v5:
time: 85.5 us; the launch traced here: 85.3 us
  waiting for transfers between devices  39.6 us (46%)
  blocking collectives  18.6 us (22%)
  Pallas kernels  15.6 us (18%)
  starting transfers between devices  10.7 us (13%)
    ppermute x2, waiting for transfers between devices, gather_rows(): lax.ppermute(block, 'owner', [(k, (k + i * count) % owners) for k in rang...  21.3 us
    all_to_all x1, blocking collectives, on_device(): lax.all_to_all(partial, 'owner', split_axis=0, concat_axis=0, tiled=True)  18.6 us
    ppermute x3, waiting for transfers between devices, on_device(): lax.ppermute(a, 'owner', [(k, k ^ i) for k in range(owners)])  18.3 us
    pallas_call x1, Pallas kernels, score_and_spread(): pl.pallas_call(lambda *refs: score_kernel(1.0 / math.sqrt(lines * length)...  7.46 us
    pallas_call x1, Pallas kernels, sort_particles(): pl.pallas_call(lambda *refs: sort_kernel(reach, count, capacity, pairs, *...  5.62 us
    ppermute x3, starting transfers between devices, on_device(): lax.ppermute(a, 'owner', [(k, k ^ i) for k in range(owners)])  4.99 us
    ppermute x2, starting transfers between devices, gather_rows(): lax.ppermute(block, 'owner', [(k, (k + i * count) % owners) for k in rang...  3.74 us
    pallas_call x1, Pallas kernels, finish(): pl.pallas_call(lambda *refs: finish_kernel(scale, *refs), out_shape=(jax....  1.92 us
  transfers between devices with their start and end apart: 7, of which 3 were waited for; matrix products, arithmetic and copies ran while one was open for 0% of the time, Pallas kernels for 1%

profile of v5, /device:TPU:0, one launch (start us, length us, event | category | flops | bytes accessed | tf_op | source)
XLA Modules:
  0.0 85.3 jit_solution(16239982013504679408)
XLA Ops:
  0.6 0.0 copy-start.1
  0.6 0.0 copy-start.3
  0.7 0.0 copy-start.4
  0.7 5.6 %sort_particles.1 = (bf16[64,8320]{1,0:T(8,128)(2,1)}, bf16[64,8320]{1,0:T(8,128)(2,1)}, bf16[64,8320]{1,0:T(8,128)(2,1)}, bf16[64,8320]{1,0:T(8,128)(2,1)}) custom-call(bf16[2048,512]{1,0:T(8,128)(2,1)} %bitcast.15, s32[1,128]{1,0:T(1,128)} %bitcast.16, s32[1,128]{1,0:T(1,128)} %bitcast.17, s32[1,128]{1,0:T(1,128)} %bitcast.18, bf16[1,128]{1,0:T(2,128)(2,1)} %bitcast.19), custom_call_target="tpu_custom_call" | custom-call | tf_op jit(solution)/shard_map/sort_particles/pallas_call | solution.py:172
  6.3 0.0 copy-start.2
  6.3 3.0 %collective-permute-start = (bf16[64,8320]{1,0:T(8,128)(2,1)}, bf16[64,8320]{1,0:T(8,128)(2,1)S(1)}, u32[]{:S(2)}, u32[]{:S(2)}) collective-permute-start(bf16[64,8320]{1,0:T(8,128)(2,1)} %get-tuple-element.7), channel_id=1, source_target_pairs={{0,1},{1,0},{2,3},{3,2},{4,5},{5,4},{6,7},{7,6},{8,9},{9,8},{10,11... | collective-permute-start | bytes 3194888 | tf_op jit(solution)/shard_map/ppermute | solution.py:365
  9.3 1.5 %collective-permute-start.1 = (bf16[64,8320]{1,0:T(8,128)(2,1)}, bf16[64,8320]{1,0:T(8,128)(2,1)S(1)}, u32[]{:S(2)}, u32[]{:S(2)}) collective-permute-start(bf16[64,8320]{1,0:T(8,128)(2,1)} %get-tuple-element.8), channel_id=1, source_target_pairs={{0,2},{1,3},{2,0},{3,1},{4,6},{5,7},{6,4},{7,5},{8,10},{9,11},{10,... | collective-permute-start | bytes 3194888 | tf_op jit(solution)/shard_map/ppermute | solution.py:365
  10.8 0.0 copy-done.3
  10.8 0.6 fold_projections.1.refs_4_
  11.5 1.6 %collective-permute-start.3 = (bf16[32,8320]{1,0:T(8,128)(2,1)S(1)}, bf16[32,8320]{1,0:T(8,128)(2,1)S(1)}, u32[]{:S(2)}, u32[]{:S(2)}) collective-permute-start(bf16[32,8320]{1,0:T(8,128)(2,1)S(1)} %fold_projections.1.refs_4_), channel_id=1, source_target_pairs={{0,4},{1,5},{2,6},{3,7},{4,8},{5,9},{6,10},{7,11},{8,12},{9,13},{1... | collective-permute-start | bytes 1597448 | tf_op jit(solution)/shard_map/ppermute | solution.py:339
  13.1 0.5 collective-permute-start.2
  13.6 2.1 %collective-permute-start.5 = (bf16[32,8320]{1,0:T(8,128)(2,1)S(1)}, bf16[32,8320]{1,0:T(8,128)(2,1)S(1)}, u32[]{:S(2)}, u32[]{:S(2)}) collective-permute-start(bf16[32,8320]{1,0:T(8,128)(2,1)S(1)} %fold_projections.1.refs_4_), channel_id=1, source_target_pairs={{0,12},{1,13},{2,14},{3,15},{4,0},{5,1},{6,2},{7,3},{8,4},{9,5},{1... | collective-permute-start | bytes 1597448 | tf_op jit(solution)/shard_map/ppermute | solution.py:339
  15.7 12.7 %collective-permute-done.3.refs_5_ = bf16[32,8320]{1,0:T(8,128)(2,1)S(1)} collective-permute-done((bf16[32,8320]{1,0:T(8,128)(2,1)S(1)}, bf16[32,8320]{1,0:T(8,128)(2,1)S(1)}, u32[]{:S(2)}, u32[]{:S(2)}) %collective-permute-start.3) | collective-permute-done | bytes 532512 | tf_op jit(solution)/shard_map/ppermute | solution.py:339
  28.4 0.7 collective-permute-start.4
  29.1 8.6 %collective-permute-done.5.refs_8_ = bf16[32,8320]{1,0:T(8,128)(2,1)S(1)} collective-permute-done((bf16[32,8320]{1,0:T(8,128)(2,1)S(1)}, bf16[32,8320]{1,0:T(8,128)(2,1)S(1)}, u32[]{:S(2)}, u32[]{:S(2)}) %collective-permute-start.5) | collective-permute-done | bytes 532512 | tf_op jit(solution)/shard_map/ppermute | solution.py:339
  37.7 1.3 %collective-permute-start.6 = (bf16[32,8320]{1,0:T(8,128)(2,1)S(1)}, bf16[32,8320]{1,0:T(8,128)(2,1)S(1)}, u32[]{:S(2)}, u32[]{:S(2)}) collective-permute-start(bf16[32,8320]{1,0:T(8,128)(2,1)S(1)} %collective-permute-done.5.refs_8_), channel_id=1, source_target_pairs={{4,0},{5,1},{6,2},{7,3},{8,4},{9,5},{10,6},{11,7},{20,16},{21,17},... | collective-permute-start | bytes 1597448 | tf_op jit(solution)/shard_map/ppermute | solution.py:345
  39.0 0.0 collective-permute-done.refs_1_
  39.0 18.3 %collective-permute-done.1.refs_2_ = bf16[64,8320]{1,0:T(8,128)(2,1)S(1)} collective-permute-done((bf16[64,8320]{1,0:T(8,128)(2,1)}, bf16[64,8320]{1,0:T(8,128)(2,1)S(1)}, u32[]{:S(2)}, u32[]{:S(2)}) %collective-permute-start.1) | collective-permute-done | bytes 1064992 | tf_op jit(solution)/shard_map/ppermute | solution.py:365
  57.3 0.0 collective-permute-done.2.refs_3_
  57.3 0.0 collective-permute-done.4.refs_6_
  57.3 0.0 collective-permute-done.6.refs_7_
  57.4 7.5 %score_and_spread.1 = bf16[256,896]{1,0:T(8,128)(2,1)S(1)} custom-call(bf16[64,8320]{1,0:T(8,128)(2,1)S(1)} %copy-done, bf16[64,8320]{1,0:T(8,128)(2,1)S(1)} %collective-permute-done.refs_1_, bf16[64,8320]{1,0:T(8,128)(2,1)S(1)} %collective-permute-done.1.refs_2_, bf16[64,8320]{1,0:T(8,128)(2,1)S(1)} %collective-permute-done.2.refs_3_, ...), custom_call_target="tpu_custom_call" | custom-call | tf_op jit(solution)/shard_map/score_and_spread/pallas_call | solution.py:285
  64.8 18.6 %all_to_all.9.refs_0_ = bf16[16,16,896]{2,1,0:T(8,128)(2,1)} all-to-all(bf16[16,16,896]{2,1,0:T(8,128)(2,1)S(1)} %bitcast.11), channel_id=1, replica_groups=mesh['half'=2,'owner'=16] {'owner'}, dimensions={0} | all-to-all | bytes 917504 | tf_op jit(solution)/shard_map/all_to_all | solution.py:370
  83.4 1.9 %finish_slab.1 = (f32[16,1024]{1,0:T(8,128)}, f32[16,512]{1,0:T(8,128)}) custom-call(bf16[16,16,896]{2,1,0:T(8,128)(2,1)} %all_to_all.9.refs_0_), custom_call_target="tpu_custom_call" | custom-call | tf_op jit(solution)/shard_map/finish_slab/pallas_call | solution.py:328
  (5 shorter events, 0.0 us)
Async XLA Ops:
  0.6 10.2 %copy-start.1 = (bf16[32,16,1024]{2,1,0:T(8,128)(2,1)S(1)}, bf16[32,16,1024]{2,1,0:T(8,128)(2,1)}, u32[]{:S(2)}) copy-start(bf16[32,16,1024]{2,1,0:T(8,128)(2,1)} %param.14) | copy-start | bytes 3145732
  0.6 10.2 %copy-start.3 = (bf16[32,4,16]{0,2,1:T(8,128)(2,1)S(1)}, bf16[32,4,16]{0,2,1:T(8,128)(2,1)}, u32[]{:S(2)}) copy-start(bf16[32,4,16]{0,2,1:T(8,128)(2,1)} %param.15) | copy-start | bytes 12292
  0.7 10.2 %copy-start.4 = (s32[32]{0:T(128)S(1)}, s32[32]{0:T(128)}, u32[]{:S(2)}) copy-start(s32[32]{0:T(128)} %param.16) | copy-start | bytes 388
  6.3 51.0 %copy-start = (bf16[64,8320]{1,0:T(8,128)(2,1)S(1)}, bf16[64,8320]{1,0:T(8,128)(2,1)}, u32[]{:S(2)}) copy-start(bf16[64,8320]{1,0:T(8,128)(2,1)} %get-tuple-element.6.refs_0_) | copy-start | bytes 3194884
  6.3 51.0 %copy-start.2 = (bf16[512,512]{1,0:T(8,128)(2,1)S(1)}, bf16[512,512]{1,0:T(8,128)(2,1)}, u32[]{:S(2)}) copy-start(bf16[512,512]{1,0:T(8,128)(2,1)} %constant.3.refs_9_) | copy-start | bytes 1572868
  6.3 32.7 %collective-permute-start = (bf16[64,8320]{1,0:T(8,128)(2,1)}, bf16[64,8320]{1,0:T(8,128)(2,1)S(1)}, u32[]{:S(2)}, u32[]{:S(2)}) collective-permute-start(bf16[64,8320]{1,0:T(8,128)(2,1)} %get-tuple-element.7), channel_id=1, source_target_pairs={{0,1},{1,0},{2,3},{3,2},{4,5},{5,4},{6,7},{7,6},{8,9},{9,8},{10,11... | collective-permute-start | bytes 3194888 | tf_op jit(solution)/shard_map/ppermute | solution.py:365
  9.3 48.0 %collective-permute-start.1 = (bf16[64,8320]{1,0:T(8,128)(2,1)}, bf16[64,8320]{1,0:T(8,128)(2,1)S(1)}, u32[]{:S(2)}, u32[]{:S(2)}) collective-permute-start(bf16[64,8320]{1,0:T(8,128)(2,1)} %get-tuple-element.8), channel_id=1, source_target_pairs={{0,2},{1,3},{2,0},{3,1},{4,6},{5,7},{6,4},{7,5},{8,10},{9,11},{10,... | collective-permute-start | bytes 3194888 | tf_op jit(solution)/shard_map/ppermute | solution.py:365
  11.5 16.9 %collective-permute-start.3 = (bf16[32,8320]{1,0:T(8,128)(2,1)S(1)}, bf16[32,8320]{1,0:T(8,128)(2,1)S(1)}, u32[]{:S(2)}, u32[]{:S(2)}) collective-permute-start(bf16[32,8320]{1,0:T(8,128)(2,1)S(1)} %fold_projections.1.refs_4_), channel_id=1, source_target_pairs={{0,4},{1,5},{2,6},{3,7},{4,8},{5,9},{6,10},{7,11},{8,12},{9,13},{1... | collective-permute-start | bytes 1597448 | tf_op jit(solution)/shard_map/ppermute | solution.py:339
  13.1 44.2 %collective-permute-start.2 = (bf16[64,8320]{1,0:T(8,128)(2,1)}, bf16[64,8320]{1,0:T(8,128)(2,1)S(1)}, u32[]{:S(2)}, u32[]{:S(2)}) collective-permute-start(bf16[64,8320]{1,0:T(8,128)(2,1)} %get-tuple-element.9), channel_id=1, source_target_pairs={{0,3},{1,2},{2,1},{3,0},{4,7},{5,6},{6,5},{7,4},{8,11},{9,10},{10,... | collective-permute-start | bytes 3194888 | tf_op jit(solution)/shard_map/ppermute | solution.py:365
  13.6 24.1 %collective-permute-start.5 = (bf16[32,8320]{1,0:T(8,128)(2,1)S(1)}, bf16[32,8320]{1,0:T(8,128)(2,1)S(1)}, u32[]{:S(2)}, u32[]{:S(2)}) collective-permute-start(bf16[32,8320]{1,0:T(8,128)(2,1)S(1)} %fold_projections.1.refs_4_), channel_id=1, source_target_pairs={{0,12},{1,13},{2,14},{3,15},{4,0},{5,1},{6,2},{7,3},{8,4},{9,5},{1... | collective-permute-start | bytes 1597448 | tf_op jit(solution)/shard_map/ppermute | solution.py:339
  28.4 28.9 %collective-permute-start.4 = (bf16[32,8320]{1,0:T(8,128)(2,1)S(1)}, bf16[32,8320]{1,0:T(8,128)(2,1)S(1)}, u32[]{:S(2)}, u32[]{:S(2)}) collective-permute-start(bf16[32,8320]{1,0:T(8,128)(2,1)S(1)} %collective-permute-done.3.refs_5_), channel_id=1, source_target_pairs={{4,8},{5,9},{6,10},{7,11},{8,12},{9,13},{10,14},{11,15},{20,24},{2... | collective-permute-start | bytes 1597448 | tf_op jit(solution)/shard_map/ppermute | solution.py:344
  37.7 19.6 %collective-permute-start.6 = (bf16[32,8320]{1,0:T(8,128)(2,1)S(1)}, bf16[32,8320]{1,0:T(8,128)(2,1)S(1)}, u32[]{:S(2)}, u32[]{:S(2)}) collective-permute-start(bf16[32,8320]{1,0:T(8,128)(2,1)S(1)} %collective-permute-done.5.refs_8_), channel_id=1, source_target_pairs={{4,0},{5,1},{6,2},{7,3},{8,4},{9,5},{10,6},{11,7},{20,16},{21,17},... | collective-permute-start | bytes 1597448 | tf_op jit(solution)/shard_map/ppermute | solution.py:345

commit v6 on v5

--- a/solution.py
+++ b/solution.py
@@ -9,6 +9,7 @@
 from jax.sharding import PartitionSpec as P
 
 CLASSES = 64
+LEVELS = 256
 F32 = jnp.float32
 BF16 = jnp.bfloat16
 HBM = pl.BlockSpec(memory_space=pltpu.MemorySpace.HBM)
@@ -102,15 +103,26 @@
 
 
 def sort_kernel(reach, count, capacity, pairs, *refs):
-    x_hbm, owner_hbm, pair_hbm, shift_hbm, defocus_hbm = refs[:5]
-    *outs, x_ref, owner_ref, pair_ref, shift_ref, defocus_ref, wide, sorted_ref, in_sem, out_sem = refs[5:]
-    hbm = (owner_hbm, pair_hbm, shift_hbm, defocus_hbm, x_hbm)
-    local = (owner_ref, pair_ref, shift_ref, defocus_ref, x_ref)
-    loads = [pltpu.make_async_copy(a, b, in_sem.at[i]) for i, (a, b) in enumerate(zip(hbm, local))]
-    for load in loads:
-        load.start()
+    sources, refs = refs[:6], refs[6:]
+    *outs, x_ref, owner_ref, pair_ref, shift_ref, defocus_ref, table_ref, wide, sorted_ref, in_sem, x_sem, out_sem = refs
+    loads = [
+        pltpu.make_async_copy(a, b, in_sem.at[i])
+        for i, (a, b) in enumerate(
+            zip(sources[1:], (owner_ref, pair_ref, shift_ref, defocus_ref, table_ref))
+        )
+    ]
+    parts = x_sem.shape[0]
+    share = x_ref.shape[0] // parts
+    cuts = [slice(i * share, (i + 1) * share) for i in range(parts)]
+    chunks = [
+        pltpu.make_async_copy(sources[0].at[cut], x_ref.at[cut], x_sem.at[i])
+        for i, cut in enumerate(cuts)
+    ]
+    for copy in loads + chunks:
+        copy.start()
     particles = owner_ref.shape[1]
     length = x_ref.shape[1]
+    half = length // 2
     lines = x_ref.shape[0] // particles
     slots = sorted_ref.shape[0]
     each = slots // len(outs)
@@ -133,19 +145,46 @@
     place = bins * capacity + earlier.astype(jnp.int32)
     pick = lax.broadcasted_iota(jnp.int32, (slots, particles), 0) == place
     pick = jnp.where(pick, 1.0, 0.0).astype(BF16)
+    defocus = defocus_ref[...].astype(F32)
+    level = jnp.where(defocus < 2.0, (defocus - 1.0) * 128.0, 128.0 + (defocus - 2.0) * 64.0)
     kind = lax.broadcasted_iota(jnp.int32, (8, particles), 0)
-    facts = jnp.where(kind == 0, defocus_ref[...].astype(F32), jnp.ones((8, particles), F32))
+    facts = jnp.where(kind == 0, jnp.floor(level + 0.5), jnp.ones((8, particles), F32))
     facts = jnp.where(kind == 1, pair.astype(F32), facts)
     facts = jnp.where(kind == 2, shift_ref[...].astype(F32), facts)
-    picked = jnp.dot(pick, flipped(facts).astype(BF16), preferred_element_type=F32)
+    facts = flipped(jnp.where(kind == 4, defocus, facts))
+    picked = jnp.dot(pick, facts.astype(BF16), preferred_element_type=F32)
     sorted_ref[:, lines * length :] = picked.astype(BF16)
+
+    column = lax.broadcasted_iota(jnp.int32, (particles, half + 128), 1)
+    folded = column.astype(F32) * (1.0 / length)
+    ctf = -sine_of(facts[:, 4:5] * 1500.0 * (folded * folded) + 0.2)
+    shift = facts[:, 2:3].astype(jnp.int32)
+    turn = (shift * column[:, :half]) & (length - 1)
+    turn = jnp.where(turn >= half, turn - length, turn).astype(F32) * (2.0 * math.pi / length)
+    size = jnp.abs(turn)
+    mirrored = jnp.where(size > 0.5 * math.pi, math.pi - size, size)
+    swing = short_sine(jnp.where(turn < 0, -mirrored, mirrored))
+    cosine = ctf[:, :half] * short_sine(0.5 * math.pi - size)
+    nyquist = ctf[:, half : half + 1] * (1 - 2 * (shift & 1)).astype(F32)
+    cosine_imag = jnp.where(column[:, :half] == 0, nyquist, cosine)
+    sine = ctf[:, :half] * swing
+
     loads[4].wait()
-    put_tiles(wide, x_ref[...].astype(F32))
+    for chunk, cut in zip(chunks, cuts):
+        chunk.wait()
+        spectra = jnp.dot(x_ref[cut], table_ref[...], preferred_element_type=F32)
+        spectra = spectra.astype(BF16).astype(F32)
+        for t in range(length // 128):
+            wide[t, cut] = spectra[:, t * 128 : (t + 1) * 128]
     groups = out_sem.shape[1]
     stores = []
     for line in range(lines):
-        rows = every(wide, line, particles, lines).astype(BF16)
-        picked = jnp.dot(pick, rows, preferred_element_type=F32)
+        spectra = every(wide, line, particles, lines)
+        real, imag = spectra[:, :half], spectra[:, half:]
+        turned = jnp.concatenate(
+            [cosine * real + sine * imag, cosine_imag * imag - sine * real], axis=1
+        )
+        picked = jnp.dot(pick, turned.astype(BF16), preferred_element_type=F32)
         sorted_ref[:, line * length : (line + 1) * length] = picked.astype(BF16)
         if (line + 1) % (lines // groups) == 0:
             group = line * groups // lines
@@ -169,9 +208,10 @@
     slots = count * capacity
     each, width, groups = slots // pieces, lines * length + 128, 4
     args = [images.reshape(particles * lines, length)] + [a[None, :] for a in (owner, pair, shift, defocus)]
+    args.append(packed_table(length))
     return pl.pallas_call(
         lambda *refs: sort_kernel(reach, count, capacity, pairs, *refs),
-        in_specs=[HBM] * 5,
+        in_specs=[HBM] * 6,
         out_specs=[HBM] * pieces,
         out_shape=[jax.ShapeDtypeStruct((each, width), BF16)] * pieces,
         scratch_shapes=[pltpu.VMEM(a.shape, a.dtype) for a in args]
@@ -179,6 +219,7 @@
             pltpu.VMEM((length // 128, particles * lines, 128), F32),
             pltpu.VMEM((slots, width), BF16),
             pltpu.SemaphoreType.DMA((5,)),
+            pltpu.SemaphoreType.DMA((4,)),
             pltpu.SemaphoreType.DMA((pieces, groups)),
         ],
         compiler_params=vmem(60),
@@ -190,36 +231,29 @@
     return jnp.concatenate([sum((ref[:, at] for ref in block[1:]), block[0][:, at]) for block in blocks], axis=0)
 
 
-def score_kernel(scale, n_images, sizes, slab_lines, lines, *refs):
+def score_kernel(scale, n_images, sizes, slab_lines, lines, length, *refs):
     images, refs = refs[:n_images], refs[n_images:]
     blocks = []
     for size in sizes:
         blocks.append(refs[:size])
         refs = refs[size:]
-    table_ref, out_ref, aligned, taps, cosine, cosine_imag, sine, tap_mask = refs
-    slots, half = cosine.shape
-    length = 2 * half
-    rows = out_ref.shape[0]
-    extra = slice(lines * length, lines * length + 128)
-    info = joined(blocks, extra)
-    pairs = info.shape[0]
-
-    found = jnp.concatenate([ref[:, extra] for ref in images], axis=0).astype(F32)
-    column = lax.broadcasted_iota(jnp.int32, (slots, half + 128), 1)
-    folded = column.astype(F32) * (1.0 / length)
-    ctf = -sine_of(found[:, :1] * 1500.0 * (folded * folded) + 0.2)
-    shift = found[:, 2:3].astype(jnp.int32)
-    turn = (shift * column[:, :half]) & (length - 1)
-    turn = jnp.where(turn >= half, turn - length, turn).astype(F32) * (2.0 * math.pi / length)
-    size = jnp.abs(turn)
-    mirrored = jnp.where(size > 0.5 * math.pi, math.pi - size, size)
-    swing = short_sine(jnp.where(turn < 0, -mirrored, mirrored))
-    along = ctf[:, :half] * short_sine(0.5 * math.pi - size)
-    nyquist = ctf[:, half : half + 1] * (1 - 2 * (shift & 1)).astype(F32)
-    cosine[...] = along
-    cosine_imag[...] = jnp.where(column[:, :half] == 0, nyquist, along)
-    sine[...] = ctf[:, :half] * swing
-    power = jnp.where(column <= half, ctf * ctf, 0.0)
+    out_ref, taps = refs
+    info = joined(blocks, slice(lines * length, lines * length + 128))
+    pairs, rows = info.shape[0], out_ref.shape[0]
+    found = jnp.concatenate([ref[:, lines * length :] for ref in images], axis=0).astype(F32)
+    slots = found.shape[0]
+    here = 4
+
+    def stacked(line):
+        return jnp.concatenate(
+            [ref[:, line * length : (line + 1) * length] for ref in images], axis=0
+        )
+
+    scores = jnp.zeros((slots, pairs), F32)
+    for line in range(lines):
+        block = joined(blocks, slice(line * length, (line + 1) * length))
+        across = block.astype(F32).T.astype(BF16)
+        scores = scores + jnp.dot(stacked(line), across, preferred_element_type=F32)
 
     pair_row = jnp.concatenate(
         [found[t : t + 128].T[1:2] for t in range(0, slots, 128)], axis=1
@@ -230,78 +264,62 @@
     put_tiles(taps, tap)
     label = tap[slab_lines * lines : slab_lines * lines + 1, :].astype(jnp.int32)
     group = lax.broadcasted_iota(jnp.int32, (rows, slots), 0) // (rows // CLASSES)
-    tap_mask[...] = jnp.where(group == label, 1.0, 0.0)
-
-    here = 4
-    scores = jnp.zeros((slots, pairs), F32)
-    for first in range(0, lines, here):
-        at = [slice((first + i) * length, (first + i + 1) * length) for i in range(here)]
-        lines_in = jnp.concatenate([ref[:, cut] for cut in at for ref in images], axis=0)
-        spectra = jnp.dot(lines_in, table_ref[...], preferred_element_type=F32)
-        spectra = spectra.astype(BF16).astype(F32)
-        turns = []
-        for i in range(here):
-            real = spectra[i * slots : (i + 1) * slots, :half]
-            imag = spectra[i * slots : (i + 1) * slots, half:]
-            turned = jnp.concatenate(
-                [cosine[...] * real + sine[...] * imag, cosine_imag[...] * imag - sine[...] * real],
-                axis=1,
-            )
-            aligned[first + i] = turned
-            turns.append(turned.astype(BF16))
-        against = joined(blocks, slice(first * length, (first + here) * length))
-        scores = scores + lax.dot_general(
-            jnp.concatenate(turns, axis=1), against, (((1,), (1,)), ((), ())),
-            preferred_element_type=F32,
-        )
+    mask = jnp.where(group == label, 1.0, 0.0).astype(BF16).reshape(rows // 16, 16, slots)
+
+    def mixer(tap):
+        tap = jnp.concatenate([tap] * (16 // slab_lines), axis=0).astype(BF16)
+        return (mask * tap[None]).reshape(rows, slots)
 
     chosen = lax.broadcasted_iota(jnp.int32, (slots, pairs), 1) == found[:, 1:2].astype(jnp.int32)
     score = jnp.sum(jnp.where(chosen, scores, 0.0), axis=1, keepdims=True)
     weight = found[:, 3:4] / (1.0 + jnp.exp(score * (-2.0 * scale)))
     slab = jnp.zeros((rows, length), F32)
     tap_sum = jnp.zeros((slab_lines, slots), F32)
-
-    def mixer(tap):
-        tap = jnp.concatenate([tap] * (8 // slab_lines), axis=0)
-        mask = tap_mask[...].reshape(rows // 8, 8, slots)
-        return (mask * tap[None]).reshape(rows, slots).astype(BF16)
-
-    for line in range(lines):
-        tap = every(taps, line, slab_lines, lines)
-        tap_sum = tap_sum + tap
-        contrib = (weight * aligned[line]).astype(BF16)
-        slab = slab + jnp.dot(mixer(tap), contrib, preferred_element_type=F32)
+    for first in range(0, lines, here):
+        mixers, contribs = [], []
+        for line in range(first, first + here):
+            tap = every(taps, line, slab_lines, lines)
+            tap_sum = tap_sum + tap
+            mixers.append(mixer(tap))
+            contribs.append((weight * stacked(line).astype(F32)).astype(BF16))
+        slab = slab + jnp.dot(
+            jnp.concatenate(mixers, axis=1), jnp.concatenate(contribs, axis=0),
+            preferred_element_type=F32,
+        )
     out_ref[:, :length] = slab.astype(BF16)
-    powers = jnp.dot(mixer(tap_sum), (weight * power).astype(BF16), preferred_element_type=F32)
-    out_ref[:, length:] = powers.astype(BF16)
+    levels = lax.broadcasted_iota(jnp.int32, (slots, LEVELS), 1) == found[:, :1].astype(jnp.int32)
+    levels = jnp.where(levels, weight, 0.0).astype(BF16)
+    levels = jnp.dot(mixer(tap_sum), levels, preferred_element_type=F32)
+    out_ref[:, length:] = levels.astype(BF16)
 
 
 def score_and_spread(images, references, rows, slab_lines, lines, length):
-    half = length // 2
     slots = sum(a.shape[0] for a in images)
     sizes = [len(a) for a in references]
     references = [a for blocks in references for a in blocks]
-    width = length + half + 128
     return pl.pallas_call(
         lambda *refs: score_kernel(
-            1.0 / math.sqrt(lines * length), len(images), sizes, slab_lines, lines, *refs
+            1.0 / math.sqrt(lines * length), len(images), sizes, slab_lines, lines, length, *refs
         ),
-        out_shape=jax.ShapeDtypeStruct((rows, width), BF16),
-        scratch_shapes=[
-            pltpu.VMEM((lines, slots, length), F32),
-            pltpu.VMEM((slots // 128, 128, 128), F32),
-            pltpu.VMEM((slots, half), F32),
-            pltpu.VMEM((slots, half), F32),
-            pltpu.VMEM((slots, half), F32),
-            pltpu.VMEM((rows, slots), F32),
-        ],
-        compiler_params=vmem(32),
+        out_shape=jax.ShapeDtypeStruct((rows, length + LEVELS), BF16),
+        scratch_shapes=[pltpu.VMEM((slots // 128, 128, 128), F32)],
+        compiler_params=vmem(24),
         name="score_and_spread",
-    )(*images, *references, packed_table(length))
-
-
-def finish_kernel(scale, x_ref, slab_ref, weights_ref):
-    half = weights_ref.shape[1] // 2
+    )(*images, *references)
+
+
+def level_powers(length, scale):
+    level = np.arange(LEVELS)
+    defocus = np.where(level < 128, 1.0 + level / 128.0, 2.0 + (level - 128) / 64.0).astype(np.float32)
+    column = np.arange(length)
+    folded = np.minimum(column, length - column).astype(np.float32) / np.float32(length)
+    phase = (defocus * np.float32(1500.0))[:, None] * (folded * folded)[None, :] + np.float32(0.2)
+    powers = np.sin(phase.astype(np.float64)) ** 2 * scale
+    return jnp.asarray(np.where(level[:, None] <= 192, powers, 0.0), F32)
+
+
+def finish_kernel(x_ref, powers_ref, slab_ref, weights_ref):
+    half = slab_ref.shape[1] // 4
     total = jnp.sum(x_ref[...].astype(F32), axis=0)
     flip = mirror(half)
 
@@ -313,26 +331,28 @@
             part = part - piece.astype(F32)
         return out
 
-    real, imag, power = total[:, :half], total[:, half : 2 * half], total[:, 2 * half : 3 * half] * scale
+    real, imag = total[:, :half], total[:, half : 2 * half]
     first = lax.broadcasted_iota(jnp.int32, real.shape, 1) == 0
     slab_ref[:, :half] = real
     slab_ref[:, half : 2 * half] = jnp.where(first, imag[:, :1], mirrored(real))
     slab_ref[:, 2 * half : 3 * half] = jnp.where(first, 0.0, imag)
     slab_ref[:, 3 * half :] = jnp.where(first, 0.0, -mirrored(imag))
-    weights_ref[:, :half] = power
-    weights_ref[:, half:] = jnp.where(first, total[:, 3 * half : 3 * half + 1] * scale, mirrored(power))
+    weights_ref[...] = jnp.dot(
+        total[:, 2 * half :], powers_ref[...], precision=lax.Precision.HIGHEST,
+        preferred_element_type=F32,
+    )
 
 
 def finish(received, length, scale):
     rows = received.shape[1]
     return pl.pallas_call(
-        lambda *refs: finish_kernel(scale, *refs),
+        finish_kernel,
         out_shape=(
             jax.ShapeDtypeStruct((rows, 2 * length), F32),
             jax.ShapeDtypeStruct((rows, length), F32),
         ),
         name="finish_slab",
-    )(received)
+    )(received, level_powers(length, scale))
 
 
 def gather_rows(block, owners, reach, count):

time: 85.5 us -> 81.7 us (0.956)
  Pallas kernels: 15.6 us -> 13.1 us
  blocking collectives: 18.6 us -> 17.3 us
    pallas_call x1, Pallas kernels: 7.46 us -> 2.9 us  [score_and_spread(): pl.pallas_call(lambda *refs: score_kernel(1.0 / math.sqrt(lines * length)...]
    pallas_call x1, Pallas kernels: 5.62 us -> 7.35 us  [sort_particles(): pl.pallas_call(lambda *refs: sort_kernel(reach, count, capacity, pairs, *...]
    all_to_all x1, blocking collectives: 18.6 us -> 17.3 us  [on_device(): lax.all_to_all(partial, 'owner', split_axis=0, concat_axis=0, tiled=True)]
where the time goes in v6:
time: 81.7 us; the launch traced here: 81.5 us
  waiting for transfers between devices  39.6 us (48%)
  blocking collectives  17.3 us (21%)
  Pallas kernels  13.1 us (16%)
  starting transfers between devices  10.7 us (13%)
    ppermute x2, waiting for transfers between devices, gather_rows(): lax.ppermute(block, 'owner', [(k, (k + i * count) % owners) for k in rang...  21.3 us
    ppermute x3, waiting for transfers between devices, on_device(): lax.ppermute(a, 'owner', [(k, k ^ i) for k in range(owners)])  18.3 us
    all_to_all x1, blocking collectives, on_device(): lax.all_to_all(partial, 'owner', split_axis=0, concat_axis=0, tiled=True)  17.3 us
    pallas_call x1, Pallas kernels, sort_particles(): pl.pallas_call(lambda *refs: sort_kernel(reach, count, capacity, pairs, *...  7.35 us
    ppermute x3, starting transfers between devices, on_device(): lax.ppermute(a, 'owner', [(k, k ^ i) for k in range(owners)])  5.01 us
    ppermute x2, starting transfers between devices, gather_rows(): lax.ppermute(block, 'owner', [(k, (k + i * count) % owners) for k in rang...  3.73 us
    pallas_call x1, Pallas kernels, score_and_spread(): pl.pallas_call(lambda *refs: score_kernel(1.0 / math.sqrt(lines * length)...  2.9 us
    pallas_call x1, Pallas kernels, finish(): pl.pallas_call(finish_kernel, out_shape=(jax.ShapeDtypeStruct((rows, 2 *...  2.23 us
  transfers between devices with their start and end apart: 7, of which 3 were waited for; matrix products, arithmetic and copies ran while one was open for 0% of the time, Pallas kernels for 1%

profile of v6, /device:TPU:0, one launch (start us, length us, event | category | flops | bytes accessed | tf_op | source)
XLA Modules:
  0.0 81.5 jit_solution(17675148526023075306)
XLA Ops:
  0.6 0.0 copy-start.1
  0.6 0.0 copy-start.2
  0.7 0.0 copy-start.3
  0.7 7.3 %sort_particles.1 = (bf16[64,8320]{1,0:T(8,128)(2,1)}, bf16[64,8320]{1,0:T(8,128)(2,1)}, bf16[64,8320]{1,0:T(8,128)(2,1)}, bf16[64,8320]{1,0:T(8,128)(2,1)}) custom-call(bf16[2048,512]{1,0:T(8,128)(2,1)} %bitcast.15, s32[1,128]{1,0:T(1,128)} %bitcast.16, s32[1,128]{1,0:T(1,128)} %bitcast.17, s32[1,128]{1,0:T(1,128)} %bitcast.18, bf16[1,128]{1,0:T(2,128)(2,1)} %bitcast.19, ...), custom_call_target="tpu_custom_call" | custom-call | tf_op jit(solution)/shard_map/sort_particles/pallas_call | solution.py:212
  8.0 0.0 copy-start
  8.0 3.0 %collective-permute-start = (bf16[64,8320]{1,0:T(8,128)(2,1)}, bf16[64,8320]{1,0:T(8,128)(2,1)S(1)}, u32[]{:S(2)}, u32[]{:S(2)}) collective-permute-start(bf16[64,8320]{1,0:T(8,128)(2,1)} %get-tuple-element.7), channel_id=1, source_target_pairs={{0,1},{1,0},{2,3},{3,2},{4,5},{5,4},{6,7},{7,6},{8,9},{9,8},{10,11... | collective-permute-start | bytes 3194888 | tf_op jit(solution)/shard_map/ppermute | solution.py:385
  11.0 1.5 %collective-permute-start.1 = (bf16[64,8320]{1,0:T(8,128)(2,1)}, bf16[64,8320]{1,0:T(8,128)(2,1)S(1)}, u32[]{:S(2)}, u32[]{:S(2)}) collective-permute-start(bf16[64,8320]{1,0:T(8,128)(2,1)} %get-tuple-element.8), channel_id=1, source_target_pairs={{0,2},{1,3},{2,0},{3,1},{4,6},{5,7},{6,4},{7,5},{8,10},{9,11},{10,... | collective-permute-start | bytes 3194888 | tf_op jit(solution)/shard_map/ppermute | solution.py:385
  12.6 0.0 copy-done.2
  12.6 0.6 fold_projections.1.refs_4_
  13.2 1.6 %collective-permute-start.3 = (bf16[32,8320]{1,0:T(8,128)(2,1)S(1)}, bf16[32,8320]{1,0:T(8,128)(2,1)S(1)}, u32[]{:S(2)}, u32[]{:S(2)}) collective-permute-start(bf16[32,8320]{1,0:T(8,128)(2,1)S(1)} %fold_projections.1.refs_4_), channel_id=1, source_target_pairs={{0,4},{1,5},{2,6},{3,7},{4,8},{5,9},{6,10},{7,11},{8,12},{9,13},{1... | collective-permute-start | bytes 1597448 | tf_op jit(solution)/shard_map/ppermute | solution.py:359
  14.8 0.5 collective-permute-start.2
  15.3 2.1 %collective-permute-start.5 = (bf16[32,8320]{1,0:T(8,128)(2,1)S(1)}, bf16[32,8320]{1,0:T(8,128)(2,1)S(1)}, u32[]{:S(2)}, u32[]{:S(2)}) collective-permute-start(bf16[32,8320]{1,0:T(8,128)(2,1)S(1)} %fold_projections.1.refs_4_), channel_id=1, source_target_pairs={{0,12},{1,13},{2,14},{3,15},{4,0},{5,1},{6,2},{7,3},{8,4},{9,5},{1... | collective-permute-start | bytes 1597448 | tf_op jit(solution)/shard_map/ppermute | solution.py:359
  17.4 12.7 %collective-permute-done.3.refs_5_ = bf16[32,8320]{1,0:T(8,128)(2,1)S(1)} collective-permute-done((bf16[32,8320]{1,0:T(8,128)(2,1)S(1)}, bf16[32,8320]{1,0:T(8,128)(2,1)S(1)}, u32[]{:S(2)}, u32[]{:S(2)}) %collective-permute-start.3) | collective-permute-done | bytes 532512 | tf_op jit(solution)/shard_map/ppermute | solution.py:359
  30.1 0.7 collective-permute-start.4
  30.8 8.6 %collective-permute-done.5.refs_8_ = bf16[32,8320]{1,0:T(8,128)(2,1)S(1)} collective-permute-done((bf16[32,8320]{1,0:T(8,128)(2,1)S(1)}, bf16[32,8320]{1,0:T(8,128)(2,1)S(1)}, u32[]{:S(2)}, u32[]{:S(2)}) %collective-permute-start.5) | collective-permute-done | bytes 532512 | tf_op jit(solution)/shard_map/ppermute | solution.py:359
  39.4 1.3 %collective-permute-start.6 = (bf16[32,8320]{1,0:T(8,128)(2,1)S(1)}, bf16[32,8320]{1,0:T(8,128)(2,1)S(1)}, u32[]{:S(2)}, u32[]{:S(2)}) collective-permute-start(bf16[32,8320]{1,0:T(8,128)(2,1)S(1)} %collective-permute-done.5.refs_8_), channel_id=1, source_target_pairs={{4,0},{5,1},{6,2},{7,3},{8,4},{9,5},{10,6},{11,7},{20,16},{21,17},... | collective-permute-start | bytes 1597448 | tf_op jit(solution)/shard_map/ppermute | solution.py:365
  40.7 0.0 collective-permute-done.refs_1_
  40.7 18.3 %collective-permute-done.1.refs_2_ = bf16[64,8320]{1,0:T(8,128)(2,1)S(1)} collective-permute-done((bf16[64,8320]{1,0:T(8,128)(2,1)}, bf16[64,8320]{1,0:T(8,128)(2,1)S(1)}, u32[]{:S(2)}, u32[]{:S(2)}) %collective-permute-start.1) | collective-permute-done | bytes 1064992 | tf_op jit(solution)/shard_map/ppermute | solution.py:385
  59.0 0.0 collective-permute-done.2.refs_3_
  59.0 0.0 collective-permute-done.4.refs_6_
  59.0 0.0 collective-permute-done.6.refs_7_
  59.1 2.9 %score_and_spread.1 = bf16[256,768]{1,0:T(8,128)(2,1)S(1)} custom-call(bf16[64,8320]{1,0:T(8,128)(2,1)S(1)} %copy-done, bf16[64,8320]{1,0:T(8,128)(2,1)S(1)} %collective-permute-done.refs_1_, bf16[64,8320]{1,0:T(8,128)(2,1)S(1)} %collective-permute-done.1.refs_2_, bf16[64,8320]{1,0:T(8,128)(2,1)S(1)} %collective-permute-done.2.refs_3_, ...), custom_call_target="tpu_custom_call" | custom-call | tf_op jit(solution)/shard_map/score_and_spread/pallas_call | solution.py:300
  62.0 17.3 %all_to_all.9.x_ref = bf16[16,16,768]{2,1,0:T(8,128)(2,1)} all-to-all(bf16[16,16,768]{2,1,0:T(8,128)(2,1)S(1)} %bitcast.11), channel_id=1, replica_groups=mesh['half'=2,'owner'=16] {'owner'}, dimensions={0} | all-to-all | bytes 786432 | tf_op jit(solution)/shard_map/all_to_all | solution.py:390
  79.2 2.2 %finish_slab.1 = (f32[16,1024]{1,0:T(8,128)}, f32[16,512]{1,0:T(8,128)}) custom-call(bf16[16,16,768]{2,1,0:T(8,128)(2,1)} %all_to_all.9.x_ref, f32[256,512]{1,0:T(8,128)} %constant.5.clone.powers_ref), custom_call_target="tpu_custom_call" | custom-call | tf_op jit(solution)/shard_map/finish_slab/pallas_call | solution.py:348
  (3 shorter events, 0.0 us)
Async XLA Ops:
  0.6 11.9 %copy-start.1 = (bf16[32,16,1024]{2,1,0:T(8,128)(2,1)S(1)}, bf16[32,16,1024]{2,1,0:T(8,128)(2,1)}, u32[]{:S(2)}) copy-start(bf16[32,16,1024]{2,1,0:T(8,128)(2,1)} %param.15) | copy-start | bytes 3145732
  0.6 11.9 %copy-start.2 = (bf16[32,4,16]{0,2,1:T(8,128)(2,1)S(1)}, bf16[32,4,16]{0,2,1:T(8,128)(2,1)}, u32[]{:S(2)}) copy-start(bf16[32,4,16]{0,2,1:T(8,128)(2,1)} %param.16) | copy-start | bytes 12292
  0.7 11.9 %copy-start.3 = (s32[32]{0:T(128)S(1)}, s32[32]{0:T(128)}, u32[]{:S(2)}) copy-start(s32[32]{0:T(128)} %param.17) | copy-start | bytes 388
  8.0 51.0 %copy-start = (bf16[64,8320]{1,0:T(8,128)(2,1)S(1)}, bf16[64,8320]{1,0:T(8,128)(2,1)}, u32[]{:S(2)}) copy-start(bf16[64,8320]{1,0:T(8,128)(2,1)} %get-tuple-element.6.refs_0_) | copy-start | bytes 3194884
  8.0 32.7 %collective-permute-start = (bf16[64,8320]{1,0:T(8,128)(2,1)}, bf16[64,8320]{1,0:T(8,128)(2,1)S(1)}, u32[]{:S(2)}, u32[]{:S(2)}) collective-permute-start(bf16[64,8320]{1,0:T(8,128)(2,1)} %get-tuple-element.7), channel_id=1, source_target_pairs={{0,1},{1,0},{2,3},{3,2},{4,5},{5,4},{6,7},{7,6},{8,9},{9,8},{10,11... | collective-permute-start | bytes 3194888 | tf_op jit(solution)/shard_map/ppermute | solution.py:385
  11.0 48.0 %collective-permute-start.1 = (bf16[64,8320]{1,0:T(8,128)(2,1)}, bf16[64,8320]{1,0:T(8,128)(2,1)S(1)}, u32[]{:S(2)}, u32[]{:S(2)}) collective-permute-start(bf16[64,8320]{1,0:T(8,128)(2,1)} %get-tuple-element.8), channel_id=1, source_target_pairs={{0,2},{1,3},{2,0},{3,1},{4,6},{5,7},{6,4},{7,5},{8,10},{9,11},{10,... | collective-permute-start | bytes 3194888 | tf_op jit(solution)/shard_map/ppermute | solution.py:385
  13.2 16.9 %collective-permute-start.3 = (bf16[32,8320]{1,0:T(8,128)(2,1)S(1)}, bf16[32,8320]{1,0:T(8,128)(2,1)S(1)}, u32[]{:S(2)}, u32[]{:S(2)}) collective-permute-start(bf16[32,8320]{1,0:T(8,128)(2,1)S(1)} %fold_projections.1.refs_4_), channel_id=1, source_target_pairs={{0,4},{1,5},{2,6},{3,7},{4,8},{5,9},{6,10},{7,11},{8,12},{9,13},{1... | collective-permute-start | bytes 1597448 | tf_op jit(solution)/shard_map/ppermute | solution.py:359
  14.8 44.2 %collective-permute-start.2 = (bf16[64,8320]{1,0:T(8,128)(2,1)}, bf16[64,8320]{1,0:T(8,128)(2,1)S(1)}, u32[]{:S(2)}, u32[]{:S(2)}) collective-permute-start(bf16[64,8320]{1,0:T(8,128)(2,1)} %get-tuple-element.9), channel_id=1, source_target_pairs={{0,3},{1,2},{2,1},{3,0},{4,7},{5,6},{6,5},{7,4},{8,11},{9,10},{10,... | collective-permute-start | bytes 3194888 | tf_op jit(solution)/shard_map/ppermute | solution.py:385
  15.3 24.1 %collective-permute-start.5 = (bf16[32,8320]{1,0:T(8,128)(2,1)S(1)}, bf16[32,8320]{1,0:T(8,128)(2,1)S(1)}, u32[]{:S(2)}, u32[]{:S(2)}) collective-permute-start(bf16[32,8320]{1,0:T(8,128)(2,1)S(1)} %fold_projections.1.refs_4_), channel_id=1, source_target_pairs={{0,12},{1,13},{2,14},{3,15},{4,0},{5,1},{6,2},{7,3},{8,4},{9,5},{1... | collective-permute-start | bytes 1597448 | tf_op jit(solution)/shard_map/ppermute | solution.py:359
  30.1 28.9 %collective-permute-start.4 = (bf16[32,8320]{1,0:T(8,128)(2,1)S(1)}, bf16[32,8320]{1,0:T(8,128)(2,1)S(1)}, u32[]{:S(2)}, u32[]{:S(2)}) collective-permute-start(bf16[32,8320]{1,0:T(8,128)(2,1)S(1)} %collective-permute-done.3.refs_5_), channel_id=1, source_target_pairs={{4,8},{5,9},{6,10},{7,11},{8,12},{9,13},{10,14},{11,15},{20,24},{2... | collective-permute-start | bytes 1597448 | tf_op jit(solution)/shard_map/ppermute | solution.py:364
  39.4 19.6 %collective-permute-start.6 = (bf16[32,8320]{1,0:T(8,128)(2,1)S(1)}, bf16[32,8320]{1,0:T(8,128)(2,1)S(1)}, u32[]{:S(2)}, u32[]{:S(2)}) collective-permute-start(bf16[32,8320]{1,0:T(8,128)(2,1)S(1)} %collective-permute-done.5.refs_8_), channel_id=1, source_target_pairs={{4,0},{5,1},{6,2},{7,3},{8,4},{9,5},{10,6},{11,7},{20,16},{21,17},... | collective-permute-start | bytes 1597448 | tf_op jit(solution)/shard_map/ppermute | solution.py:365

commit v7 on v6

--- a/solution.py
+++ b/solution.py
@@ -219,7 +219,7 @@
             pltpu.VMEM((length // 128, particles * lines, 128), F32),
             pltpu.VMEM((slots, width), BF16),
             pltpu.SemaphoreType.DMA((5,)),
-            pltpu.SemaphoreType.DMA((4,)),
+            pltpu.SemaphoreType.DMA((2,)),
             pltpu.SemaphoreType.DMA((pieces, groups)),
         ],
         compiler_params=vmem(60),
@@ -315,32 +315,36 @@
     folded = np.minimum(column, length - column).astype(np.float32) / np.float32(length)
     phase = (defocus * np.float32(1500.0))[:, None] * (folded * folded)[None, :] + np.float32(0.2)
     powers = np.sin(phase.astype(np.float64)) ** 2 * scale
-    return jnp.asarray(np.where(level[:, None] <= 192, powers, 0.0), F32)
+    powers = np.where(level[:, None] <= 192, powers, 0.0)
+    coarse = powers.astype(jnp.bfloat16)
+    fine = (powers - coarse.astype(np.float64)).astype(jnp.bfloat16)
+    return jnp.asarray(np.stack([coarse, fine]))
+
+
+def pieces_of(values, count):
+    pieces = []
+    for _ in range(count):
+        pieces.append(values.astype(BF16))
+        values = values - pieces[-1].astype(F32)
+    return jnp.concatenate([piece.astype(F32) for piece in pieces], axis=0).astype(BF16)
 
 
 def finish_kernel(x_ref, powers_ref, slab_ref, weights_ref):
-    half = slab_ref.shape[1] // 4
+    rows, half = slab_ref.shape[0], slab_ref.shape[1] // 4
     total = jnp.sum(x_ref[...].astype(F32), axis=0)
-    flip = mirror(half)
-
-    def mirrored(part):
-        out = jnp.zeros(part.shape, F32)
-        for _ in range(3):
-            piece = part.astype(BF16)
-            out = out + jnp.dot(piece, flip, preferred_element_type=F32)
-            part = part - piece.astype(F32)
-        return out
-
     real, imag = total[:, :half], total[:, half : 2 * half]
+    both = pieces_of(jnp.concatenate([real, imag], axis=0), 3)
+    turned = jnp.dot(both, mirror(half), preferred_element_type=F32)
+    turned = turned[: 2 * rows] + turned[2 * rows : 4 * rows] + turned[4 * rows :]
     first = lax.broadcasted_iota(jnp.int32, real.shape, 1) == 0
     slab_ref[:, :half] = real
-    slab_ref[:, half : 2 * half] = jnp.where(first, imag[:, :1], mirrored(real))
+    slab_ref[:, half : 2 * half] = jnp.where(first, imag[:, :1], turned[:rows])
     slab_ref[:, 2 * half : 3 * half] = jnp.where(first, 0.0, imag)
-    slab_ref[:, 3 * half :] = jnp.where(first, 0.0, -mirrored(imag))
-    weights_ref[...] = jnp.dot(
-        total[:, 2 * half :], powers_ref[...], precision=lax.Precision.HIGHEST,
-        preferred_element_type=F32,
-    )
+    slab_ref[:, 3 * half :] = jnp.where(first, 0.0, -turned[rows:])
+    levels = pieces_of(total[:, 2 * half :], 2)
+    coarse = jnp.dot(levels, powers_ref[0], preferred_element_type=F32)
+    fine = jnp.dot(levels[:rows], powers_ref[1], preferred_element_type=F32)
+    weights_ref[...] = coarse[:rows] + coarse[rows:] + fine
 
 
 def finish(received, length, scale):

time: 81.7 us -> 80.9 us (level)
  no operation moved by 1% of the time
where the time goes in v7:
time: 80.9 us; the launch traced here: 80.7 us
  waiting for transfers between devices  39.6 us (49%)
  blocking collectives  17.3 us (21%)
  Pallas kernels  12.4 us (15%)
  starting transfers between devices  10.7 us (13%)
    ppermute x2, waiting for transfers between devices, gather_rows(): lax.ppermute(block, 'owner', [(k, (k + i * count) % owners) for k in rang...  21.3 us
    ppermute x3, waiting for transfers between devices, on_device(): lax.ppermute(a, 'owner', [(k, k ^ i) for k in range(owners)])  18.3 us
    all_to_all x1, blocking collectives, on_device(): lax.all_to_all(partial, 'owner', split_axis=0, concat_axis=0, tiled=True)  17.3 us
    pallas_call x1, Pallas kernels, sort_particles(): pl.pallas_call(lambda *refs: sort_kernel(reach, count, capacity, pairs, *...  6.8 us
    ppermute x3, starting transfers between devices, on_device(): lax.ppermute(a, 'owner', [(k, k ^ i) for k in range(owners)])  5 us
    ppermute x2, starting transfers between devices, gather_rows(): lax.ppermute(block, 'owner', [(k, (k + i * count) % owners) for k in rang...  3.74 us
    pallas_call x1, Pallas kernels, score_and_spread(): pl.pallas_call(lambda *refs: score_kernel(1.0 / math.sqrt(lines * length)...  2.9 us
    pallas_call x1, Pallas kernels, finish(): pl.pallas_call(finish_kernel, out_shape=(jax.ShapeDtypeStruct((rows, 2 *...  2.03 us
  transfers between devices with their start and end apart: 7, of which 3 were waited for; matrix products, arithmetic and copies ran while one was open for 0% of the time, Pallas kernels for 1%

profile of v7, /device:TPU:0, one launch (start us, length us, event | category | flops | bytes accessed | tf_op | source)
XLA Modules:
  0.0 80.7 jit_solution(6158328506165192191)
XLA Ops:
  0.6 0.0 copy-start.1
  0.6 0.0 copy-start.2
  0.7 0.0 copy-start.3
  0.7 6.8 %sort_particles.1 = (bf16[64,8320]{1,0:T(8,128)(2,1)}, bf16[64,8320]{1,0:T(8,128)(2,1)}, bf16[64,8320]{1,0:T(8,128)(2,1)}, bf16[64,8320]{1,0:T(8,128)(2,1)}) custom-call(bf16[2048,512]{1,0:T(8,128)(2,1)} %bitcast.15, s32[1,128]{1,0:T(1,128)} %bitcast.16, s32[1,128]{1,0:T(1,128)} %bitcast.17, s32[1,128]{1,0:T(1,128)} %bitcast.18, bf16[1,128]{1,0:T(2,128)(2,1)} %bitcast.19, ...), custom_call_target="tpu_custom_call" | custom-call | tf_op jit(solution)/shard_map/sort_particles/pallas_call | solution.py:212
  7.5 0.0 copy-start
  7.5 3.0 %collective-permute-start = (bf16[64,8320]{1,0:T(8,128)(2,1)}, bf16[64,8320]{1,0:T(8,128)(2,1)S(1)}, u32[]{:S(2)}, u32[]{:S(2)}) collective-permute-start(bf16[64,8320]{1,0:T(8,128)(2,1)} %get-tuple-element.7), channel_id=1, source_target_pairs={{0,1},{1,0},{2,3},{3,2},{4,5},{5,4},{6,7},{7,6},{8,9},{9,8},{10,11... | collective-permute-start | bytes 3194888 | tf_op jit(solution)/shard_map/ppermute | solution.py:389
  10.5 1.5 %collective-permute-start.1 = (bf16[64,8320]{1,0:T(8,128)(2,1)}, bf16[64,8320]{1,0:T(8,128)(2,1)S(1)}, u32[]{:S(2)}, u32[]{:S(2)}) collective-permute-start(bf16[64,8320]{1,0:T(8,128)(2,1)} %get-tuple-element.8), channel_id=1, source_target_pairs={{0,2},{1,3},{2,0},{3,1},{4,6},{5,7},{6,4},{7,5},{8,10},{9,11},{10,... | collective-permute-start | bytes 3194888 | tf_op jit(solution)/shard_map/ppermute | solution.py:389
  12.0 0.0 copy-done.1
  12.0 0.6 fold_projections.1.refs_4_
  12.7 1.6 %collective-permute-start.3 = (bf16[32,8320]{1,0:T(8,128)(2,1)S(1)}, bf16[32,8320]{1,0:T(8,128)(2,1)S(1)}, u32[]{:S(2)}, u32[]{:S(2)}) collective-permute-start(bf16[32,8320]{1,0:T(8,128)(2,1)S(1)} %fold_projections.1.refs_4_), channel_id=1, source_target_pairs={{0,4},{1,5},{2,6},{3,7},{4,8},{5,9},{6,10},{7,11},{8,12},{9,13},{1... | collective-permute-start | bytes 1597448 | tf_op jit(solution)/shard_map/ppermute | solution.py:363
  14.3 0.5 collective-permute-start.2
  14.8 2.1 %collective-permute-start.5 = (bf16[32,8320]{1,0:T(8,128)(2,1)S(1)}, bf16[32,8320]{1,0:T(8,128)(2,1)S(1)}, u32[]{:S(2)}, u32[]{:S(2)}) collective-permute-start(bf16[32,8320]{1,0:T(8,128)(2,1)S(1)} %fold_projections.1.refs_4_), channel_id=1, source_target_pairs={{0,12},{1,13},{2,14},{3,15},{4,0},{5,1},{6,2},{7,3},{8,4},{9,5},{1... | collective-permute-start | bytes 1597448 | tf_op jit(solution)/shard_map/ppermute | solution.py:363
  16.9 12.7 %collective-permute-done.3.refs_5_ = bf16[32,8320]{1,0:T(8,128)(2,1)S(1)} collective-permute-done((bf16[32,8320]{1,0:T(8,128)(2,1)S(1)}, bf16[32,8320]{1,0:T(8,128)(2,1)S(1)}, u32[]{:S(2)}, u32[]{:S(2)}) %collective-permute-start.3) | collective-permute-done | bytes 532512 | tf_op jit(solution)/shard_map/ppermute | solution.py:363
  29.6 0.7 collective-permute-start.4
  30.3 8.6 %collective-permute-done.5.refs_8_ = bf16[32,8320]{1,0:T(8,128)(2,1)S(1)} collective-permute-done((bf16[32,8320]{1,0:T(8,128)(2,1)S(1)}, bf16[32,8320]{1,0:T(8,128)(2,1)S(1)}, u32[]{:S(2)}, u32[]{:S(2)}) %collective-permute-start.5) | collective-permute-done | bytes 532512 | tf_op jit(solution)/shard_map/ppermute | solution.py:363
  38.9 1.3 %collective-permute-start.6 = (bf16[32,8320]{1,0:T(8,128)(2,1)S(1)}, bf16[32,8320]{1,0:T(8,128)(2,1)S(1)}, u32[]{:S(2)}, u32[]{:S(2)}) collective-permute-start(bf16[32,8320]{1,0:T(8,128)(2,1)S(1)} %collective-permute-done.5.refs_8_), channel_id=1, source_target_pairs={{4,0},{5,1},{6,2},{7,3},{8,4},{9,5},{10,6},{11,7},{20,16},{21,17},... | collective-permute-start | bytes 1597448 | tf_op jit(solution)/shard_map/ppermute | solution.py:369
  40.2 0.0 collective-permute-done.refs_1_
  40.2 18.3 %collective-permute-done.1.refs_2_ = bf16[64,8320]{1,0:T(8,128)(2,1)S(1)} collective-permute-done((bf16[64,8320]{1,0:T(8,128)(2,1)}, bf16[64,8320]{1,0:T(8,128)(2,1)S(1)}, u32[]{:S(2)}, u32[]{:S(2)}) %collective-permute-start.1) | collective-permute-done | bytes 1064992 | tf_op jit(solution)/shard_map/ppermute | solution.py:389
  58.5 0.0 collective-permute-done.2.refs_3_
  58.5 0.0 collective-permute-done.4.refs_6_
  58.5 0.0 collective-permute-done.6.refs_7_
  58.5 2.9 %score_and_spread.1 = bf16[256,768]{1,0:T(8,128)(2,1)S(1)} custom-call(bf16[64,8320]{1,0:T(8,128)(2,1)S(1)} %copy-done, bf16[64,8320]{1,0:T(8,128)(2,1)S(1)} %collective-permute-done.refs_1_, bf16[64,8320]{1,0:T(8,128)(2,1)S(1)} %collective-permute-done.1.refs_2_, bf16[64,8320]{1,0:T(8,128)(2,1)S(1)} %collective-permute-done.2.refs_3_, ...), custom_call_target="tpu_custom_call" | custom-call | tf_op jit(solution)/shard_map/score_and_spread/pallas_call | solution.py:300
  61.4 17.3 %all_to_all.9.x_ref = bf16[16,16,768]{2,1,0:T(8,128)(2,1)} all-to-all(bf16[16,16,768]{2,1,0:T(8,128)(2,1)S(1)} %bitcast.11), channel_id=1, replica_groups=mesh['half'=2,'owner'=16] {'owner'}, dimensions={0} | all-to-all | bytes 786432 | tf_op jit(solution)/shard_map/all_to_all | solution.py:394
  78.7 2.0 %finish_slab.1 = (f32[16,1024]{1,0:T(8,128)}, f32[16,512]{1,0:T(8,128)}) custom-call(bf16[16,16,768]{2,1,0:T(8,128)(2,1)} %all_to_all.9.x_ref, bf16[2,256,512]{2,1,0:T(8,128)(2,1)} %constant.5.clone.powers_ref), custom_call_target="tpu_custom_call" | custom-call | tf_op jit(solution)/shard_map/finish_slab/pallas_call | solution.py:352
  (3 shorter events, 0.0 us)
Async XLA Ops:
  0.6 11.4 %copy-start.1 = (bf16[32,16,1024]{2,1,0:T(8,128)(2,1)S(1)}, bf16[32,16,1024]{2,1,0:T(8,128)(2,1)}, u32[]{:S(2)}) copy-start(bf16[32,16,1024]{2,1,0:T(8,128)(2,1)} %param.15) | copy-start | bytes 3145732
  0.6 11.4 %copy-start.2 = (bf16[32,4,16]{0,2,1:T(8,128)(2,1)S(1)}, bf16[32,4,16]{0,2,1:T(8,128)(2,1)}, u32[]{:S(2)}) copy-start(bf16[32,4,16]{0,2,1:T(8,128)(2,1)} %param.16) | copy-start | bytes 12292
  0.7 11.4 %copy-start.3 = (s32[32]{0:T(128)S(1)}, s32[32]{0:T(128)}, u32[]{:S(2)}) copy-start(s32[32]{0:T(128)} %param.17) | copy-start | bytes 388
  7.5 51.0 %copy-start = (bf16[64,8320]{1,0:T(8,128)(2,1)S(1)}, bf16[64,8320]{1,0:T(8,128)(2,1)}, u32[]{:S(2)}) copy-start(bf16[64,8320]{1,0:T(8,128)(2,1)} %get-tuple-element.6.refs_0_) | copy-start | bytes 3194884
  7.5 32.7 %collective-permute-start = (bf16[64,8320]{1,0:T(8,128)(2,1)}, bf16[64,8320]{1,0:T(8,128)(2,1)S(1)}, u32[]{:S(2)}, u32[]{:S(2)}) collective-permute-start(bf16[64,8320]{1,0:T(8,128)(2,1)} %get-tuple-element.7), channel_id=1, source_target_pairs={{0,1},{1,0},{2,3},{3,2},{4,5},{5,4},{6,7},{7,6},{8,9},{9,8},{10,11... | collective-permute-start | bytes 3194888 | tf_op jit(solution)/shard_map/ppermute | solution.py:389
  10.5 48.0 %collective-permute-start.1 = (bf16[64,8320]{1,0:T(8,128)(2,1)}, bf16[64,8320]{1,0:T(8,128)(2,1)S(1)}, u32[]{:S(2)}, u32[]{:S(2)}) collective-permute-start(bf16[64,8320]{1,0:T(8,128)(2,1)} %get-tuple-element.8), channel_id=1, source_target_pairs={{0,2},{1,3},{2,0},{3,1},{4,6},{5,7},{6,4},{7,5},{8,10},{9,11},{10,... | collective-permute-start | bytes 3194888 | tf_op jit(solution)/shard_map/ppermute | solution.py:389
  12.7 16.9 %collective-permute-start.3 = (bf16[32,8320]{1,0:T(8,128)(2,1)S(1)}, bf16[32,8320]{1,0:T(8,128)(2,1)S(1)}, u32[]{:S(2)}, u32[]{:S(2)}) collective-permute-start(bf16[32,8320]{1,0:T(8,128)(2,1)S(1)} %fold_projections.1.refs_4_), channel_id=1, source_target_pairs={{0,4},{1,5},{2,6},{3,7},{4,8},{5,9},{6,10},{7,11},{8,12},{9,13},{1... | collective-permute-start | bytes 1597448 | tf_op jit(solution)/shard_map/ppermute | solution.py:363
  14.3 44.2 %collective-permute-start.2 = (bf16[64,8320]{1,0:T(8,128)(2,1)}, bf16[64,8320]{1,0:T(8,128)(2,1)S(1)}, u32[]{:S(2)}, u32[]{:S(2)}) collective-permute-start(bf16[64,8320]{1,0:T(8,128)(2,1)} %get-tuple-element.9), channel_id=1, source_target_pairs={{0,3},{1,2},{2,1},{3,0},{4,7},{5,6},{6,5},{7,4},{8,11},{9,10},{10,... | collective-permute-start | bytes 3194888 | tf_op jit(solution)/shard_map/ppermute | solution.py:389
  14.8 24.1 %collective-permute-start.5 = (bf16[32,8320]{1,0:T(8,128)(2,1)S(1)}, bf16[32,8320]{1,0:T(8,128)(2,1)S(1)}, u32[]{:S(2)}, u32[]{:S(2)}) collective-permute-start(bf16[32,8320]{1,0:T(8,128)(2,1)S(1)} %fold_projections.1.refs_4_), channel_id=1, source_target_pairs={{0,12},{1,13},{2,14},{3,15},{4,0},{5,1},{6,2},{7,3},{8,4},{9,5},{1... | collective-permute-start | bytes 1597448 | tf_op jit(solution)/shard_map/ppermute | solution.py:363
  29.6 28.9 %collective-permute-start.4 = (bf16[32,8320]{1,0:T(8,128)(2,1)S(1)}, bf16[32,8320]{1,0:T(8,128)(2,1)S(1)}, u32[]{:S(2)}, u32[]{:S(2)}) collective-permute-start(bf16[32,8320]{1,0:T(8,128)(2,1)S(1)} %collective-permute-done.3.refs_5_), channel_id=1, source_target_pairs={{4,8},{5,9},{6,10},{7,11},{8,12},{9,13},{10,14},{11,15},{20,24},{2... | collective-permute-start | bytes 1597448 | tf_op jit(solution)/shard_map/ppermute | solution.py:368
  38.9 19.6 %collective-permute-start.6 = (bf16[32,8320]{1,0:T(8,128)(2,1)S(1)}, bf16[32,8320]{1,0:T(8,128)(2,1)S(1)}, u32[]{:S(2)}, u32[]{:S(2)}) collective-permute-start(bf16[32,8320]{1,0:T(8,128)(2,1)S(1)} %collective-permute-done.5.refs_8_), channel_id=1, source_target_pairs={{4,0},{5,1},{6,2},{7,3},{8,4},{9,5},{10,6},{11,7},{20,16},{21,17},... | collective-permute-start | bytes 1597448 | tf_op jit(solution)/shard_map/ppermute | solution.py:369

commit v8 on v7

--- a/solution.py
+++ b/solution.py
@@ -102,7 +102,7 @@
     )(projections.reshape(pairs * lines, width), taps, pair_class[None, :])
 
 
-def sort_kernel(reach, count, capacity, pairs, *refs):
+def sort_kernel(first, reach, count, capacity, pairs, *refs):
     sources, refs = refs[:6], refs[6:]
     *outs, x_ref, owner_ref, pair_ref, shift_ref, defocus_ref, table_ref, wide, sorted_ref, in_sem, x_sem, out_sem = refs
     loads = [
@@ -112,18 +112,16 @@
         )
     ]
     parts = x_sem.shape[0]
-    share = x_ref.shape[0] // parts
+    particles, lines, length = x_ref.shape
+    share = particles // parts
     cuts = [slice(i * share, (i + 1) * share) for i in range(parts)]
     chunks = [
-        pltpu.make_async_copy(sources[0].at[cut], x_ref.at[cut], x_sem.at[i])
+        pltpu.make_async_copy(sources[0].at[cut, first : first + lines], x_ref.at[cut], x_sem.at[i])
         for i, cut in enumerate(cuts)
     ]
     for copy in loads + chunks:
         copy.start()
-    particles = owner_ref.shape[1]
-    length = x_ref.shape[1]
     half = length // 2
-    lines = x_ref.shape[0] // particles
     slots = sorted_ref.shape[0]
     each = slots // len(outs)
     row = lax.broadcasted_iota(jnp.int32, (particles, particles), 0)
@@ -152,8 +150,10 @@
     facts = jnp.where(kind == 1, pair.astype(F32), facts)
     facts = jnp.where(kind == 2, shift_ref[...].astype(F32), facts)
     facts = flipped(jnp.where(kind == 4, defocus, facts))
-    picked = jnp.dot(pick, facts.astype(BF16), preferred_element_type=F32)
-    sorted_ref[:, lines * length :] = picked.astype(BF16)
+    extra = 0 if first else 128
+    if extra:
+        picked = jnp.dot(pick, facts.astype(BF16), preferred_element_type=F32)
+        sorted_ref[:, lines * length :] = picked.astype(BF16)
 
     column = lax.broadcasted_iota(jnp.int32, (particles, half + 128), 1)
     folded = column.astype(F32) * (1.0 / length)
@@ -170,12 +170,13 @@
     sine = ctf[:, :half] * swing
 
     loads[4].wait()
-    for chunk, cut in zip(chunks, cuts):
+    for i, (chunk, cut) in enumerate(zip(chunks, cuts)):
         chunk.wait()
-        spectra = jnp.dot(x_ref[cut], table_ref[...], preferred_element_type=F32)
+        rows = x_ref[cut].reshape(share * lines, length)
+        spectra = jnp.dot(rows, table_ref[...], preferred_element_type=F32)
         spectra = spectra.astype(BF16).astype(F32)
         for t in range(length // 128):
-            wide[t, cut] = spectra[:, t * 128 : (t + 1) * 128]
+            wide[t, i * share * lines : (i + 1) * share * lines] = spectra[:, t * 128 : (t + 1) * 128]
     groups = out_sem.shape[1]
     stores = []
     for line in range(lines):
@@ -189,7 +190,7 @@
         if (line + 1) % (lines // groups) == 0:
             group = line * groups // lines
             wide_group = lines // groups * length
-            end = (group + 1) * wide_group + (128 if line == lines - 1 else 0)
+            end = (group + 1) * wide_group + (extra if line == lines - 1 else 0)
             for j, out in enumerate(outs):
                 stores.append(
                     pltpu.make_async_copy(
@@ -203,18 +204,19 @@
         store.wait()
 
 
-def sort_particles(images, owner, pair, shift, defocus, reach, count, capacity, pairs, pieces):
-    particles, lines, length = images.shape
+def sort_particles(first, lines, images, owner, pair, shift, defocus, reach, count, capacity, pairs, pieces):
+    particles, _, length = images.shape
     slots = count * capacity
-    each, width, groups = slots // pieces, lines * length + 128, 4
-    args = [images.reshape(particles * lines, length)] + [a[None, :] for a in (owner, pair, shift, defocus)]
+    each, width, groups = slots // pieces, lines * length + (0 if first else 128), 4
+    args = [images] + [a[None, :] for a in (owner, pair, shift, defocus)]
     args.append(packed_table(length))
     return pl.pallas_call(
-        lambda *refs: sort_kernel(reach, count, capacity, pairs, *refs),
+        lambda *refs: sort_kernel(first, reach, count, capacity, pairs, *refs),
         in_specs=[HBM] * 6,
         out_specs=[HBM] * pieces,
         out_shape=[jax.ShapeDtypeStruct((each, width), BF16)] * pieces,
-        scratch_shapes=[pltpu.VMEM(a.shape, a.dtype) for a in args]
+        scratch_shapes=[pltpu.VMEM((particles, lines, length), BF16)]
+        + [pltpu.VMEM(a.shape, a.dtype) for a in args[1:]]
         + [
             pltpu.VMEM((length // 128, particles * lines, 128), F32),
             pltpu.VMEM((slots, width), BF16),
@@ -233,6 +235,8 @@
 
 def score_kernel(scale, n_images, sizes, slab_lines, lines, length, *refs):
     images, refs = refs[:n_images], refs[n_images:]
+    later, refs = refs[:n_images], refs[n_images:]
+    early = images[0].shape[1] // length
     blocks = []
     for size in sizes:
         blocks.append(refs[:size])
@@ -240,13 +244,14 @@
     out_ref, taps = refs
     info = joined(blocks, slice(lines * length, lines * length + 128))
     pairs, rows = info.shape[0], out_ref.shape[0]
-    found = jnp.concatenate([ref[:, lines * length :] for ref in images], axis=0).astype(F32)
+    found = jnp.concatenate([ref[:, early * length :] for ref in images], axis=0).astype(F32)
     slots = found.shape[0]
     here = 4
 
     def stacked(line):
+        refs, place = (images, line) if line < early else (later, line - early)
         return jnp.concatenate(
-            [ref[:, line * length : (line + 1) * length] for ref in images], axis=0
+            [ref[:, place * length : (place + 1) * length] for ref in refs], axis=0
         )
 
     scores = jnp.zeros((slots, pairs), F32)
@@ -293,7 +298,7 @@
     out_ref[:, length:] = levels.astype(BF16)
 
 
-def score_and_spread(images, references, rows, slab_lines, lines, length):
+def score_and_spread(images, later, references, rows, slab_lines, lines, length):
     slots = sum(a.shape[0] for a in images)
     sizes = [len(a) for a in references]
     references = [a for blocks in references for a in blocks]
@@ -305,7 +310,7 @@
         scratch_shapes=[pltpu.VMEM((slots // 128, 128, 128), F32)],
         compiler_params=vmem(24),
         name="score_and_spread",
-    )(*images, *references)
+    )(*images, *later, *references)
 
 
 def level_powers(length, scale):
@@ -381,16 +386,21 @@
     reach = max(1, capacity // 4)
     count = owners // reach
     pieces = count if reach > 1 else 1
-    moved = sort_particles(
-        images, owner_of[:, 0], pair_of, shift_of, defocus, reach, count, reach * capacity, pairs, pieces
-    )
+    early = lines // 2
+    swap = lambda a, i: lax.ppermute(a, "owner", [(k, k ^ i) for k in range(owners)]) if i else a
+    arrived = []
+    for first, some in ((0, early), (early, lines - early)):
+        moved = sort_particles(
+            first, some, images, owner_of[:, 0], pair_of, shift_of, defocus, reach, count,
+            reach * capacity, pairs, pieces,
+        )
+        if reach > 1:
+            arrived.append([swap(a, i) for i, a in enumerate(moved)])
+        else:
+            send = lambda a: lax.all_to_all(a, "owner", split_axis=0, concat_axis=0, tiled=True)
+            arrived.append([send(moved[0])])
     references = gather_rows(fold(projections, interp_weights, pair_class), owners, reach, count)
-    if reach > 1:
-        swap = lambda a, i: lax.ppermute(a, "owner", [(k, k ^ i) for k in range(owners)]) if i else a
-        arrived = [swap(a, i) for i, a in enumerate(moved)]
-    else:
-        arrived = [lax.all_to_all(moved[0], "owner", split_axis=0, concat_axis=0, tiled=True)]
-    partial = score_and_spread(arrived, references, rows, slab_lines, lines, length)
+    partial = score_and_spread(*arrived, references, rows, slab_lines, lines, length)
     received = lax.all_to_all(partial, "owner", split_axis=0, concat_axis=0, tiled=True)
     return finish(
         received.reshape(owners, rows // owners, -1), length, CLASSES / (particles * owners)

time: 80.9 us -> 79.5 us (0.983)
  waiting for transfers between devices: 39.6 us -> 31.1 us
  starting transfers between devices: 10.7 us -> 15.1 us
  Pallas kernels: 12.4 us -> 13.9 us
  local copies, waits for them, and re-layouts: 0.02 us -> 1.06 us
    ppermute x2, waiting for transfers between devices: 21.3 us -> 0.01 us  [gather_rows(): lax.ppermute(block, 'owner', [(k, (k + i * count) % owners) for k in rang...]
    ppermute x3 -> x6, waiting for transfers between devices: 18.3 us -> 31.1 us  [on_device(): lax.ppermute(a, 'owner', [(k, k ^ i) for k in range(owners)])]
    ppermute x3 -> x6, starting transfers between devices: 5 us -> 8.98 us  [on_device(): lax.ppermute(a, 'owner', [(k, k ^ i) for k in range(owners)])]
    pallas_call x1 -> x2, Pallas kernels: 6.8 us -> 8.27 us  [sort_particles(): pl.pallas_call(lambda *refs: sort_kernel(first, reach, count, capacity, p...]
    unnamed x8 -> x10, local copies, waits for them, and re-layouts: 0.02 us -> 1.06 us
  transfers between devices with their start and end apart: 7 -> 10, of which waited for: 3 -> 4; matrix products, arithmetic and copies ran while one was open for 0% -> 0% of each run, Pallas kernels for 1% -> 6%
where the time goes in v8:
time: 79.5 us; the launch traced here: 79.2 us
  waiting for transfers between devices  31.1 us (39%)
  blocking collectives  17.3 us (22%)
  starting transfers between devices  15.1 us (19%)
  Pallas kernels  13.9 us (17%)
  local copies, waits for them, and re-layouts  1.06 us (1%)
    ppermute x6, waiting for transfers between devices, on_device(): lax.ppermute(a, 'owner', [(k, k ^ i) for k in range(owners)])  31.1 us
    all_to_all x1, blocking collectives, on_device(): lax.all_to_all(partial, 'owner', split_axis=0, concat_axis=0, tiled=True)  17.3 us
    ppermute x6, starting transfers between devices, on_device(): lax.ppermute(a, 'owner', [(k, k ^ i) for k in range(owners)])  8.98 us
    pallas_call x2, Pallas kernels, sort_particles(): pl.pallas_call(lambda *refs: sort_kernel(first, reach, count, capacity, p...  8.27 us
    ppermute x2, starting transfers between devices, gather_rows(): lax.ppermute(block, 'owner', [(k, (k + i * count) % owners) for k in rang...  4.18 us
    pallas_call x1, Pallas kernels, score_and_spread(): pl.pallas_call(lambda *refs: score_kernel(1.0 / math.sqrt(lines * length)...  2.94 us
    pallas_call x1, Pallas kernels, finish(): pl.pallas_call(finish_kernel, out_shape=(jax.ShapeDtypeStruct((rows, 2 *...  2.03 us
  transfers between devices with their start and end apart: 10, of which 4 were waited for; matrix products, arithmetic and copies ran while one was open for 0% of the time, Pallas kernels for 6%

profile of v8, /device:TPU:0, one launch (start us, length us, event | category | flops | bytes accessed | tf_op | source)
XLA Modules:
  0.0 79.2 jit_solution(1995182578788885461)
XLA Ops:
  0.7 4.2 %sort_particles.3 = (bf16[64,4096]{1,0:T(8,128)(2,1)}, bf16[64,4096]{1,0:T(8,128)(2,1)}, bf16[64,4096]{1,0:T(8,128)(2,1)}, bf16[64,4096]{1,0:T(8,128)(2,1)}) custom-call(bf16[128,16,512]{2,1,0:T(8,128)(2,1)} %refs_0_.3, s32[1,128]{1,0:T(1,128)} %bitcast.14, s32[1,128]{1,0:T(1,128)} %bitcast.16, s32[1,128]{1,0:T(1,128)} %bitcast.18, bf16[1,128]{1,0:T(2,128)(2,1)} %bitcast.20, ...), custom_call_target="tpu_custom_call" | custom-call | tf_op jit(solution)/shard_map/sort_particles/pallas_call | solution.py:213
  4.9 3.0 %collective-permute-start.3 = (bf16[64,4096]{1,0:T(8,128)(2,1)}, bf16[64,4096]{1,0:T(8,128)(2,1)S(1)}, u32[]{:S(2)}, u32[]{:S(2)}) collective-permute-start(bf16[64,4096]{1,0:T(8,128)(2,1)} %get-tuple-element.15), channel_id=1, source_target_pairs={{0,1},{1,0},{2,3},{3,2},{4,5},{5,4},{6,7},{7,6},{8,9},{9,8},{10,11... | collective-permute-start | bytes 1572872 | tf_op jit(solution)/shard_map/ppermute | solution.py:390
  7.9 1.5 %collective-permute-start.4 = (bf16[64,4096]{1,0:T(8,128)(2,1)}, bf16[64,4096]{1,0:T(8,128)(2,1)S(1)}, u32[]{:S(2)}, u32[]{:S(2)}) collective-permute-start(bf16[64,4096]{1,0:T(8,128)(2,1)} %get-tuple-element.16), channel_id=1, source_target_pairs={{0,2},{1,3},{2,0},{3,1},{4,6},{5,7},{6,4},{7,5},{8,10},{9,11},{10,... | collective-permute-start | bytes 1572872 | tf_op jit(solution)/shard_map/ppermute | solution.py:390
  9.4 0.0 collective-permute-start.5
  9.4 0.6 fold_projections.1.refs_8_
  10.1 2.1 %collective-permute-start.6 = (bf16[32,8320]{1,0:T(8,128)(2,1)S(1)}, bf16[32,8320]{1,0:T(8,128)(2,1)S(1)}, u32[]{:S(2)}, u32[]{:S(2)}) collective-permute-start(bf16[32,8320]{1,0:T(8,128)(2,1)S(1)} %fold_projections.1.refs_8_), channel_id=1, source_target_pairs={{0,4},{1,5},{2,6},{3,7},{4,8},{5,9},{6,10},{7,11},{8,12},{9,13},{1... | collective-permute-start | bytes 1597448 | tf_op jit(solution)/shard_map/ppermute | solution.py:368
  12.2 2.1 %collective-permute-start.8 = (bf16[32,8320]{1,0:T(8,128)(2,1)S(1)}, bf16[32,8320]{1,0:T(8,128)(2,1)S(1)}, u32[]{:S(2)}, u32[]{:S(2)}) collective-permute-start(bf16[32,8320]{1,0:T(8,128)(2,1)S(1)} %fold_projections.1.refs_8_), channel_id=1, source_target_pairs={{0,12},{1,13},{2,14},{3,15},{4,0},{5,1},{6,2},{7,3},{8,4},{9,5},{1... | collective-permute-start | bytes 1597448 | tf_op jit(solution)/shard_map/ppermute | solution.py:368
  14.2 4.1 %sort_particles.2 = (bf16[64,4224]{1,0:T(8,128)(2,1)}, bf16[64,4224]{1,0:T(8,128)(2,1)}, bf16[64,4224]{1,0:T(8,128)(2,1)}, bf16[64,4224]{1,0:T(8,128)(2,1)}) custom-call(bf16[128,16,512]{2,1,0:T(8,128)(2,1)} %refs_0_.3, s32[1,128]{1,0:T(1,128)} %bitcast.15, s32[1,128]{1,0:T(1,128)} %bitcast.17, s32[1,128]{1,0:T(1,128)} %bitcast.19, bf16[1,128]{1,0:T(2,128)(2,1)} %bitcast.21, ...), custom_call_target="tpu_custom_call" | custom-call | tf_op jit(solution)/shard_map/sort_particles/pallas_call | solution.py:213
  18.3 2.5 %collective-permute-done.3.refs_5_ = bf16[64,4096]{1,0:T(8,128)(2,1)S(1)} collective-permute-done((bf16[64,4096]{1,0:T(8,128)(2,1)}, bf16[64,4096]{1,0:T(8,128)(2,1)S(1)}, u32[]{:S(2)}, u32[]{:S(2)}) %collective-permute-start.3) | collective-permute-done | bytes 524320 | tf_op jit(solution)/shard_map/ppermute | solution.py:390
  20.8 2.1 %collective-permute-start = (bf16[64,4224]{1,0:T(8,128)(2,1)}, bf16[64,4224]{1,0:T(8,128)(2,1)S(1)}, u32[]{:S(2)}, u32[]{:S(2)}) collective-permute-start(bf16[64,4224]{1,0:T(8,128)(2,1)} %get-tuple-element.11), channel_id=1, source_target_pairs={{0,1},{1,0},{2,3},{3,2},{4,5},{5,4},{6,7},{7,6},{8,9},{9,8},{10,11... | collective-permute-start | bytes 1622024 | tf_op jit(solution)/shard_map/ppermute | solution.py:390
  22.9 10.3 %collective-permute-done.4.refs_6_ = bf16[64,4096]{1,0:T(8,128)(2,1)S(1)} collective-permute-done((bf16[64,4096]{1,0:T(8,128)(2,1)}, bf16[64,4096]{1,0:T(8,128)(2,1)S(1)}, u32[]{:S(2)}, u32[]{:S(2)}) %collective-permute-start.4) | collective-permute-done | bytes 524320 | tf_op jit(solution)/shard_map/ppermute | solution.py:390
  33.2 2.4 %collective-permute-start.1 = (bf16[64,4224]{1,0:T(8,128)(2,1)}, bf16[64,4224]{1,0:T(8,128)(2,1)S(1)}, u32[]{:S(2)}, u32[]{:S(2)}) collective-permute-start(bf16[64,4224]{1,0:T(8,128)(2,1)} %get-tuple-element.12), channel_id=1, source_target_pairs={{0,2},{1,3},{2,0},{3,1},{4,6},{5,7},{6,4},{7,5},{8,10},{9,11},{10,... | collective-permute-start | bytes 1622024 | tf_op jit(solution)/shard_map/ppermute | solution.py:390
  35.6 0.0 collective-permute-done.5.refs_7_
  35.6 0.0 collective-permute-start.2
  35.6 0.7 collective-permute-start.7
  36.3 0.0 collective-permute-done.8.refs_12_
  36.3 1.3 %collective-permute-start.9 = (bf16[32,8320]{1,0:T(8,128)(2,1)S(1)}, bf16[32,8320]{1,0:T(8,128)(2,1)S(1)}, u32[]{:S(2)}, u32[]{:S(2)}) collective-permute-start(bf16[32,8320]{1,0:T(8,128)(2,1)S(1)} %collective-permute-done.8.refs_12_), channel_id=1, source_target_pairs={{4,0},{5,1},{6,2},{7,3},{8,4},{9,5},{10,6},{11,7},{20,16},{21,17},... | collective-permute-start | bytes 1597448 | tf_op jit(solution)/shard_map/ppermute | solution.py:374
  37.6 6.1 %collective-permute-done.refs_1_ = bf16[64,4224]{1,0:T(8,128)(2,1)S(1)} collective-permute-done((bf16[64,4224]{1,0:T(8,128)(2,1)}, bf16[64,4224]{1,0:T(8,128)(2,1)S(1)}, u32[]{:S(2)}, u32[]{:S(2)}) %collective-permute-start) | collective-permute-done | bytes 540704 | tf_op jit(solution)/shard_map/ppermute | solution.py:390
  43.7 12.2 %collective-permute-done.1.refs_2_ = bf16[64,4224]{1,0:T(8,128)(2,1)S(1)} collective-permute-done((bf16[64,4224]{1,0:T(8,128)(2,1)}, bf16[64,4224]{1,0:T(8,128)(2,1)S(1)}, u32[]{:S(2)}, u32[]{:S(2)}) %collective-permute-start.1) | collective-permute-done | bytes 540704 | tf_op jit(solution)/shard_map/ppermute | solution.py:390
  55.9 0.0 collective-permute-done.2.refs_3_
  55.9 1.0 %copy-done.1 = bf16[64,4224]{1,0:T(8,128)(2,1)S(1)} copy-done((bf16[64,4224]{1,0:T(8,128)(2,1)S(1)}, bf16[64,4224]{1,0:T(8,128)(2,1)}, u32[]{:S(2)}) %copy-start.1) | copy-done | bytes 540696
  56.9 2.9 %score_and_spread.1 = bf16[256,768]{1,0:T(8,128)(2,1)S(1)} custom-call(bf16[64,4224]{1,0:T(8,128)(2,1)S(1)} %copy-done.1, bf16[64,4224]{1,0:T(8,128)(2,1)S(1)} %collective-permute-done.refs_1_, bf16[64,4224]{1,0:T(8,128)(2,1)S(1)} %collective-permute-done.1.refs_2_, bf16[64,4224]{1,0:T(8,128)(2,1)S(1)} %collective-permute-done.2.refs_3_, ...), custom_call_target="tpu_custom_call" | custom-call | tf_op jit(solution)/shard_map/score_and_spread/pallas_call | solution.py:305
  59.9 17.3 %all_to_all.9.x_ref = bf16[16,16,768]{2,1,0:T(8,128)(2,1)} all-to-all(bf16[16,16,768]{2,1,0:T(8,128)(2,1)S(1)} %bitcast.10), channel_id=1, replica_groups=mesh['half'=2,'owner'=16] {'owner'}, dimensions={0} | all-to-all | bytes 786432 | tf_op jit(solution)/shard_map/all_to_all | solution.py:404
  77.2 2.0 %finish_slab.1 = (f32[16,1024]{1,0:T(8,128)}, f32[16,512]{1,0:T(8,128)}) custom-call(bf16[16,16,768]{2,1,0:T(8,128)(2,1)} %all_to_all.9.x_ref, bf16[2,256,512]{2,1,0:T(8,128)(2,1)} %constant.5.clone.powers_ref), custom_call_target="tpu_custom_call" | custom-call | tf_op jit(solution)/shard_map/finish_slab/pallas_call | solution.py:357
  (12 shorter events, 0.0 us)
Async XLA Ops:
  0.6 8.8 %copy-start = (bf16[32,16,1024]{2,1,0:T(8,128)(2,1)S(1)}, bf16[32,16,1024]{2,1,0:T(8,128)(2,1)}, u32[]{:S(2)}) copy-start(bf16[32,16,1024]{2,1,0:T(8,128)(2,1)} %param.16) | copy-start | bytes 3145732
  0.6 8.8 %copy-start.3 = (bf16[32,4,16]{0,2,1:T(8,128)(2,1)S(1)}, bf16[32,4,16]{0,2,1:T(8,128)(2,1)}, u32[]{:S(2)}) copy-start(bf16[32,4,16]{0,2,1:T(8,128)(2,1)} %param.17) | copy-start | bytes 12292
  0.7 8.8 %copy-start.4 = (s32[32]{0:T(128)S(1)}, s32[32]{0:T(128)}, u32[]{:S(2)}) copy-start(s32[32]{0:T(128)} %param.18) | copy-start | bytes 388
  4.9 16.0 %collective-permute-start.3 = (bf16[64,4096]{1,0:T(8,128)(2,1)}, bf16[64,4096]{1,0:T(8,128)(2,1)S(1)}, u32[]{:S(2)}, u32[]{:S(2)}) collective-permute-start(bf16[64,4096]{1,0:T(8,128)(2,1)} %get-tuple-element.15), channel_id=1, source_target_pairs={{0,1},{1,0},{2,3},{3,2},{4,5},{5,4},{6,7},{7,6},{8,9},{9,8},{10,11... | collective-permute-start | bytes 1572872 | tf_op jit(solution)/shard_map/ppermute | solution.py:390
  7.9 25.3 %collective-permute-start.4 = (bf16[64,4096]{1,0:T(8,128)(2,1)}, bf16[64,4096]{1,0:T(8,128)(2,1)S(1)}, u32[]{:S(2)}, u32[]{:S(2)}) collective-permute-start(bf16[64,4096]{1,0:T(8,128)(2,1)} %get-tuple-element.16), channel_id=1, source_target_pairs={{0,2},{1,3},{2,0},{3,1},{4,6},{5,7},{6,4},{7,5},{8,10},{9,11},{10,... | collective-permute-start | bytes 1572872 | tf_op jit(solution)/shard_map/ppermute | solution.py:390
  9.4 26.2 %collective-permute-start.5 = (bf16[64,4096]{1,0:T(8,128)(2,1)}, bf16[64,4096]{1,0:T(8,128)(2,1)S(1)}, u32[]{:S(2)}, u32[]{:S(2)}) collective-permute-start(bf16[64,4096]{1,0:T(8,128)(2,1)} %get-tuple-element.17), channel_id=1, source_target_pairs={{0,3},{1,2},{2,1},{3,0},{4,7},{5,6},{6,5},{7,4},{8,11},{9,10},{10,... | collective-permute-start | bytes 1572872 | tf_op jit(solution)/shard_map/ppermute | solution.py:390
  9.4 46.5 %copy-start.2 = (bf16[64,4096]{1,0:T(8,128)(2,1)S(1)}, bf16[64,4096]{1,0:T(8,128)(2,1)}, u32[]{:S(2)}) copy-start(bf16[64,4096]{1,0:T(8,128)(2,1)} %get-tuple-element.14.refs_4_) | copy-start | bytes 1572868
  10.1 25.5 %collective-permute-start.6 = (bf16[32,8320]{1,0:T(8,128)(2,1)S(1)}, bf16[32,8320]{1,0:T(8,128)(2,1)S(1)}, u32[]{:S(2)}, u32[]{:S(2)}) collective-permute-start(bf16[32,8320]{1,0:T(8,128)(2,1)S(1)} %fold_projections.1.refs_8_), channel_id=1, source_target_pairs={{0,4},{1,5},{2,6},{3,7},{4,8},{5,9},{6,10},{7,11},{8,12},{9,13},{1... | collective-permute-start | bytes 1597448 | tf_op jit(solution)/shard_map/ppermute | solution.py:368
  12.2 24.1 %collective-permute-start.8 = (bf16[32,8320]{1,0:T(8,128)(2,1)S(1)}, bf16[32,8320]{1,0:T(8,128)(2,1)S(1)}, u32[]{:S(2)}, u32[]{:S(2)}) collective-permute-start(bf16[32,8320]{1,0:T(8,128)(2,1)S(1)} %fold_projections.1.refs_8_), channel_id=1, source_target_pairs={{0,12},{1,13},{2,14},{3,15},{4,0},{5,1},{6,2},{7,3},{8,4},{9,5},{1... | collective-permute-start | bytes 1597448 | tf_op jit(solution)/shard_map/ppermute | solution.py:368
  20.8 22.9 %collective-permute-start = (bf16[64,4224]{1,0:T(8,128)(2,1)}, bf16[64,4224]{1,0:T(8,128)(2,1)S(1)}, u32[]{:S(2)}, u32[]{:S(2)}) collective-permute-start(bf16[64,4224]{1,0:T(8,128)(2,1)} %get-tuple-element.11), channel_id=1, source_target_pairs={{0,1},{1,0},{2,3},{3,2},{4,5},{5,4},{6,7},{7,6},{8,9},{9,8},{10,11... | collective-permute-start | bytes 1622024 | tf_op jit(solution)/shard_map/ppermute | solution.py:390
  33.2 22.7 %collective-permute-start.1 = (bf16[64,4224]{1,0:T(8,128)(2,1)}, bf16[64,4224]{1,0:T(8,128)(2,1)S(1)}, u32[]{:S(2)}, u32[]{:S(2)}) collective-permute-start(bf16[64,4224]{1,0:T(8,128)(2,1)} %get-tuple-element.12), channel_id=1, source_target_pairs={{0,2},{1,3},{2,0},{3,1},{4,6},{5,7},{6,4},{7,5},{8,10},{9,11},{10,... | collective-permute-start | bytes 1622024 | tf_op jit(solution)/shard_map/ppermute | solution.py:390
  35.6 20.3 %collective-permute-start.2 = (bf16[64,4224]{1,0:T(8,128)(2,1)}, bf16[64,4224]{1,0:T(8,128)(2,1)S(1)}, u32[]{:S(2)}, u32[]{:S(2)}) collective-permute-start(bf16[64,4224]{1,0:T(8,128)(2,1)} %get-tuple-element.13), channel_id=1, source_target_pairs={{0,3},{1,2},{2,1},{3,0},{4,7},{5,6},{6,5},{7,4},{8,11},{9,10},{10,... | collective-permute-start | bytes 1622024 | tf_op jit(solution)/shard_map/ppermute | solution.py:390
  35.6 20.3 %collective-permute-start.7 = (bf16[32,8320]{1,0:T(8,128)(2,1)S(1)}, bf16[32,8320]{1,0:T(8,128)(2,1)S(1)}, u32[]{:S(2)}, u32[]{:S(2)}) collective-permute-start(bf16[32,8320]{1,0:T(8,128)(2,1)S(1)} %collective-permute-done.6.refs_9_), channel_id=1, source_target_pairs={{4,8},{5,9},{6,10},{7,11},{8,12},{9,13},{10,14},{11,15},{20,24},{2... | collective-permute-start | bytes 1597448 | tf_op jit(solution)/shard_map/ppermute | solution.py:373
  36.3 19.6 %collective-permute-start.9 = (bf16[32,8320]{1,0:T(8,128)(2,1)S(1)}, bf16[32,8320]{1,0:T(8,128)(2,1)S(1)}, u32[]{:S(2)}, u32[]{:S(2)}) collective-permute-start(bf16[32,8320]{1,0:T(8,128)(2,1)S(1)} %collective-permute-done.8.refs_12_), channel_id=1, source_target_pairs={{4,0},{5,1},{6,2},{7,3},{8,4},{9,5},{10,6},{11,7},{20,16},{21,17},... | collective-permute-start | bytes 1597448 | tf_op jit(solution)/shard_map/ppermute | solution.py:374
  55.9 1.0 %copy-start.1 = (bf16[64,4224]{1,0:T(8,128)(2,1)S(1)}, bf16[64,4224]{1,0:T(8,128)(2,1)}, u32[]{:S(2)}) copy-start(bf16[64,4224]{1,0:T(8,128)(2,1)} %get-tuple-element.10.refs_0_) | copy-start | bytes 1622020

commit v9 on v8

--- a/solution.py
+++ b/solution.py
@@ -207,7 +207,7 @@
 def sort_particles(first, lines, images, owner, pair, shift, defocus, reach, count, capacity, pairs, pieces):
     particles, _, length = images.shape
     slots = count * capacity
-    each, width, groups = slots // pieces, lines * length + (0 if first else 128), 4
+    each, width, groups = slots // pieces, lines * length + (0 if first else 128), 2
     args = [images] + [a[None, :] for a in (owner, pair, shift, defocus)]
     args.append(packed_table(length))
     return pl.pallas_call(

time: 79.5 us -> 79.6 us (level)
  no operation moved by 1% of the time
where the time goes in v9:
time: 79.6 us; the launch traced here: 79.3 us
  waiting for transfers between devices  31 us (39%)
  blocking collectives  17.3 us (22%)
  starting transfers between devices  15.1 us (19%)
  Pallas kernels  14 us (18%)
  local copies, waits for them, and re-layouts  1.06 us (1%)
    ppermute x6, waiting for transfers between devices, on_device(): lax.ppermute(a, 'owner', [(k, k ^ i) for k in range(owners)])  31 us
    all_to_all x1, blocking collectives, on_device(): lax.all_to_all(partial, 'owner', split_axis=0, concat_axis=0, tiled=True)  17.3 us
    ppermute x6, starting transfers between devices, on_device(): lax.ppermute(a, 'owner', [(k, k ^ i) for k in range(owners)])  8.98 us
    pallas_call x2, Pallas kernels, sort_particles(): pl.pallas_call(lambda *refs: sort_kernel(first, reach, count, capacity, p...  8.41 us
    ppermute x2, starting transfers between devices, gather_rows(): lax.ppermute(block, 'owner', [(k, (k + i * count) % owners) for k in rang...  4.18 us
    pallas_call x1, Pallas kernels, score_and_spread(): pl.pallas_call(lambda *refs: score_kernel(1.0 / math.sqrt(lines * length)...  2.94 us
    pallas_call x1, Pallas kernels, finish(): pl.pallas_call(finish_kernel, out_shape=(jax.ShapeDtypeStruct((rows, 2 *...  2.03 us
  transfers between devices with their start and end apart: 10, of which 4 were waited for; matrix products, arithmetic and copies ran while one was open for 0% of the time, Pallas kernels for 6%

profile of v9, /device:TPU:0, one launch (start us, length us, event | category | flops | bytes accessed | tf_op | source)
XLA Modules:
  0.0 79.3 jit_solution(4555264271033289361)
XLA Ops:
  0.7 4.3 %sort_particles.3 = (bf16[64,4096]{1,0:T(8,128)(2,1)}, bf16[64,4096]{1,0:T(8,128)(2,1)}, bf16[64,4096]{1,0:T(8,128)(2,1)}, bf16[64,4096]{1,0:T(8,128)(2,1)}) custom-call(bf16[128,16,512]{2,1,0:T(8,128)(2,1)} %refs_0_.3, s32[1,128]{1,0:T(1,128)} %bitcast.14, s32[1,128]{1,0:T(1,128)} %bitcast.16, s32[1,128]{1,0:T(1,128)} %bitcast.18, bf16[1,128]{1,0:T(2,128)(2,1)} %bitcast.20, ...), custom_call_target="tpu_custom_call" | custom-call | tf_op jit(solution)/shard_map/sort_particles/pallas_call | solution.py:213
  4.9 3.0 %collective-permute-start.3 = (bf16[64,4096]{1,0:T(8,128)(2,1)}, bf16[64,4096]{1,0:T(8,128)(2,1)S(1)}, u32[]{:S(2)}, u32[]{:S(2)}) collective-permute-start(bf16[64,4096]{1,0:T(8,128)(2,1)} %get-tuple-element.15), channel_id=1, source_target_pairs={{0,1},{1,0},{2,3},{3,2},{4,5},{5,4},{6,7},{7,6},{8,9},{9,8},{10,11... | collective-permute-start | bytes 1572872 | tf_op jit(solution)/shard_map/ppermute | solution.py:390
  7.9 1.5 %collective-permute-start.4 = (bf16[64,4096]{1,0:T(8,128)(2,1)}, bf16[64,4096]{1,0:T(8,128)(2,1)S(1)}, u32[]{:S(2)}, u32[]{:S(2)}) collective-permute-start(bf16[64,4096]{1,0:T(8,128)(2,1)} %get-tuple-element.16), channel_id=1, source_target_pairs={{0,2},{1,3},{2,0},{3,1},{4,6},{5,7},{6,4},{7,5},{8,10},{9,11},{10,... | collective-permute-start | bytes 1572872 | tf_op jit(solution)/shard_map/ppermute | solution.py:390
  9.5 0.0 collective-permute-start.5
  9.5 0.6 fold_projections.1.refs_8_
  10.1 2.1 %collective-permute-start.6 = (bf16[32,8320]{1,0:T(8,128)(2,1)S(1)}, bf16[32,8320]{1,0:T(8,128)(2,1)S(1)}, u32[]{:S(2)}, u32[]{:S(2)}) collective-permute-start(bf16[32,8320]{1,0:T(8,128)(2,1)S(1)} %fold_projections.1.refs_8_), channel_id=1, source_target_pairs={{0,4},{1,5},{2,6},{3,7},{4,8},{5,9},{6,10},{7,11},{8,12},{9,13},{1... | collective-permute-start | bytes 1597448 | tf_op jit(solution)/shard_map/ppermute | solution.py:368
  12.2 2.1 %collective-permute-start.8 = (bf16[32,8320]{1,0:T(8,128)(2,1)S(1)}, bf16[32,8320]{1,0:T(8,128)(2,1)S(1)}, u32[]{:S(2)}, u32[]{:S(2)}) collective-permute-start(bf16[32,8320]{1,0:T(8,128)(2,1)S(1)} %fold_projections.1.refs_8_), channel_id=1, source_target_pairs={{0,12},{1,13},{2,14},{3,15},{4,0},{5,1},{6,2},{7,3},{8,4},{9,5},{1... | collective-permute-start | bytes 1597448 | tf_op jit(solution)/shard_map/ppermute | solution.py:368
  14.3 4.2 %sort_particles.2 = (bf16[64,4224]{1,0:T(8,128)(2,1)}, bf16[64,4224]{1,0:T(8,128)(2,1)}, bf16[64,4224]{1,0:T(8,128)(2,1)}, bf16[64,4224]{1,0:T(8,128)(2,1)}) custom-call(bf16[128,16,512]{2,1,0:T(8,128)(2,1)} %refs_0_.3, s32[1,128]{1,0:T(1,128)} %bitcast.15, s32[1,128]{1,0:T(1,128)} %bitcast.17, s32[1,128]{1,0:T(1,128)} %bitcast.19, bf16[1,128]{1,0:T(2,128)(2,1)} %bitcast.21, ...), custom_call_target="tpu_custom_call" | custom-call | tf_op jit(solution)/shard_map/sort_particles/pallas_call | solution.py:213
  18.5 2.4 %collective-permute-done.3.refs_5_ = bf16[64,4096]{1,0:T(8,128)(2,1)S(1)} collective-permute-done((bf16[64,4096]{1,0:T(8,128)(2,1)}, bf16[64,4096]{1,0:T(8,128)(2,1)S(1)}, u32[]{:S(2)}, u32[]{:S(2)}) %collective-permute-start.3) | collective-permute-done | bytes 524320 | tf_op jit(solution)/shard_map/ppermute | solution.py:390
  20.9 2.1 %collective-permute-start = (bf16[64,4224]{1,0:T(8,128)(2,1)}, bf16[64,4224]{1,0:T(8,128)(2,1)S(1)}, u32[]{:S(2)}, u32[]{:S(2)}) collective-permute-start(bf16[64,4224]{1,0:T(8,128)(2,1)} %get-tuple-element.11), channel_id=1, source_target_pairs={{0,1},{1,0},{2,3},{3,2},{4,5},{5,4},{6,7},{7,6},{8,9},{9,8},{10,11... | collective-permute-start | bytes 1622024 | tf_op jit(solution)/shard_map/ppermute | solution.py:390
  23.0 10.3 %collective-permute-done.4.refs_6_ = bf16[64,4096]{1,0:T(8,128)(2,1)S(1)} collective-permute-done((bf16[64,4096]{1,0:T(8,128)(2,1)}, bf16[64,4096]{1,0:T(8,128)(2,1)S(1)}, u32[]{:S(2)}, u32[]{:S(2)}) %collective-permute-start.4) | collective-permute-done | bytes 524320 | tf_op jit(solution)/shard_map/ppermute | solution.py:390
  33.3 2.4 %collective-permute-start.1 = (bf16[64,4224]{1,0:T(8,128)(2,1)}, bf16[64,4224]{1,0:T(8,128)(2,1)S(1)}, u32[]{:S(2)}, u32[]{:S(2)}) collective-permute-start(bf16[64,4224]{1,0:T(8,128)(2,1)} %get-tuple-element.12), channel_id=1, source_target_pairs={{0,2},{1,3},{2,0},{3,1},{4,6},{5,7},{6,4},{7,5},{8,10},{9,11},{10,... | collective-permute-start | bytes 1622024 | tf_op jit(solution)/shard_map/ppermute | solution.py:390
  35.6 0.0 collective-permute-start.2
  35.6 0.0 collective-permute-done.6.refs_9_
  35.6 0.7 collective-permute-start.7
  36.3 0.0 collective-permute-done.8.refs_12_
  36.4 1.3 %collective-permute-start.9 = (bf16[32,8320]{1,0:T(8,128)(2,1)S(1)}, bf16[32,8320]{1,0:T(8,128)(2,1)S(1)}, u32[]{:S(2)}, u32[]{:S(2)}) collective-permute-start(bf16[32,8320]{1,0:T(8,128)(2,1)S(1)} %collective-permute-done.8.refs_12_), channel_id=1, source_target_pairs={{4,0},{5,1},{6,2},{7,3},{8,4},{9,5},{10,6},{11,7},{20,16},{21,17},... | collective-permute-start | bytes 1597448 | tf_op jit(solution)/shard_map/ppermute | solution.py:374
  37.7 6.1 %collective-permute-done.refs_1_ = bf16[64,4224]{1,0:T(8,128)(2,1)S(1)} collective-permute-done((bf16[64,4224]{1,0:T(8,128)(2,1)}, bf16[64,4224]{1,0:T(8,128)(2,1)S(1)}, u32[]{:S(2)}, u32[]{:S(2)}) %collective-permute-start) | collective-permute-done | bytes 540704 | tf_op jit(solution)/shard_map/ppermute | solution.py:390
  43.8 12.2 %collective-permute-done.1.refs_2_ = bf16[64,4224]{1,0:T(8,128)(2,1)S(1)} collective-permute-done((bf16[64,4224]{1,0:T(8,128)(2,1)}, bf16[64,4224]{1,0:T(8,128)(2,1)S(1)}, u32[]{:S(2)}, u32[]{:S(2)}) %collective-permute-start.1) | collective-permute-done | bytes 540704 | tf_op jit(solution)/shard_map/ppermute | solution.py:390
  55.9 0.0 collective-permute-done.2.refs_3_
  56.0 1.0 %copy-done.1 = bf16[64,4224]{1,0:T(8,128)(2,1)S(1)} copy-done((bf16[64,4224]{1,0:T(8,128)(2,1)S(1)}, bf16[64,4224]{1,0:T(8,128)(2,1)}, u32[]{:S(2)}) %copy-start.1) | copy-done | bytes 540696
  57.0 2.9 %score_and_spread.1 = bf16[256,768]{1,0:T(8,128)(2,1)S(1)} custom-call(bf16[64,4224]{1,0:T(8,128)(2,1)S(1)} %copy-done.1, bf16[64,4224]{1,0:T(8,128)(2,1)S(1)} %collective-permute-done.refs_1_, bf16[64,4224]{1,0:T(8,128)(2,1)S(1)} %collective-permute-done.1.refs_2_, bf16[64,4224]{1,0:T(8,128)(2,1)S(1)} %collective-permute-done.2.refs_3_, ...), custom_call_target="tpu_custom_call" | custom-call | tf_op jit(solution)/shard_map/score_and_spread/pallas_call | solution.py:305
  60.0 17.3 %all_to_all.9.x_ref = bf16[16,16,768]{2,1,0:T(8,128)(2,1)} all-to-all(bf16[16,16,768]{2,1,0:T(8,128)(2,1)S(1)} %bitcast.10), channel_id=1, replica_groups=mesh['half'=2,'owner'=16] {'owner'}, dimensions={0} | all-to-all | bytes 786432 | tf_op jit(solution)/shard_map/all_to_all | solution.py:404
  77.3 2.0 %finish_slab.1 = (f32[16,1024]{1,0:T(8,128)}, f32[16,512]{1,0:T(8,128)}) custom-call(bf16[16,16,768]{2,1,0:T(8,128)(2,1)} %all_to_all.9.x_ref, bf16[2,256,512]{2,1,0:T(8,128)(2,1)} %constant.5.clone.powers_ref), custom_call_target="tpu_custom_call" | custom-call | tf_op jit(solution)/shard_map/finish_slab/pallas_call | solution.py:357
  (12 shorter events, 0.0 us)
Async XLA Ops:
  0.6 8.8 %copy-start = (bf16[32,16,1024]{2,1,0:T(8,128)(2,1)S(1)}, bf16[32,16,1024]{2,1,0:T(8,128)(2,1)}, u32[]{:S(2)}) copy-start(bf16[32,16,1024]{2,1,0:T(8,128)(2,1)} %param.16) | copy-start | bytes 3145732
  0.6 8.8 %copy-start.3 = (bf16[32,4,16]{0,2,1:T(8,128)(2,1)S(1)}, bf16[32,4,16]{0,2,1:T(8,128)(2,1)}, u32[]{:S(2)}) copy-start(bf16[32,4,16]{0,2,1:T(8,128)(2,1)} %param.17) | copy-start | bytes 12292
  0.7 8.8 %copy-start.4 = (s32[32]{0:T(128)S(1)}, s32[32]{0:T(128)}, u32[]{:S(2)}) copy-start(s32[32]{0:T(128)} %param.18) | copy-start | bytes 388
  4.9 16.0 %collective-permute-start.3 = (bf16[64,4096]{1,0:T(8,128)(2,1)}, bf16[64,4096]{1,0:T(8,128)(2,1)S(1)}, u32[]{:S(2)}, u32[]{:S(2)}) collective-permute-start(bf16[64,4096]{1,0:T(8,128)(2,1)} %get-tuple-element.15), channel_id=1, source_target_pairs={{0,1},{1,0},{2,3},{3,2},{4,5},{5,4},{6,7},{7,6},{8,9},{9,8},{10,11... | collective-permute-start | bytes 1572872 | tf_op jit(solution)/shard_map/ppermute | solution.py:390
  7.9 25.3 %collective-permute-start.4 = (bf16[64,4096]{1,0:T(8,128)(2,1)}, bf16[64,4096]{1,0:T(8,128)(2,1)S(1)}, u32[]{:S(2)}, u32[]{:S(2)}) collective-permute-start(bf16[64,4096]{1,0:T(8,128)(2,1)} %get-tuple-element.16), channel_id=1, source_target_pairs={{0,2},{1,3},{2,0},{3,1},{4,6},{5,7},{6,4},{7,5},{8,10},{9,11},{10,... | collective-permute-start | bytes 1572872 | tf_op jit(solution)/shard_map/ppermute | solution.py:390
  9.5 26.2 %collective-permute-start.5 = (bf16[64,4096]{1,0:T(8,128)(2,1)}, bf16[64,4096]{1,0:T(8,128)(2,1)S(1)}, u32[]{:S(2)}, u32[]{:S(2)}) collective-permute-start(bf16[64,4096]{1,0:T(8,128)(2,1)} %get-tuple-element.17), channel_id=1, source_target_pairs={{0,3},{1,2},{2,1},{3,0},{4,7},{5,6},{6,5},{7,4},{8,11},{9,10},{10,... | collective-permute-start | bytes 1572872 | tf_op jit(solution)/shard_map/ppermute | solution.py:390
  9.5 46.5 %copy-start.2 = (bf16[64,4096]{1,0:T(8,128)(2,1)S(1)}, bf16[64,4096]{1,0:T(8,128)(2,1)}, u32[]{:S(2)}) copy-start(bf16[64,4096]{1,0:T(8,128)(2,1)} %get-tuple-element.14.refs_4_) | copy-start | bytes 1572868
  10.1 25.5 %collective-permute-start.6 = (bf16[32,8320]{1,0:T(8,128)(2,1)S(1)}, bf16[32,8320]{1,0:T(8,128)(2,1)S(1)}, u32[]{:S(2)}, u32[]{:S(2)}) collective-permute-start(bf16[32,8320]{1,0:T(8,128)(2,1)S(1)} %fold_projections.1.refs_8_), channel_id=1, source_target_pairs={{0,4},{1,5},{2,6},{3,7},{4,8},{5,9},{6,10},{7,11},{8,12},{9,13},{1... | collective-permute-start | bytes 1597448 | tf_op jit(solution)/shard_map/ppermute | solution.py:368
  12.2 24.1 %collective-permute-start.8 = (bf16[32,8320]{1,0:T(8,128)(2,1)S(1)}, bf16[32,8320]{1,0:T(8,128)(2,1)S(1)}, u32[]{:S(2)}, u32[]{:S(2)}) collective-permute-start(bf16[32,8320]{1,0:T(8,128)(2,1)S(1)} %fold_projections.1.refs_8_), channel_id=1, source_target_pairs={{0,12},{1,13},{2,14},{3,15},{4,0},{5,1},{6,2},{7,3},{8,4},{9,5},{1... | collective-permute-start | bytes 1597448 | tf_op jit(solution)/shard_map/ppermute | solution.py:368
  20.9 22.9 %collective-permute-start = (bf16[64,4224]{1,0:T(8,128)(2,1)}, bf16[64,4224]{1,0:T(8,128)(2,1)S(1)}, u32[]{:S(2)}, u32[]{:S(2)}) collective-permute-start(bf16[64,4224]{1,0:T(8,128)(2,1)} %get-tuple-element.11), channel_id=1, source_target_pairs={{0,1},{1,0},{2,3},{3,2},{4,5},{5,4},{6,7},{7,6},{8,9},{9,8},{10,11... | collective-permute-start | bytes 1622024 | tf_op jit(solution)/shard_map/ppermute | solution.py:390
  33.3 22.7 %collective-permute-start.1 = (bf16[64,4224]{1,0:T(8,128)(2,1)}, bf16[64,4224]{1,0:T(8,128)(2,1)S(1)}, u32[]{:S(2)}, u32[]{:S(2)}) collective-permute-start(bf16[64,4224]{1,0:T(8,128)(2,1)} %get-tuple-element.12), channel_id=1, source_target_pairs={{0,2},{1,3},{2,0},{3,1},{4,6},{5,7},{6,4},{7,5},{8,10},{9,11},{10,... | collective-permute-start | bytes 1622024 | tf_op jit(solution)/shard_map/ppermute | solution.py:390
  35.6 20.3 %collective-permute-start.2 = (bf16[64,4224]{1,0:T(8,128)(2,1)}, bf16[64,4224]{1,0:T(8,128)(2,1)S(1)}, u32[]{:S(2)}, u32[]{:S(2)}) collective-permute-start(bf16[64,4224]{1,0:T(8,128)(2,1)} %get-tuple-element.13), channel_id=1, source_target_pairs={{0,3},{1,2},{2,1},{3,0},{4,7},{5,6},{6,5},{7,4},{8,11},{9,10},{10,... | collective-permute-start | bytes 1622024 | tf_op jit(solution)/shard_map/ppermute | solution.py:390
  35.6 20.3 %collective-permute-start.7 = (bf16[32,8320]{1,0:T(8,128)(2,1)S(1)}, bf16[32,8320]{1,0:T(8,128)(2,1)S(1)}, u32[]{:S(2)}, u32[]{:S(2)}) collective-permute-start(bf16[32,8320]{1,0:T(8,128)(2,1)S(1)} %collective-permute-done.6.refs_9_), channel_id=1, source_target_pairs={{4,8},{5,9},{6,10},{7,11},{8,12},{9,13},{10,14},{11,15},{20,24},{2... | collective-permute-start | bytes 1597448 | tf_op jit(solution)/shard_map/ppermute | solution.py:373
  36.4 19.6 %collective-permute-start.9 = (bf16[32,8320]{1,0:T(8,128)(2,1)S(1)}, bf16[32,8320]{1,0:T(8,128)(2,1)S(1)}, u32[]{:S(2)}, u32[]{:S(2)}) collective-permute-start(bf16[32,8320]{1,0:T(8,128)(2,1)S(1)} %collective-permute-done.8.refs_12_), channel_id=1, source_target_pairs={{4,0},{5,1},{6,2},{7,3},{8,4},{9,5},{10,6},{11,7},{20,16},{21,17},... | collective-permute-start | bytes 1597448 | tf_op jit(solution)/shard_map/ppermute | solution.py:374
  56.0 1.0 %copy-start.1 = (bf16[64,4224]{1,0:T(8,128)(2,1)S(1)}, bf16[64,4224]{1,0:T(8,128)(2,1)}, u32[]{:S(2)}) copy-start(bf16[64,4224]{1,0:T(8,128)(2,1)} %get-tuple-element.10.refs_0_) | copy-start | bytes 1622020

commit v10 on v8

--- a/solution.py
+++ b/solution.py
@@ -246,7 +246,7 @@
     pairs, rows = info.shape[0], out_ref.shape[0]
     found = jnp.concatenate([ref[:, early * length :] for ref in images], axis=0).astype(F32)
     slots = found.shape[0]
-    here = 4
+    here = 8
 
     def stacked(line):
         refs, place = (images, line) if line < early else (later, line - early)

time: 79.5 us -> 79.5 us (level)
  no operation moved by 1% of the time
where the time goes in v10:
time: 79.5 us; the launch traced here: 79.2 us
  waiting for transfers between devices  31.1 us (39%)
  blocking collectives  17.3 us (22%)
  starting transfers between devices  15.1 us (19%)
  Pallas kernels  13.8 us (17%)
  local copies, waits for them, and re-layouts  1.06 us (1%)
    ppermute x6, waiting for transfers between devices, on_device(): lax.ppermute(a, 'owner', [(k, k ^ i) for k in range(owners)])  31.1 us
    all_to_all x1, blocking collectives, on_device(): lax.all_to_all(partial, 'owner', split_axis=0, concat_axis=0, tiled=True)  17.3 us
    ppermute x6, starting transfers between devices, on_device(): lax.ppermute(a, 'owner', [(k, k ^ i) for k in range(owners)])  8.98 us
    pallas_call x2, Pallas kernels, sort_particles(): pl.pallas_call(lambda *refs: sort_kernel(first, reach, count, capacity, p...  8.27 us
    ppermute x2, starting transfers between devices, gather_rows(): lax.ppermute(block, 'owner', [(k, (k + i * count) % owners) for k in rang...  4.18 us
    pallas_call x1, Pallas kernels, score_and_spread(): pl.pallas_call(lambda *refs: score_kernel(1.0 / math.sqrt(lines * length)...  2.91 us
    pallas_call x1, Pallas kernels, finish(): pl.pallas_call(finish_kernel, out_shape=(jax.ShapeDtypeStruct((rows, 2 *...  2.03 us
  transfers between devices with their start and end apart: 10, of which 4 were waited for; matrix products, arithmetic and copies ran while one was open for 0% of the time, Pallas kernels for 6%

profile of v10, /device:TPU:0, one launch (start us, length us, event | category | flops | bytes accessed | tf_op | source)
XLA Modules:
  0.0 79.2 jit_solution(57221487860572827)
XLA Ops:
  0.7 4.2 %sort_particles.3 = (bf16[64,4096]{1,0:T(8,128)(2,1)}, bf16[64,4096]{1,0:T(8,128)(2,1)}, bf16[64,4096]{1,0:T(8,128)(2,1)}, bf16[64,4096]{1,0:T(8,128)(2,1)}) custom-call(bf16[128,16,512]{2,1,0:T(8,128)(2,1)} %refs_0_.3, s32[1,128]{1,0:T(1,128)} %bitcast.14, s32[1,128]{1,0:T(1,128)} %bitcast.16, s32[1,128]{1,0:T(1,128)} %bitcast.18, bf16[1,128]{1,0:T(2,128)(2,1)} %bitcast.20, ...), custom_call_target="tpu_custom_call" | custom-call | tf_op jit(solution)/shard_map/sort_particles/pallas_call | solution.py:213
  4.9 3.0 %collective-permute-start.3 = (bf16[64,4096]{1,0:T(8,128)(2,1)}, bf16[64,4096]{1,0:T(8,128)(2,1)S(1)}, u32[]{:S(2)}, u32[]{:S(2)}) collective-permute-start(bf16[64,4096]{1,0:T(8,128)(2,1)} %get-tuple-element.15), channel_id=1, source_target_pairs={{0,1},{1,0},{2,3},{3,2},{4,5},{5,4},{6,7},{7,6},{8,9},{9,8},{10,11... | collective-permute-start | bytes 1572872 | tf_op jit(solution)/shard_map/ppermute | solution.py:390
  7.9 1.5 %collective-permute-start.4 = (bf16[64,4096]{1,0:T(8,128)(2,1)}, bf16[64,4096]{1,0:T(8,128)(2,1)S(1)}, u32[]{:S(2)}, u32[]{:S(2)}) collective-permute-start(bf16[64,4096]{1,0:T(8,128)(2,1)} %get-tuple-element.16), channel_id=1, source_target_pairs={{0,2},{1,3},{2,0},{3,1},{4,6},{5,7},{6,4},{7,5},{8,10},{9,11},{10,... | collective-permute-start | bytes 1572872 | tf_op jit(solution)/shard_map/ppermute | solution.py:390
  9.4 0.0 collective-permute-start.5
  9.4 0.6 fold_projections.1.refs_8_
  10.1 2.1 %collective-permute-start.6 = (bf16[32,8320]{1,0:T(8,128)(2,1)S(1)}, bf16[32,8320]{1,0:T(8,128)(2,1)S(1)}, u32[]{:S(2)}, u32[]{:S(2)}) collective-permute-start(bf16[32,8320]{1,0:T(8,128)(2,1)S(1)} %fold_projections.1.refs_8_), channel_id=1, source_target_pairs={{0,4},{1,5},{2,6},{3,7},{4,8},{5,9},{6,10},{7,11},{8,12},{9,13},{1... | collective-permute-start | bytes 1597448 | tf_op jit(solution)/shard_map/ppermute | solution.py:368
  12.2 2.1 %collective-permute-start.8 = (bf16[32,8320]{1,0:T(8,128)(2,1)S(1)}, bf16[32,8320]{1,0:T(8,128)(2,1)S(1)}, u32[]{:S(2)}, u32[]{:S(2)}) collective-permute-start(bf16[32,8320]{1,0:T(8,128)(2,1)S(1)} %fold_projections.1.refs_8_), channel_id=1, source_target_pairs={{0,12},{1,13},{2,14},{3,15},{4,0},{5,1},{6,2},{7,3},{8,4},{9,5},{1... | collective-permute-start | bytes 1597448 | tf_op jit(solution)/shard_map/ppermute | solution.py:368
  14.2 4.1 %sort_particles.2 = (bf16[64,4224]{1,0:T(8,128)(2,1)}, bf16[64,4224]{1,0:T(8,128)(2,1)}, bf16[64,4224]{1,0:T(8,128)(2,1)}, bf16[64,4224]{1,0:T(8,128)(2,1)}) custom-call(bf16[128,16,512]{2,1,0:T(8,128)(2,1)} %refs_0_.3, s32[1,128]{1,0:T(1,128)} %bitcast.15, s32[1,128]{1,0:T(1,128)} %bitcast.17, s32[1,128]{1,0:T(1,128)} %bitcast.19, bf16[1,128]{1,0:T(2,128)(2,1)} %bitcast.21, ...), custom_call_target="tpu_custom_call" | custom-call | tf_op jit(solution)/shard_map/sort_particles/pallas_call | solution.py:213
  18.3 2.5 %collective-permute-done.3.refs_5_ = bf16[64,4096]{1,0:T(8,128)(2,1)S(1)} collective-permute-done((bf16[64,4096]{1,0:T(8,128)(2,1)}, bf16[64,4096]{1,0:T(8,128)(2,1)S(1)}, u32[]{:S(2)}, u32[]{:S(2)}) %collective-permute-start.3) | collective-permute-done | bytes 524320 | tf_op jit(solution)/shard_map/ppermute | solution.py:390
  20.8 2.1 %collective-permute-start = (bf16[64,4224]{1,0:T(8,128)(2,1)}, bf16[64,4224]{1,0:T(8,128)(2,1)S(1)}, u32[]{:S(2)}, u32[]{:S(2)}) collective-permute-start(bf16[64,4224]{1,0:T(8,128)(2,1)} %get-tuple-element.11), channel_id=1, source_target_pairs={{0,1},{1,0},{2,3},{3,2},{4,5},{5,4},{6,7},{7,6},{8,9},{9,8},{10,11... | collective-permute-start | bytes 1622024 | tf_op jit(solution)/shard_map/ppermute | solution.py:390
  22.9 10.3 %collective-permute-done.4.refs_6_ = bf16[64,4096]{1,0:T(8,128)(2,1)S(1)} collective-permute-done((bf16[64,4096]{1,0:T(8,128)(2,1)}, bf16[64,4096]{1,0:T(8,128)(2,1)S(1)}, u32[]{:S(2)}, u32[]{:S(2)}) %collective-permute-start.4) | collective-permute-done | bytes 524320 | tf_op jit(solution)/shard_map/ppermute | solution.py:390
  33.2 2.4 %collective-permute-start.1 = (bf16[64,4224]{1,0:T(8,128)(2,1)}, bf16[64,4224]{1,0:T(8,128)(2,1)S(1)}, u32[]{:S(2)}, u32[]{:S(2)}) collective-permute-start(bf16[64,4224]{1,0:T(8,128)(2,1)} %get-tuple-element.12), channel_id=1, source_target_pairs={{0,2},{1,3},{2,0},{3,1},{4,6},{5,7},{6,4},{7,5},{8,10},{9,11},{10,... | collective-permute-start | bytes 1622024 | tf_op jit(solution)/shard_map/ppermute | solution.py:390
  35.6 0.0 collective-permute-done.5.refs_7_
  35.6 0.0 collective-permute-start.2
  35.6 0.7 collective-permute-start.7
  36.3 0.0 collective-permute-done.8.refs_12_
  36.3 1.3 %collective-permute-start.9 = (bf16[32,8320]{1,0:T(8,128)(2,1)S(1)}, bf16[32,8320]{1,0:T(8,128)(2,1)S(1)}, u32[]{:S(2)}, u32[]{:S(2)}) collective-permute-start(bf16[32,8320]{1,0:T(8,128)(2,1)S(1)} %collective-permute-done.8.refs_12_), channel_id=1, source_target_pairs={{4,0},{5,1},{6,2},{7,3},{8,4},{9,5},{10,6},{11,7},{20,16},{21,17},... | collective-permute-start | bytes 1597448 | tf_op jit(solution)/shard_map/ppermute | solution.py:374
  37.6 6.1 %collective-permute-done.refs_1_ = bf16[64,4224]{1,0:T(8,128)(2,1)S(1)} collective-permute-done((bf16[64,4224]{1,0:T(8,128)(2,1)}, bf16[64,4224]{1,0:T(8,128)(2,1)S(1)}, u32[]{:S(2)}, u32[]{:S(2)}) %collective-permute-start) | collective-permute-done | bytes 540704 | tf_op jit(solution)/shard_map/ppermute | solution.py:390
  43.7 12.2 %collective-permute-done.1.refs_2_ = bf16[64,4224]{1,0:T(8,128)(2,1)S(1)} collective-permute-done((bf16[64,4224]{1,0:T(8,128)(2,1)}, bf16[64,4224]{1,0:T(8,128)(2,1)S(1)}, u32[]{:S(2)}, u32[]{:S(2)}) %collective-permute-start.1) | collective-permute-done | bytes 540704 | tf_op jit(solution)/shard_map/ppermute | solution.py:390
  55.9 0.0 collective-permute-done.2.refs_3_
  55.9 1.0 %copy-done.1 = bf16[64,4224]{1,0:T(8,128)(2,1)S(1)} copy-done((bf16[64,4224]{1,0:T(8,128)(2,1)S(1)}, bf16[64,4224]{1,0:T(8,128)(2,1)}, u32[]{:S(2)}) %copy-start.1) | copy-done | bytes 540696
  56.9 2.9 %score_and_spread.1 = bf16[256,768]{1,0:T(8,128)(2,1)S(1)} custom-call(bf16[64,4224]{1,0:T(8,128)(2,1)S(1)} %copy-done.1, bf16[64,4224]{1,0:T(8,128)(2,1)S(1)} %collective-permute-done.refs_1_, bf16[64,4224]{1,0:T(8,128)(2,1)S(1)} %collective-permute-done.1.refs_2_, bf16[64,4224]{1,0:T(8,128)(2,1)S(1)} %collective-permute-done.2.refs_3_, ...), custom_call_target="tpu_custom_call" | custom-call | tf_op jit(solution)/shard_map/score_and_spread/pallas_call | solution.py:305
  59.8 17.3 %all_to_all.9.x_ref = bf16[16,16,768]{2,1,0:T(8,128)(2,1)} all-to-all(bf16[16,16,768]{2,1,0:T(8,128)(2,1)S(1)} %bitcast.10), channel_id=1, replica_groups=mesh['half'=2,'owner'=16] {'owner'}, dimensions={0} | all-to-all | bytes 786432 | tf_op jit(solution)/shard_map/all_to_all | solution.py:404
  77.2 2.0 %finish_slab.1 = (f32[16,1024]{1,0:T(8,128)}, f32[16,512]{1,0:T(8,128)}) custom-call(bf16[16,16,768]{2,1,0:T(8,128)(2,1)} %all_to_all.9.x_ref, bf16[2,256,512]{2,1,0:T(8,128)(2,1)} %constant.5.clone.powers_ref), custom_call_target="tpu_custom_call" | custom-call | tf_op jit(solution)/shard_map/finish_slab/pallas_call | solution.py:357
  (12 shorter events, 0.0 us)
Async XLA Ops:
  0.6 8.8 %copy-start = (bf16[32,16,1024]{2,1,0:T(8,128)(2,1)S(1)}, bf16[32,16,1024]{2,1,0:T(8,128)(2,1)}, u32[]{:S(2)}) copy-start(bf16[32,16,1024]{2,1,0:T(8,128)(2,1)} %param.16) | copy-start | bytes 3145732
  0.6 8.8 %copy-start.3 = (bf16[32,4,16]{0,2,1:T(8,128)(2,1)S(1)}, bf16[32,4,16]{0,2,1:T(8,128)(2,1)}, u32[]{:S(2)}) copy-start(bf16[32,4,16]{0,2,1:T(8,128)(2,1)} %param.17) | copy-start | bytes 12292
  0.7 8.8 %copy-start.4 = (s32[32]{0:T(128)S(1)}, s32[32]{0:T(128)}, u32[]{:S(2)}) copy-start(s32[32]{0:T(128)} %param.18) | copy-start | bytes 388
  4.9 16.0 %collective-permute-start.3 = (bf16[64,4096]{1,0:T(8,128)(2,1)}, bf16[64,4096]{1,0:T(8,128)(2,1)S(1)}, u32[]{:S(2)}, u32[]{:S(2)}) collective-permute-start(bf16[64,4096]{1,0:T(8,128)(2,1)} %get-tuple-element.15), channel_id=1, source_target_pairs={{0,1},{1,0},{2,3},{3,2},{4,5},{5,4},{6,7},{7,6},{8,9},{9,8},{10,11... | collective-permute-start | bytes 1572872 | tf_op jit(solution)/shard_map/ppermute | solution.py:390
  7.9 25.3 %collective-permute-start.4 = (bf16[64,4096]{1,0:T(8,128)(2,1)}, bf16[64,4096]{1,0:T(8,128)(2,1)S(1)}, u32[]{:S(2)}, u32[]{:S(2)}) collective-permute-start(bf16[64,4096]{1,0:T(8,128)(2,1)} %get-tuple-element.16), channel_id=1, source_target_pairs={{0,2},{1,3},{2,0},{3,1},{4,6},{5,7},{6,4},{7,5},{8,10},{9,11},{10,... | collective-permute-start | bytes 1572872 | tf_op jit(solution)/shard_map/ppermute | solution.py:390
  9.4 26.2 %collective-permute-start.5 = (bf16[64,4096]{1,0:T(8,128)(2,1)}, bf16[64,4096]{1,0:T(8,128)(2,1)S(1)}, u32[]{:S(2)}, u32[]{:S(2)}) collective-permute-start(bf16[64,4096]{1,0:T(8,128)(2,1)} %get-tuple-element.17), channel_id=1, source_target_pairs={{0,3},{1,2},{2,1},{3,0},{4,7},{5,6},{6,5},{7,4},{8,11},{9,10},{10,... | collective-permute-start | bytes 1572872 | tf_op jit(solution)/shard_map/ppermute | solution.py:390
  9.4 46.5 %copy-start.2 = (bf16[64,4096]{1,0:T(8,128)(2,1)S(1)}, bf16[64,4096]{1,0:T(8,128)(2,1)}, u32[]{:S(2)}) copy-start(bf16[64,4096]{1,0:T(8,128)(2,1)} %get-tuple-element.14.refs_4_) | copy-start | bytes 1572868
  10.1 25.5 %collective-permute-start.6 = (bf16[32,8320]{1,0:T(8,128)(2,1)S(1)}, bf16[32,8320]{1,0:T(8,128)(2,1)S(1)}, u32[]{:S(2)}, u32[]{:S(2)}) collective-permute-start(bf16[32,8320]{1,0:T(8,128)(2,1)S(1)} %fold_projections.1.refs_8_), channel_id=1, source_target_pairs={{0,4},{1,5},{2,6},{3,7},{4,8},{5,9},{6,10},{7,11},{8,12},{9,13},{1... | collective-permute-start | bytes 1597448 | tf_op jit(solution)/shard_map/ppermute | solution.py:368
  12.2 24.1 %collective-permute-start.8 = (bf16[32,8320]{1,0:T(8,128)(2,1)S(1)}, bf16[32,8320]{1,0:T(8,128)(2,1)S(1)}, u32[]{:S(2)}, u32[]{:S(2)}) collective-permute-start(bf16[32,8320]{1,0:T(8,128)(2,1)S(1)} %fold_projections.1.refs_8_), channel_id=1, source_target_pairs={{0,12},{1,13},{2,14},{3,15},{4,0},{5,1},{6,2},{7,3},{8,4},{9,5},{1... | collective-permute-start | bytes 1597448 | tf_op jit(solution)/shard_map/ppermute | solution.py:368
  20.8 22.9 %collective-permute-start = (bf16[64,4224]{1,0:T(8,128)(2,1)}, bf16[64,4224]{1,0:T(8,128)(2,1)S(1)}, u32[]{:S(2)}, u32[]{:S(2)}) collective-permute-start(bf16[64,4224]{1,0:T(8,128)(2,1)} %get-tuple-element.11), channel_id=1, source_target_pairs={{0,1},{1,0},{2,3},{3,2},{4,5},{5,4},{6,7},{7,6},{8,9},{9,8},{10,11... | collective-permute-start | bytes 1622024 | tf_op jit(solution)/shard_map/ppermute | solution.py:390
  33.2 22.7 %collective-permute-start.1 = (bf16[64,4224]{1,0:T(8,128)(2,1)}, bf16[64,4224]{1,0:T(8,128)(2,1)S(1)}, u32[]{:S(2)}, u32[]{:S(2)}) collective-permute-start(bf16[64,4224]{1,0:T(8,128)(2,1)} %get-tuple-element.12), channel_id=1, source_target_pairs={{0,2},{1,3},{2,0},{3,1},{4,6},{5,7},{6,4},{7,5},{8,10},{9,11},{10,... | collective-permute-start | bytes 1622024 | tf_op jit(solution)/shard_map/ppermute | solution.py:390
  35.6 20.3 %collective-permute-start.2 = (bf16[64,4224]{1,0:T(8,128)(2,1)}, bf16[64,4224]{1,0:T(8,128)(2,1)S(1)}, u32[]{:S(2)}, u32[]{:S(2)}) collective-permute-start(bf16[64,4224]{1,0:T(8,128)(2,1)} %get-tuple-element.13), channel_id=1, source_target_pairs={{0,3},{1,2},{2,1},{3,0},{4,7},{5,6},{6,5},{7,4},{8,11},{9,10},{10,... | collective-permute-start | bytes 1622024 | tf_op jit(solution)/shard_map/ppermute | solution.py:390
  35.6 20.3 %collective-permute-start.7 = (bf16[32,8320]{1,0:T(8,128)(2,1)S(1)}, bf16[32,8320]{1,0:T(8,128)(2,1)S(1)}, u32[]{:S(2)}, u32[]{:S(2)}) collective-permute-start(bf16[32,8320]{1,0:T(8,128)(2,1)S(1)} %collective-permute-done.6.refs_9_), channel_id=1, source_target_pairs={{4,8},{5,9},{6,10},{7,11},{8,12},{9,13},{10,14},{11,15},{20,24},{2... | collective-permute-start | bytes 1597448 | tf_op jit(solution)/shard_map/ppermute | solution.py:373
  36.3 19.6 %collective-permute-start.9 = (bf16[32,8320]{1,0:T(8,128)(2,1)S(1)}, bf16[32,8320]{1,0:T(8,128)(2,1)S(1)}, u32[]{:S(2)}, u32[]{:S(2)}) collective-permute-start(bf16[32,8320]{1,0:T(8,128)(2,1)S(1)} %collective-permute-done.8.refs_12_), channel_id=1, source_target_pairs={{4,0},{5,1},{6,2},{7,3},{8,4},{9,5},{10,6},{11,7},{20,16},{21,17},... | collective-permute-start | bytes 1597448 | tf_op jit(solution)/shard_map/ppermute | solution.py:374
  55.9 1.0 %copy-start.1 = (bf16[64,4224]{1,0:T(8,128)(2,1)S(1)}, bf16[64,4224]{1,0:T(8,128)(2,1)}, u32[]{:S(2)}) copy-start(bf16[64,4224]{1,0:T(8,128)(2,1)} %get-tuple-element.10.refs_0_) | copy-start | bytes 1622020
